TPU v7x, 32 devices: a whole 2x2x4 slice. The times are simulated.
32 devices in a mesh: sky: 2 (over y), ma: 4 (over z), freq: 2 (over x), pol: 2 (over core).
Axes of the slice: x: 2, y: 2, z: 4, core: 2. Of those that a mesh axis runs over, the one named last changes fastest.
Arguments:
- alm: bfloat16 [2, 2, 1024, 4, 1024], P(None, 'freq', ('ma', 'pol'), None, 'sky'), parts along dimension 4, may hold values from -6 to 6
- beam: bfloat16 [4, 2, 2, 1024, 1024], P('ma', 'freq', None, 'pol'), may hold values from -0.1875 to 0.1875
- m_table: int32 [4], P('ma'), may hold values from 0 to 511, as said below
- chan_mask: int32 [2], P('freq'), may hold values from 0 to 1, as said below
- noise: float32 [2, 1024], P('freq', 'pol'), may hold values from 0.5 to 4
Outputs:
- scaled: bfloat16 [2, 2, 4, 1024, 1024], P(None, 'freq', 'ma', 'pol', 'sky'), parts along dimension 4
- channel_power: float32 [4], P(('sky', 'freq')), parts along dimension 0
There are 2 independent parts, one for each index of `sky`. A program takes and returns all parts, laid end to end along the dimension named above; an argument that names none is the same for every part. Nothing has to cross between parts.
Inputs may be any that keep to these rules, and one draw needn't show every extreme that they name: `m_table`: the 4 values are distinct whole numbers below 512. `chan_mask`: at least one of the 2 channels is usable.
All inputs are finite; a program needn't handle non-finite values.
Results may differ from a plain program's by a relative error of at most 0.00055.
Values may be sent and summed in bfloat16 or wider, within the bound.
No kernel may reach another device: no remote copies, remote signals or barrier semaphores. Data moves between devices by JAX's collectives and lax.ppermute only.
A program may use at most 64 MiB of HBM per device.

v0:
```python
import jax
import jax.numpy as jnp
from jax import lax
from jax.sharding import PartitionSpec as P


def on_device(alm, beam, m_table, chan_mask, noise):
    arrived = lax.all_to_all(alm, "ma", split_axis=3, concat_axis=2, tiled=True)
    blocks = arrived.reshape(
        arrived.shape[0],
        arrived.shape[1],
        lax.axis_size("ma"),
        arrived.shape[2] // lax.axis_size("ma"),
        arrived.shape[4],
    )
    joined = lax.all_gather(blocks, "pol", axis=3, tiled=True)
    coeffs_all = joined.reshape(
        joined.shape[0], joined.shape[1], joined.shape[2] * joined.shape[3], joined.shape[4]
    )
    degree = lax.iota(jnp.int32, coeffs_all.shape[2])
    keep_mask = (degree >= m_table[0])[None, None, :, None]
    coeffs = jnp.where(keep_mask, coeffs_all, jnp.zeros((), coeffs_all.dtype))
    response = beam[0]
    real_part = jnp.einsum(
        "fkl,fls->fks", response[:, 0], coeffs[0], preferred_element_type=jnp.float32
    ) - jnp.einsum("fkl,fls->fks", response[:, 1], coeffs[1], preferred_element_type=jnp.float32)
    imag_part = jnp.einsum(
        "fkl,fls->fks", response[:, 0], coeffs[1], preferred_element_type=jnp.float32
    ) + jnp.einsum("fkl,fls->fks", response[:, 1], coeffs[0], preferred_element_type=jnp.float32)
    visibility = jnp.stack([real_part, imag_part])
    weighted = visibility * visibility / noise[None, :, :, None]
    partial_power = jnp.sum(weighted, axis=(0, 2, 3))
    modes_total = jnp.float32(
        lax.axis_size("ma") * noise.shape[1] * lax.axis_size("pol") * visibility.shape[3]
    )
    mask_float = chan_mask.astype(jnp.float32)
    channel_power = lax.psum(partial_power, ("ma", "pol")) / modes_total
    masked_sum, live_count = lax.psum(
        (jnp.sum(mask_float * channel_power), jnp.sum(mask_float)), "freq"
    )
    band_power = masked_sum / live_count
    factor = mask_float / jnp.sqrt(0.5 * channel_power + 0.5 * band_power + 1e-06)
    scaled = visibility * (lax.rsqrt(noise) * factor[:, None])[None, :, :, None]
    return (scaled[:, :, None].astype(jnp.bfloat16), channel_power)


def solution(mesh):
    return jax.shard_map(
        on_device,
        mesh=mesh,
        in_specs=(
            P(None, "freq", ("ma", "pol"), None, "sky"),
            P("ma", "freq", None, "pol", None),
            P("ma"),
            P("freq"),
            P("freq", "pol"),
        ),
        out_specs=(P(None, "freq", "ma", "pol", "sky"), P(("sky", "freq"))),
        check_vma=False,
    )
```

profile of v0, /device:TPU:0, one launch (start us, length us, event | category | flops | bytes accessed | tf_op | source)
XLA Modules:
  0.0 94.6 jit_solution(7890521315917420241)
XLA Ops:
  7.2 0.0 all-gather.3.cloned.1.call-start
  7.2 1.4 %copy.10 = bf16[2,1,128,4,512]{4,2,0,1,3:T(8,128)(2,1)S(1)} copy(bf16[2,1,128,4,512]{4,3,2,1,0:T(4,128)(2,1)} %param.5) | data formatting | bytes 2097152 | tf_op args[0]
  8.6 31.9 %all_to_all.15 = bf16[2,1,128,4,512]{4,2,0,1,3:T(8,128)(2,1)S(1)} all-to-all(bf16[2,1,128,4,512]{4,2,0,1,3:T(8,128)(2,1)S(1)} %copy.10), channel_id=1, replica_groups=mesh['sky'=2,'ma'=4,'freq'=2,'pol'=2] {'ma'}, dimensions={3} | all-to-all | bytes 2097152 | tf_op jit(solution)/shard_map/all_to_all | solution.py:8
  40.5 1.1 %copy.14 = bf16[2,1,128,4,512]{4,2,3,0,1:T(8,128)(2,1)} copy(bf16[2,1,128,4,512]{4,2,0,1,3:T(8,128)(2,1)S(1)} %all_to_all.15) | data formatting | bytes 2097152 | tf_op jit(solution)/shard_map/all_to_all | solution.py:8
  41.6 0.0 all-gather.3.cloned.1.call-update
  42.9 8.5 %all-gather.3.cloned.1.call-done = bf16[2,1,4,256,1,512]{5,3,2,0,4,1:T(8,128)(2,1)} async-done(((bf16[2,1,4,128,1,512]{5,3,2,0,4,1:T(8,128)(2,1)}), bf16[2,1,4,256,1,512]{5,3,2,0,4,1:T(8,128)(2,1)}) %all-gather.3.cloned.1.call-update) | async-done | bytes 2097168 | tf_op jit(solution)/shard_map/all_gather | solution.py:16
  51.5 0.0 copy-start.1
  51.5 2.0 %broadcast_select_fusion = bf16[2,1,1024,512]{3,2,0,1:T(8,128)(2,1)S(1)} fusion(bf16[2,1,1024,512]{3,2,0,1:T(8,128)(2,1)} %bitcast.47, pred[1024]{0:T(1024)(128)(4,1)S(1)} %iota_compare_fusion), kind=kLoop, calls=%fused_computation.5 | loop fusion | flops 1048576 | bytes 4195328 | tf_op jit(solution)/shard_map/jit(_where)/select_n | solution.py:22
  53.4 0.3 copy-done.1
  53.7 0.7 fusion.3
  54.4 0.8 fusion.4
  55.2 0.8 convolution_subtract_fusion
  55.9 0.0 copy-start
  56.0 0.8 convolution_add_fusion
  56.7 0.0 copy-done
  56.7 1.1 %fusion.2 = f32[]{:T(128)} fusion(f32[1,1,512,512]{2,3,1,0:T(8,128)S(1)} %bitcast.45, f32[1,1,512,512]{2,3,1,0:T(8,128)S(1)} %bitcast.43, f32[512]{0:T(512)S(1)} %bitcast.48), kind=kLoop, calls=%fused_computation.4 | loop fusion | flops 2097151 | bytes 2099204 | tf_op jit(solution)/shard_map/reduce_sum | solution.py:32
  57.9 17.7 %psum.21 = f32[1]{0:T(128)} all-reduce(f32[1]{0:T(128)} %bitcast.16), channel_id=1, replica_groups=mesh['sky'=2,'ma'=4,'freq'=2,'pol'=2] {'ma','pol'}, use_global_device_ids=true, to_apply=%region_1.2 | all-reduce | flops 1 | bytes 8 | tf_op jit(solution)/shard_map/psum | solution.py:37
  76.9 6.7 %all-reduce = (f32[]{:T(128)}, f32[]{:T(128)}) all-reduce(f32[]{:T(128)} %bitcast.17, f32[]{:T(128)} %bitcast.18), channel_id=1, replica_groups=mesh['sky'=2,'ma'=4,'freq'=2,'pol'=2] {'freq'}, use_global_device_ids=true, to_apply=%region_2.3 | all-reduce | flops 2 | bytes 16 | tf_op jit(solution)/shard_map/psum | solution.py:38
  85.0 0.3 fusion
  85.3 1.3 %copy.12 = bf16[2,1,1,512,512]{4,3,2,1,0:T(8,128)(2,1)} copy(bf16[2,1,1,512,512]{3,4,2,1,0:T(8,128)(2,1)S(1)} %fusion) | data formatting | bytes 2097152
  (2 shorter events, 0.0 us)
Async XLA Ops:
  7.2 44.3 %all-gather.3.cloned.1.call-start = ((), (), s32[]{:S(2)}) async-start(), calls=%async_computation.1 | async-start | bytes 3145728 | tf_op jit(solution)/shard_map/all_gather | solution.py:16
  51.5 2.2 %copy-start.1 = (bf16[1,1,2,512,1024]{4,3,2,1,0:T(8,128)(2,1)S(1)}, bf16[1,1,2,512,1024]{4,3,2,1,0:T(8,128)(2,1)}, u32[]{:S(2)}) copy-start(bf16[1,1,2,512,1024]{4,3,2,1,0:T(8,128)(2,1)} %param.6) | copy-start | bytes 6291460
  55.9 0.8 copy-start
Sparse Core Ops, SparseCore 0:
  41.7 9.6 all-gather.2
where the time goes:
time: 94.9 us; the launch traced here: 94.6 us
  blocking collectives  56.3 us (59%)
  between operations  19.3 us (20%)
  waiting for transfers between devices  8.54 us (9%)
  local copies, waits for them, and re-layouts  4.09 us (4%)
  other arithmetic  3.39 us (4%)
  matrix products  3.01 us (3%)
    all_to_all x1, blocking collectives, on_device(): arrived = lax.all_to_all(alm, 'ma', split_axis=3, concat_axis=2, tiled=True)  31.9 us
    psum x1, blocking collectives, on_device(): channel_power = lax.psum(partial_power, ('ma', 'pol')) / modes_total  17.7 us
    all_gather x1, waiting for transfers between devices, on_device(): joined = lax.all_gather(blocks, 'pol', axis=3, tiled=True)  8.53 us
    psum x1, blocking collectives, on_device(): lax.psum((jnp.sum(mask_float * channel_power), jnp.sum(mask_float)), 'freq')  6.71 us
    unnamed x6, local copies, waits for them, and re-layouts  3.01 us
    select_n x1, other arithmetic, on_device(): coeffs = jnp.where(keep_mask, coeffs_all, jnp.zeros((), coeffs_all.dtype))  1.96 us
  transfers between devices with their start and end apart: 1, of which 1 were waited for; matrix products, arithmetic and copies ran while one was open for 0% of the time, Pallas kernels for 0%

commit v1 on v0

--- a/solution.py
+++ b/solution.py
@@ -1,10 +1,252 @@
+import functools
+
 import jax
 import jax.numpy as jnp
 from jax import lax
+from jax.experimental import pallas as pl
+from jax.experimental.pallas import tpu as pltpu
 from jax.sharding import PartitionSpec as P
 
+VMEM = pl.BlockSpec(memory_space=pltpu.VMEM)
+SMEM = pl.BlockSpec(memory_space=pltpu.SMEM)
+
+
+def column(row):
+    return jnp.transpose(jnp.broadcast_to(row, (128, row.shape[1])))
+
+
+def split_kernel(steps, alm_ref, *refs):
+    *slab_refs, modes_ref = refs
+    place = lax.axis_index("ma")
+    for c in range(alm_ref.shape[0]):
+        modes_ref[...] = pltpu.einshape("lms->mls", alm_ref[c])
+        for ref, step in zip(slab_refs, steps, strict=True):
+            ref[c] = modes_ref[place ^ step]
+
+
+def contract(m_ref, beam_ref, block_refs, steps):
+    ell = block_refs[0].shape[1]
+    left, right_real, right_imag = [], [], []
+    for ref, (step, other) in zip(block_refs, steps, strict=True):
+        owner = lax.axis_index("ma") ^ step
+        half = lax.axis_index("pol") ^ other
+        start = (owner * lax.axis_size("pol") + half) * ell
+        columns = pl.ds(pl.multiple_of(start, ell), ell)
+        degree = start + lax.broadcasted_iota(jnp.int32, (ell, ref.shape[2]), 0)
+        keep = degree >= m_ref[0]
+        real = jnp.where(keep, ref[0], jnp.zeros((), ref.dtype))
+        imag = jnp.where(keep, ref[1], jnp.zeros((), ref.dtype))
+        left += [beam_ref[0, :, columns], beam_ref[1, :, columns]]
+        right_real += [real, -imag]
+        right_imag += [imag, real]
+    left = jnp.concatenate(left, axis=1)
+    dot = functools.partial(jnp.dot, preferred_element_type=jnp.float32)
+    return (
+        dot(left, jnp.concatenate(right_real, axis=0)),
+        dot(left, jnp.concatenate(right_imag, axis=0)),
+    )
+
+
+def first_kernel(steps, m_ref, mask_ref, beam_ref, noise_ref, *refs):
+    *blocks, vis_ref, weight_ref = refs
+    vis_ref[0], vis_ref[1] = contract(m_ref, beam_ref, blocks, steps)
+    weight_ref[...] = column(lax.rsqrt(noise_ref[...]))
+
+
+def at_edge():
+    place = lax.axis_index("ma")
+    return (place == 0) | (place == lax.axis_size("ma") - 1)
+
+
+def weigh(vis, weight):
+    return jnp.concatenate(
+        [vis[:, i : i + 128] * weight for i in range(0, vis.shape[1], 128)], axis=1
+    )
+
+
+def power_of(real, imag):
+    squares = real * real + imag * imag
+    folded = functools.reduce(
+        jnp.add, [squares[:, i : i + 128] for i in range(0, squares.shape[1], 128)]
+    )
+    return jnp.sum(folded)
+
+
+def edge_kernel(steps, m_ref, beam_ref, weight_ref, before_ref, *refs):
+    *blocks, vis_ref, power_ref = refs
+    real, imag = contract(m_ref, beam_ref, blocks, steps)
+    real += before_ref[0]
+    imag += before_ref[1]
+    vis_ref[0] = real
+    vis_ref[1] = imag
+    weight = weight_ref[...]
+    total = power_of(weigh(real, weight), weigh(imag, weight))
+    lane = lax.broadcasted_iota(jnp.int32, power_ref.shape, 1)
+    here = (lane == lax.axis_index("freq")) & at_edge()
+    power_ref[...] = jnp.where(here, total, 0.0)
+
+
+def next_kernel(steps, m_ref, beam_ref, before_ref, *refs):
+    *blocks, vis_ref = refs
+    real, imag = contract(m_ref, beam_ref, blocks, steps)
+    vis_ref[0] = real + before_ref[0]
+    vis_ref[1] = imag + before_ref[1]
+
+
+def live_kernel(slots, mask_ref, live_ref):
+    lane = lax.broadcasted_iota(jnp.int32, live_ref.shape, 1)
+    leader = (lax.axis_index("ma") == 1) & (lax.axis_index("pol") == 0)
+    here = (lane == lax.axis_index("freq") + slots) & leader
+    live_ref[...] = jnp.where(here, mask_ref[0].astype(jnp.float32), 0.0)
+
+
+def last_kernel(steps, m_ref, beam_ref, weight_ref, before_ref, *refs):
+    *blocks, edge_ref, live_ref, vis_ref, power_ref = refs
+    real, imag = contract(m_ref, beam_ref, blocks, steps)
+    weight = weight_ref[...]
+    real = weigh(real + before_ref[0], weight)
+    imag = weigh(imag + before_ref[1], weight)
+    vis_ref[0] = real
+    vis_ref[1] = imag
+    total = power_of(real, imag)
+    lane = lax.broadcasted_iota(jnp.int32, power_ref.shape, 1)
+    here = (lane == lax.axis_index("freq")) & jnp.logical_not(at_edge())
+    power_ref[...] = jnp.where(here, total, 0.0) + edge_ref[...] + live_ref[...]
+
+
+def finish_kernel(slots, modes, mask_ref, total_ref, vis_ref, scaled_ref, power_ref, held_ref, sems):
+    lane = lax.broadcasted_iota(jnp.int32, (1, 128), 1)
+    totals = total_ref[0:1, :]
+    powers = totals / modes
+    masks = pltpu.roll(totals, 128 - slots, 1)
+
+    def over(where, values):
+        return jnp.sum(jnp.where(where, values, 0.0), axis=1, keepdims=True)
+
+    band = over(lane < slots, powers * masks) / over(lane < slots, masks)
+    own = over(lane == lax.axis_index("freq"), powers)
+    mask = mask_ref[0].astype(jnp.float32)
+    factor = mask / jnp.sqrt(0.5 * own + 0.5 * band + 1e-06)
+    power_ref[...] = jnp.where(lane == 0, own, 0.0)
+    copies = []
+    parts, rows, _ = vis_ref.shape
+    chunk = rows // 4
+    for c in range(parts):
+        for j in range(0, rows, chunk):
+            held_ref[c, j : j + chunk] = (vis_ref[c, j : j + chunk] * factor).astype(
+                scaled_ref.dtype
+            )
+            copies.append(
+                pltpu.make_async_copy(
+                    held_ref.at[c, pl.ds(j, chunk)],
+                    scaled_ref.at[c, pl.ds(j, chunk)],
+                    sems.at[len(copies)],
+                )
+            )
+            copies[-1].start()
+    for copy in copies:
+        copy.wait()
+
+
+def swap(x, name, step):
+    return lax.ppermute(x, name, [(i, i ^ step) for i in range(lax.axis_size(name))])
+
 
 def on_device(alm, beam, m_table, chan_mask, noise):
+    n_ma, n_pol, n_freq = (lax.axis_size(name) for name in ("ma", "pol", "freq"))
+    parts, _, ell, _, maps = alm.shape
+    modes = beam.shape[3]
+    response = beam[0, 0]
+    params = pltpu.CompilerParams(vmem_limit_bytes=24 << 20)
+    vis_shape = jax.ShapeDtypeStruct((parts, modes, maps), jnp.float32)
+    slab = jax.ShapeDtypeStruct((parts, ell, maps), alm.dtype)
+    row = jax.ShapeDtypeStruct((8, 128), jnp.float32)
+    weights = jax.ShapeDtypeStruct((modes, 128), jnp.float32)
+
+    def call(kernel, out_shape, scalars, operands, blocks, **more):
+        return pl.pallas_call(
+            kernel,
+            out_shape=out_shape,
+            in_specs=[SMEM] * len(scalars) + [VMEM] * len(operands),
+            out_specs=more.pop("out_specs", jax.tree.map(lambda _: VMEM, out_shape)),
+            compiler_params=params,
+            cost_estimate=pl.CostEstimate(
+                flops=blocks * 2 * 4 * modes * maps * ell,
+                bytes_accessed=(blocks + 4) * parts * ell * (maps + modes) * 2,
+                transcendentals=0,
+            ),
+            **more,
+        )(*scalars, *operands)
+
+    two, one, three, own = call(
+        functools.partial(split_kernel, (2, 1, 3, 0)),
+        [slab] * n_ma,
+        (),
+        (alm[:, 0],),
+        0,
+        scratch_shapes=[pltpu.VMEM((n_ma, ell, maps), alm.dtype)],
+    )
+    two = swap(two, "ma", 2)
+    one = swap(one, "ma", 1)
+    edge = lax.ppermute(three, "ma", [(0, 3), (3, 0)])
+    middle = lax.ppermute(three, "ma", [(1, 2), (2, 1)])
+    own_far = swap(own, "pol", 1)
+    one_far = swap(one, "pol", 1)
+    two_far = swap(two, "pol", 1)
+    edge_far = swap(edge, "pol", 1)
+    middle_far = swap(middle, "pol", 1)
+    steps = ((0, 0), (0, 1), (1, 0), (1, 1), (2, 0), (2, 1))
+    vis, weight = call(
+        functools.partial(first_kernel, steps),
+        (vis_shape, weights),
+        (m_table, chan_mask),
+        (response, noise, own, own_far, one, one_far, two, two_far),
+        6,
+    )
+    vis, edge_power = call(
+        functools.partial(edge_kernel, ((3, 0), (3, 1))),
+        (vis_shape, row),
+        (m_table,),
+        (response, weight, vis, edge, edge_far),
+        2,
+    )
+    edge_power = lax.ppermute(edge_power, "ma", [(0, 1), (3, 2)])
+    live = call(functools.partial(live_kernel, n_freq), row, (chan_mask,), (), 0)
+    vis = call(
+        functools.partial(next_kernel, ((3, 0),)), vis_shape, (m_table,), (response, vis, middle), 1
+    )
+    vis, total = call(
+        functools.partial(last_kernel, ((3, 1),)),
+        (vis_shape, row),
+        (m_table,),
+        (response, weight, vis, middle_far, edge_power, live),
+        1,
+    )
+    total += swap(total, "pol", 1)
+    total += swap(total, "freq", 1)
+    beyond = lax.ppermute(total, "ma", [(1, 3), (2, 0)])
+    beside = lax.ppermute(total, "ma", [(1, 0), (2, 3)])
+    across = lax.ppermute(total, "ma", [(1, 2), (2, 1)])
+    total = total + beyond + beside + across
+    scaled, own_power = call(
+        functools.partial(finish_kernel, n_freq, n_ma * n_pol * modes * maps),
+        (
+            jax.ShapeDtypeStruct((parts, modes, maps), jnp.bfloat16),
+            jax.ShapeDtypeStruct((1, 128), jnp.float32),
+        ),
+        (chan_mask,),
+        (total, vis),
+        0,
+        out_specs=(pl.BlockSpec(memory_space=pltpu.HBM), VMEM),
+        scratch_shapes=[
+            pltpu.VMEM((parts, modes, maps), jnp.bfloat16),
+            pltpu.SemaphoreType.DMA((4 * parts,)),
+        ],
+    )
+    return scaled[:, None, None], own_power[0, :1]
+
+
+def on_device_plain(alm, beam, m_table, chan_mask, noise):
     arrived = lax.all_to_all(alm, "ma", split_axis=3, concat_axis=2, tiled=True)
     blocks = arrived.reshape(
         arrived.shape[0],
@@ -44,9 +286,16 @@
     return (scaled[:, :, None].astype(jnp.bfloat16), channel_power)
 
 
+def step(alm, beam, m_table, chan_mask, noise):
+    sizes = [lax.axis_size(name) for name in ("ma", "freq", "pol")]
+    if alm.shape[2] % 128 == 0 and sizes == [4, 2, 2]:
+        return on_device(alm, beam, m_table, chan_mask, noise)
+    return on_device_plain(alm, beam, m_table, chan_mask, noise)
+
+
 def solution(mesh):
     return jax.shard_map(
-        on_device,
+        step,
         mesh=mesh,
         in_specs=(
             P(None, "freq", ("ma", "pol"), None, "sky"),

time: 94.9 us -> 57.3 us (0.60)
  the two profiles are of different devices: /device:TPU:0 before, /device:TPU:14 now
where the time goes in v1:
time: 57.3 us; the launch traced here: 57 us
  waiting for transfers between devices  30.4 us (53%)
  starting transfers between devices  15 us (26%)
  Pallas kernels  5.94 us (10%)
  local copies, waits for them, and re-layouts  3.49 us (6%)
  between operations  2.12 us (4%)
    ppermute x9, waiting for transfers between devices, swap(): lax.ppermute(x, name, [(i, i ^ step) for i in range(lax.axis_size(name))])  19 us
    pallas_call x7, Pallas kernels, call(): pl.pallas_call(kernel, out_shape=out_shape, in_specs=[SMEM] * len(scalars...  5.94 us
    ppermute x1, waiting for transfers between devices, on_device(): middle = lax.ppermute(three, 'ma', [(1, 2), (2, 1)])  4.65 us
    ppermute x9, starting transfers between devices, swap(): lax.ppermute(x, name, [(i, i ^ step) for i in range(lax.axis_size(name))])  4.29 us
    ppermute x1, waiting for transfers between devices, on_device(): edge_power = lax.ppermute(edge_power, 'ma', [(0, 1), (3, 2)])  3.73 us
    unnamed x8, local copies, waits for them, and re-layouts  3.49 us
    ppermute x1, waiting for transfers between devices, on_device(): across = lax.ppermute(total, 'ma', [(1, 2), (2, 1)])  3 us
    ppermute x1, starting transfers between devices, on_device(): beyond = lax.ppermute(total, 'ma', [(1, 3), (2, 0)])  2.63 us
  transfers between devices with their start and end apart: 15, of which 7 were waited for; matrix products, arithmetic and copies ran while one was open for 0% of the time, Pallas kernels for 6%

profile of v1, /device:TPU:14, one launch (start us, length us, event | category | flops | bytes accessed | tf_op | source)
XLA Modules:
  0.0 57.0 jit_solution(15773932343047605803)
XLA Ops:
  0.6 1.2 %copy-done.2 = bf16[2,1,128,4,512]{4,3,2,1,0:T(4,128)(2,1)S(1)} copy-done((bf16[2,1,128,4,512]{4,3,2,1,0:T(4,128)(2,1)S(1)}, bf16[2,1,128,4,512]{4,3,2,1,0:T(4,128)(2,1)}, u32[]{:S(2)}) %copy-start.2) | copy-done | bytes 1048600
  1.9 0.3 shard_map.68
  2.2 0.5 collective-permute-start.1
  2.7 2.6 %collective-permute-start.3 = (bf16[2,128,512]{2,1,0:T(8,128)(2,1)S(1)}, bf16[2,128,512]{2,1,0:T(8,128)(2,1)S(1)}, u32[]{:S(2)}, u32[]{:S(2)}) collective-permute-start(bf16[2,128,512]{2,1,0:T(8,128)(2,1)S(1)} %get-tuple-element.16), channel_id=1, source_target_pairs={{0,8},{4,12},{8,0},{12,4},{1,9},{5,13},{9,1},{13,5},{2,10},{6,14},... | collective-permute-start | bytes 786440 | tf_op jit(solution)/shard_map/ppermute | solution.py:152
  5.3 0.7 %collective-permute-start.5 = (bf16[2,128,512]{2,1,0:T(8,128)(2,1)S(1)}, bf16[2,128,512]{2,1,0:T(8,128)(2,1)S(1)}, u32[]{:S(2)}, u32[]{:S(2)}) collective-permute-start(bf16[2,128,512]{2,1,0:T(8,128)(2,1)S(1)} %get-tuple-element.19), channel_id=1, source_target_pairs={{0,12},{12,0},{1,13},{13,1},{2,14},{14,2},{3,15},{15,3},{16,28},{2... | collective-permute-start | bytes 786440 | tf_op jit(solution)/shard_map/ppermute | solution.py:191
  5.9 2.4 %collective-permute-start.7 = (bf16[2,128,512]{2,1,0:T(8,128)(2,1)S(1)}, bf16[2,128,512]{2,1,0:T(8,128)(2,1)S(1)}, u32[]{:S(2)}, u32[]{:S(2)}) collective-permute-start(bf16[2,128,512]{2,1,0:T(8,128)(2,1)S(1)} %get-tuple-element.19), channel_id=1, source_target_pairs={{4,8},{8,4},{5,9},{9,5},{6,10},{10,6},{7,11},{11,7},{20,24},{24,20... | collective-permute-start | bytes 786440 | tf_op jit(solution)/shard_map/ppermute | solution.py:192
  8.3 0.1 collective-permute-start
  8.4 4.7 %collective-permute-done.1.refs_2_ = bf16[2,128,512]{2,1,0:T(8,128)(2,1)S(1)} collective-permute-done((bf16[2,128,512]{2,1,0:T(8,128)(2,1)S(1)}, bf16[2,128,512]{2,1,0:T(8,128)(2,1)S(1)}, u32[]{:S(2)}, u32[]{:S(2)}) %collective-permute-start.1) | collective-permute-done | bytes 262176 | tf_op jit(solution)/shard_map/ppermute | solution.py:152
  13.1 10.1 %collective-permute-done.3.refs_4_ = bf16[2,128,512]{2,1,0:T(8,128)(2,1)S(1)} collective-permute-done((bf16[2,128,512]{2,1,0:T(8,128)(2,1)S(1)}, bf16[2,128,512]{2,1,0:T(8,128)(2,1)S(1)}, u32[]{:S(2)}, u32[]{:S(2)}) %collective-permute-start.3) | collective-permute-done | bytes 262176 | tf_op jit(solution)/shard_map/ppermute | solution.py:152
  23.2 0.0 collective-permute-start.4
  23.2 0.0 collective-permute-done.5.refs_0_
  23.2 0.5 collective-permute-start.6
  23.7 4.6 %collective-permute-done.7.refs_0_ = bf16[2,128,512]{2,1,0:T(8,128)(2,1)S(1)} collective-permute-done((bf16[2,128,512]{2,1,0:T(8,128)(2,1)S(1)}, bf16[2,128,512]{2,1,0:T(8,128)(2,1)S(1)}, u32[]{:S(2)}, u32[]{:S(2)}) %collective-permute-start.7) | collective-permute-done | bytes 262176 | tf_op jit(solution)/shard_map/ppermute | solution.py:192
  28.3 0.0 collective-permute-start.8
  29.7 0.0 copy-start
  29.7 1.6 %copy-done = bf16[1,1,2,512,1024]{4,3,2,1,0:T(8,128)(2,1)S(1)} copy-done((bf16[1,1,2,512,1024]{4,3,2,1,0:T(8,128)(2,1)S(1)}, bf16[1,1,2,512,1024]{4,3,2,1,0:T(8,128)(2,1)}, u32[]{:S(2)}) %copy-start) | copy-done | bytes 2097176
  31.3 0.7 %copy-done.3 = f32[1,512]{1,0:T(1,128)S(1)} copy-done((f32[1,512]{1,0:T(1,128)S(1)}, f32[1,512]{1,0:T(1,128)}, u32[]{:S(2)}) %copy-start.3) | copy-done | bytes 2072
  32.0 1.8 %shard_map.69 = (f32[2,512,512]{2,1,0:T(8,128)S(1)}, f32[512,128]{1,0:T(8,128)S(1)}) custom-call(s32[1]{0:T(128)S(6)} %copy.8.m_ref, s32[1]{0:T(128)S(6)} %copy.9.mask_ref, bf16[2,512,1024]{2,1,0:T(8,128)(2,1)S(1)} %bitcast.7, f32[1,512]{1,0:T(1,128)S(1)} %copy-done.3, bf16[2,128,512]{2,1,0:T(8,128)(2,1)S(1)} %get-tuple-element.14.refs_0_, ...), custom_call_target="tpu_custom_call" | custom-call | flops 1610612736 | bytes 5242880 | tf_op jit(solution)/shard_map/pallas_call | solution.py:167
  33.8 1.0 %shard_map.70 = (f32[2,512,512]{2,1,0:T(8,128)S(1)}, f32[8,128]{1,0:T(8,128)S(1)}) custom-call(s32[1]{0:T(128)S(6)} %copy.8.m_ref, bf16[2,512,1024]{2,1,0:T(8,128)(2,1)S(1)} %bitcast.8, f32[512,128]{1,0:T(8,128)S(1)} %get-tuple-element.17.weight_ref, f32[2,512,512]{2,1,0:T(8,128)S(1)} %get-tuple-element.18.before_ref, ...), custom_call_target="tpu_custom_call" | custom-call | flops 536870912 | bytes 3145728 | tf_op jit(solution)/shard_map/pallas_call | solution.py:167
  34.8 1.3 %collective-permute-start.9 = (f32[8,128]{1,0:T(8,128)S(1)}, f32[8,128]{1,0:T(8,128)S(1)}, u32[]{:S(2)}, u32[]{:S(2)}) collective-permute-start(f32[8,128]{1,0:T(8,128)S(1)} %get-tuple-element.21), channel_id=1, source_target_pairs={{0,4},{12,8},{1,5},{13,9},{2,6},{14,10},{3,7},{15,11},{16,20},{28,... | collective-permute-start | bytes 12296 | tf_op jit(solution)/shard_map/ppermute | solution.py:213
  36.1 0.5 shard_map.71.before_ref
  36.6 3.7 %collective-permute-done.9.refs_1_ = f32[8,128]{1,0:T(8,128)S(1)} collective-permute-done((f32[8,128]{1,0:T(8,128)S(1)}, f32[8,128]{1,0:T(8,128)S(1)}, u32[]{:S(2)}, u32[]{:S(2)}) %collective-permute-start.9) | collective-permute-done | bytes 4128 | tf_op jit(solution)/shard_map/ppermute | solution.py:213
  40.3 0.7 %shard_map.73 = (f32[2,512,512]{2,1,0:T(8,128)S(1)}, f32[8,128]{1,0:T(8,128)S(1)}) custom-call(s32[1]{0:T(128)S(6)} %copy.8.m_ref, bf16[2,512,1024]{2,1,0:T(8,128)(2,1)S(1)} %bitcast.10, f32[512,128]{1,0:T(8,128)S(1)} %get-tuple-element.17.weight_ref, f32[2,512,512]{2,1,0:T(8,128)S(1)} %shard_map.71.before_ref, ...), custom_call_target="tpu_custom_call" | custom-call | flops 268435456 | bytes 2621440 | tf_op jit(solution)/shard_map/pallas_call | solution.py:167
  41.0 0.1 collective-permute-start.10
  41.1 1.2 %collective-permute-done.10 = f32[8,128]{1,0:T(8,128)S(1)} collective-permute-done((f32[8,128]{1,0:T(8,128)S(1)}, f32[8,128]{1,0:T(8,128)S(1)}, u32[]{:S(2)}, u32[]{:S(2)}) %collective-permute-start.10) | collective-permute-done | bytes 4128 | tf_op jit(solution)/shard_map/ppermute | solution.py:152
  42.2 0.5 collective-permute-start.11
  42.7 3.1 %collective-permute-done.11 = f32[8,128]{1,0:T(8,128)S(1)} collective-permute-done((f32[8,128]{1,0:T(8,128)S(1)}, f32[8,128]{1,0:T(8,128)S(1)}, u32[]{:S(2)}, u32[]{:S(2)}) %collective-permute-start.11) | collective-permute-done | bytes 4128 | tf_op jit(solution)/shard_map/ppermute | solution.py:152
  45.8 2.6 %collective-permute-start.12 = (f32[8,128]{1,0:T(8,128)S(1)}, f32[8,128]{1,0:T(8,128)S(1)}, u32[]{:S(2)}, u32[]{:S(2)}) collective-permute-start(f32[8,128]{1,0:T(8,128)S(1)} %add.16), channel_id=1, source_target_pairs={{4,12},{8,0},{5,13},{9,1},{6,14},{10,2},{7,15},{11,3},{20,28},{24,... | collective-permute-start | bytes 12296 | tf_op jit(solution)/shard_map/ppermute | solution.py:227
  48.5 1.3 %collective-permute-start.13 = (f32[8,128]{1,0:T(8,128)S(1)}, f32[8,128]{1,0:T(8,128)S(1)}, u32[]{:S(2)}, u32[]{:S(2)}) collective-permute-start(f32[8,128]{1,0:T(8,128)S(1)} %add.16), channel_id=1, source_target_pairs={{4,0},{8,12},{5,1},{9,13},{6,2},{10,14},{7,3},{11,15},{20,16},{24,... | collective-permute-start | bytes 12296 | tf_op jit(solution)/shard_map/ppermute | solution.py:228
  49.8 2.5 %collective-permute-start.14 = (f32[8,128]{1,0:T(8,128)S(1)}, f32[8,128]{1,0:T(8,128)S(1)}, u32[]{:S(2)}, u32[]{:S(2)}) collective-permute-start(f32[8,128]{1,0:T(8,128)S(1)} %add.16), channel_id=1, source_target_pairs={{4,8},{8,4},{5,9},{9,5},{6,10},{10,6},{7,11},{11,7},{20,24},{24,20... | collective-permute-start | bytes 12296 | tf_op jit(solution)/shard_map/ppermute | solution.py:229
  52.3 3.0 %collective-permute-done.14 = f32[8,128]{1,0:T(8,128)S(1)} collective-permute-done((f32[8,128]{1,0:T(8,128)S(1)}, f32[8,128]{1,0:T(8,128)S(1)}, u32[]{:S(2)}, u32[]{:S(2)}) %collective-permute-start.14) | collective-permute-done | bytes 4128 | tf_op jit(solution)/shard_map/ppermute | solution.py:229
  55.3 1.7 %shard_map.74 = (bf16[2,512,512]{2,1,0:T(8,128)(2,1)}, f32[1,128]{1,0:T(1,128)}) custom-call(s32[1]{0:T(128)S(6)} %copy.9.mask_ref, f32[8,128]{1,0:T(8,128)S(1)} %add_add_fusion.total_ref, f32[2,512,512]{2,1,0:T(8,128)S(1)} %get-tuple-element.23.vis_ref), custom_call_target="tpu_custom_call" | custom-call | bytes 2097152 | tf_op jit(solution)/shard_map/pallas_call | solution.py:167
  (16 shorter events, 0.1 us)
Async XLA Ops:
  0.6 1.2 %copy-start.2 = (bf16[2,1,128,4,512]{4,3,2,1,0:T(4,128)(2,1)S(1)}, bf16[2,1,128,4,512]{4,3,2,1,0:T(4,128)(2,1)}, u32[]{:S(2)}) copy-start(bf16[2,1,128,4,512]{4,3,2,1,0:T(4,128)(2,1)} %param.5) | copy-start | bytes 3145732
  2.2 11.0 %collective-permute-start.1 = (bf16[2,128,512]{2,1,0:T(8,128)(2,1)S(1)}, bf16[2,128,512]{2,1,0:T(8,128)(2,1)S(1)}, u32[]{:S(2)}, u32[]{:S(2)}) collective-permute-start(bf16[2,128,512]{2,1,0:T(8,128)(2,1)S(1)} %get-tuple-element.15), channel_id=1, source_target_pairs={{0,4},{4,0},{8,12},{12,8},{1,5},{5,1},{9,13},{13,9},{2,6},{6,2},{1... | collective-permute-start | bytes 786440 | tf_op jit(solution)/shard_map/ppermute | solution.py:152
  2.7 20.5 %collective-permute-start.3 = (bf16[2,128,512]{2,1,0:T(8,128)(2,1)S(1)}, bf16[2,128,512]{2,1,0:T(8,128)(2,1)S(1)}, u32[]{:S(2)}, u32[]{:S(2)}) collective-permute-start(bf16[2,128,512]{2,1,0:T(8,128)(2,1)S(1)} %get-tuple-element.16), channel_id=1, source_target_pairs={{0,8},{4,12},{8,0},{12,4},{1,9},{5,13},{9,1},{13,5},{2,10},{6,14},... | collective-permute-start | bytes 786440 | tf_op jit(solution)/shard_map/ppermute | solution.py:152
  5.3 17.9 %collective-permute-start.5 = (bf16[2,128,512]{2,1,0:T(8,128)(2,1)S(1)}, bf16[2,128,512]{2,1,0:T(8,128)(2,1)S(1)}, u32[]{:S(2)}, u32[]{:S(2)}) collective-permute-start(bf16[2,128,512]{2,1,0:T(8,128)(2,1)S(1)} %get-tuple-element.19), channel_id=1, source_target_pairs={{0,12},{12,0},{1,13},{13,1},{2,14},{14,2},{3,15},{15,3},{16,28},{2... | collective-permute-start | bytes 786440 | tf_op jit(solution)/shard_map/ppermute | solution.py:191
  5.9 22.4 %collective-permute-start.7 = (bf16[2,128,512]{2,1,0:T(8,128)(2,1)S(1)}, bf16[2,128,512]{2,1,0:T(8,128)(2,1)S(1)}, u32[]{:S(2)}, u32[]{:S(2)}) collective-permute-start(bf16[2,128,512]{2,1,0:T(8,128)(2,1)S(1)} %get-tuple-element.19), channel_id=1, source_target_pairs={{4,8},{8,4},{5,9},{9,5},{6,10},{10,6},{7,11},{11,7},{20,24},{24,20... | collective-permute-start | bytes 786440 | tf_op jit(solution)/shard_map/ppermute | solution.py:192
  8.3 21.4 %collective-permute-start = (bf16[2,128,512]{2,1,0:T(8,128)(2,1)S(1)}, bf16[2,128,512]{2,1,0:T(8,128)(2,1)S(1)}, u32[]{:S(2)}, u32[]{:S(2)}) collective-permute-start(bf16[2,128,512]{2,1,0:T(8,128)(2,1)S(1)} %get-tuple-element.14.refs_0_), channel_id=1, source_target_pairs={{0,1},{1,0},{2,3},{3,2},{4,5},{5,4},{6,7},{7,6},{8,9},{9,8},{10,11... | collective-permute-start | bytes 786440 | tf_op jit(solution)/shard_map/ppermute | solution.py:152
  13.1 16.6 %collective-permute-start.2 = (bf16[2,128,512]{2,1,0:T(8,128)(2,1)S(1)}, bf16[2,128,512]{2,1,0:T(8,128)(2,1)S(1)}, u32[]{:S(2)}, u32[]{:S(2)}) collective-permute-start(bf16[2,128,512]{2,1,0:T(8,128)(2,1)S(1)} %collective-permute-done.1.refs_2_), channel_id=1, source_target_pairs={{0,1},{1,0},{2,3},{3,2},{4,5},{5,4},{6,7},{7,6},{8,9},{9,8},{10,11... | collective-permute-start | bytes 786440 | tf_op jit(solution)/shard_map/ppermute | solution.py:152
  23.2 6.5 %collective-permute-start.4 = (bf16[2,128,512]{2,1,0:T(8,128)(2,1)S(1)}, bf16[2,128,512]{2,1,0:T(8,128)(2,1)S(1)}, u32[]{:S(2)}, u32[]{:S(2)}) collective-permute-start(bf16[2,128,512]{2,1,0:T(8,128)(2,1)S(1)} %collective-permute-done.3.refs_4_), channel_id=1, source_target_pairs={{0,1},{1,0},{2,3},{3,2},{4,5},{5,4},{6,7},{7,6},{8,9},{9,8},{10,11... | collective-permute-start | bytes 786440 | tf_op jit(solution)/shard_map/ppermute | solution.py:152
  23.2 10.6 %collective-permute-start.6 = (bf16[2,128,512]{2,1,0:T(8,128)(2,1)S(1)}, bf16[2,128,512]{2,1,0:T(8,128)(2,1)S(1)}, u32[]{:S(2)}, u32[]{:S(2)}) collective-permute-start(bf16[2,128,512]{2,1,0:T(8,128)(2,1)S(1)} %collective-permute-done.5.refs_0_), channel_id=1, source_target_pairs={{0,1},{1,0},{2,3},{3,2},{4,5},{5,4},{6,7},{7,6},{8,9},{9,8},{10,11... | collective-permute-start | bytes 786440 | tf_op jit(solution)/shard_map/ppermute | solution.py:152
  28.3 8.2 %collective-permute-start.8 = (bf16[2,128,512]{2,1,0:T(8,128)(2,1)S(1)}, bf16[2,128,512]{2,1,0:T(8,128)(2,1)S(1)}, u32[]{:S(2)}, u32[]{:S(2)}) collective-permute-start(bf16[2,128,512]{2,1,0:T(8,128)(2,1)S(1)} %collective-permute-done.7.refs_0_), channel_id=1, source_target_pairs={{0,1},{1,0},{2,3},{3,2},{4,5},{5,4},{6,7},{7,6},{8,9},{9,8},{10,11... | collective-permute-start | bytes 786440 | tf_op jit(solution)/shard_map/ppermute | solution.py:152
  29.7 1.6 %copy-start = (bf16[1,1,2,512,1024]{4,3,2,1,0:T(8,128)(2,1)S(1)}, bf16[1,1,2,512,1024]{4,3,2,1,0:T(8,128)(2,1)}, u32[]{:S(2)}) copy-start(bf16[1,1,2,512,1024]{4,3,2,1,0:T(8,128)(2,1)} %param.6) | copy-start | bytes 6291460
  31.3 0.7 %copy-start.3 = (f32[1,512]{1,0:T(1,128)S(1)}, f32[1,512]{1,0:T(1,128)}, u32[]{:S(2)}) copy-start(f32[1,512]{1,0:T(1,128)} %noise_ref.1) | copy-start | bytes 6148
  32.0 1.8 %copy-start.1 = (bf16[1,1,2,512,1024]{4,3,2,1,0:T(8,128)(2,1)S(1)}, bf16[1,1,2,512,1024]{4,3,2,1,0:T(8,128)(2,1)}, u32[]{:S(2)}) copy-start(bf16[1,1,2,512,1024]{4,3,2,1,0:T(8,128)(2,1)} %param.6) | copy-start | bytes 6291460
  34.8 5.5 %collective-permute-start.9 = (f32[8,128]{1,0:T(8,128)S(1)}, f32[8,128]{1,0:T(8,128)S(1)}, u32[]{:S(2)}, u32[]{:S(2)}) collective-permute-start(f32[8,128]{1,0:T(8,128)S(1)} %get-tuple-element.21), channel_id=1, source_target_pairs={{0,4},{12,8},{1,5},{13,9},{2,6},{14,10},{3,7},{15,11},{16,20},{28,... | collective-permute-start | bytes 12296 | tf_op jit(solution)/shard_map/ppermute | solution.py:213
  41.0 1.2 %collective-permute-start.10 = (f32[8,128]{1,0:T(8,128)S(1)}, f32[8,128]{1,0:T(8,128)S(1)}, u32[]{:S(2)}, u32[]{:S(2)}) collective-permute-start(f32[8,128]{1,0:T(8,128)S(1)} %get-tuple-element.22), channel_id=1, source_target_pairs={{0,1},{1,0},{2,3},{3,2},{4,5},{5,4},{6,7},{7,6},{8,9},{9,8},{10,11... | collective-permute-start | bytes 12296 | tf_op jit(solution)/shard_map/ppermute | solution.py:152
  42.2 3.6 %collective-permute-start.11 = (f32[8,128]{1,0:T(8,128)S(1)}, f32[8,128]{1,0:T(8,128)S(1)}, u32[]{:S(2)}, u32[]{:S(2)}) collective-permute-start(f32[8,128]{1,0:T(8,128)S(1)} %add.15), channel_id=1, source_target_pairs={{0,2},{2,0},{1,3},{3,1},{4,6},{6,4},{5,7},{7,5},{8,10},{10,8},{9,1... | collective-permute-start | bytes 12296 | tf_op jit(solution)/shard_map/ppermute | solution.py:152
  45.8 6.4 %collective-permute-start.12 = (f32[8,128]{1,0:T(8,128)S(1)}, f32[8,128]{1,0:T(8,128)S(1)}, u32[]{:S(2)}, u32[]{:S(2)}) collective-permute-start(f32[8,128]{1,0:T(8,128)S(1)} %add.16), channel_id=1, source_target_pairs={{4,12},{8,0},{5,13},{9,1},{6,14},{10,2},{7,15},{11,3},{20,28},{24,... | collective-permute-start | bytes 12296 | tf_op jit(solution)/shard_map/ppermute | solution.py:227
  48.5 3.8 %collective-permute-start.13 = (f32[8,128]{1,0:T(8,128)S(1)}, f32[8,128]{1,0:T(8,128)S(1)}, u32[]{:S(2)}, u32[]{:S(2)}) collective-permute-start(f32[8,128]{1,0:T(8,128)S(1)} %add.16), channel_id=1, source_target_pairs={{4,0},{8,12},{5,1},{9,13},{6,2},{10,14},{7,3},{11,15},{20,16},{24,... | collective-permute-start | bytes 12296 | tf_op jit(solution)/shard_map/ppermute | solution.py:228
  49.8 5.5 %collective-permute-start.14 = (f32[8,128]{1,0:T(8,128)S(1)}, f32[8,128]{1,0:T(8,128)S(1)}, u32[]{:S(2)}, u32[]{:S(2)}) collective-permute-start(f32[8,128]{1,0:T(8,128)S(1)} %add.16), channel_id=1, source_target_pairs={{4,8},{8,4},{5,9},{9,5},{6,10},{10,6},{7,11},{11,7},{20,24},{24,20... | collective-permute-start | bytes 12296 | tf_op jit(solution)/shard_map/ppermute | solution.py:229

commit v2 on v1

--- a/solution.py
+++ b/solution.py
@@ -9,6 +9,7 @@
 
 VMEM = pl.BlockSpec(memory_space=pltpu.VMEM)
 SMEM = pl.BlockSpec(memory_space=pltpu.SMEM)
+HBM = pl.BlockSpec(memory_space=pltpu.HBM)
 
 
 def column(row):
@@ -24,19 +25,38 @@
             ref[c] = modes_ref[place ^ step]
 
 
-def contract(m_ref, beam_ref, block_refs, steps):
+def load_kernel(beam_ref, noise_ref, left_ref, weight_ref, sems):
+    _, _, total = beam_ref.shape
+    blocks = left_ref.shape[0]
+    ell = total // blocks
+    copies = []
+    for block in range(blocks):
+        for c in range(2):
+            copies.append(
+                pltpu.make_async_copy(
+                    beam_ref.at[c, :, pl.ds(block * ell, ell)],
+                    left_ref.at[block, :, pl.ds(c * ell, ell)],
+                    sems.at[2 * block + c],
+                )
+            )
+            copies[-1].start()
+    weight_ref[...] = column(lax.rsqrt(noise_ref[...]))
+    for copy in copies:
+        copy.wait()
+
+
+def contract(m_ref, left_ref, block_refs, steps):
     ell = block_refs[0].shape[1]
     left, right_real, right_imag = [], [], []
     for ref, (step, other) in zip(block_refs, steps, strict=True):
         owner = lax.axis_index("ma") ^ step
         half = lax.axis_index("pol") ^ other
-        start = (owner * lax.axis_size("pol") + half) * ell
-        columns = pl.ds(pl.multiple_of(start, ell), ell)
-        degree = start + lax.broadcasted_iota(jnp.int32, (ell, ref.shape[2]), 0)
+        block = owner * lax.axis_size("pol") + half
+        degree = block * ell + lax.broadcasted_iota(jnp.int32, (ell, ref.shape[2]), 0)
         keep = degree >= m_ref[0]
         real = jnp.where(keep, ref[0], jnp.zeros((), ref.dtype))
         imag = jnp.where(keep, ref[1], jnp.zeros((), ref.dtype))
-        left += [beam_ref[0, :, columns], beam_ref[1, :, columns]]
+        left.append(left_ref[block])
         right_real += [real, -imag]
         right_imag += [imag, real]
     left = jnp.concatenate(left, axis=1)
@@ -47,15 +67,10 @@
     )
 
 
-def first_kernel(steps, m_ref, mask_ref, beam_ref, noise_ref, *refs):
-    *blocks, vis_ref, weight_ref = refs
-    vis_ref[0], vis_ref[1] = contract(m_ref, beam_ref, blocks, steps)
-    weight_ref[...] = column(lax.rsqrt(noise_ref[...]))
-
-
-def at_edge():
-    place = lax.axis_index("ma")
-    return (place == 0) | (place == lax.axis_size("ma") - 1)
+def first_kernel(steps, m_ref, mask_ref, left_ref, *refs):
+    del mask_ref
+    *blocks, vis_ref = refs
+    vis_ref[0], vis_ref[1] = contract(m_ref, left_ref, blocks, steps)
 
 
 def weigh(vis, weight):
@@ -72,37 +87,16 @@
     return jnp.sum(folded)
 
 
-def edge_kernel(steps, m_ref, beam_ref, weight_ref, before_ref, *refs):
-    *blocks, vis_ref, power_ref = refs
-    real, imag = contract(m_ref, beam_ref, blocks, steps)
-    real += before_ref[0]
-    imag += before_ref[1]
-    vis_ref[0] = real
-    vis_ref[1] = imag
-    weight = weight_ref[...]
-    total = power_of(weigh(real, weight), weigh(imag, weight))
-    lane = lax.broadcasted_iota(jnp.int32, power_ref.shape, 1)
-    here = (lane == lax.axis_index("freq")) & at_edge()
-    power_ref[...] = jnp.where(here, total, 0.0)
-
-
-def next_kernel(steps, m_ref, beam_ref, before_ref, *refs):
+def next_kernel(steps, m_ref, left_ref, before_ref, *refs):
     *blocks, vis_ref = refs
-    real, imag = contract(m_ref, beam_ref, blocks, steps)
+    real, imag = contract(m_ref, left_ref, blocks, steps)
     vis_ref[0] = real + before_ref[0]
     vis_ref[1] = imag + before_ref[1]
 
 
-def live_kernel(slots, mask_ref, live_ref):
-    lane = lax.broadcasted_iota(jnp.int32, live_ref.shape, 1)
-    leader = (lax.axis_index("ma") == 1) & (lax.axis_index("pol") == 0)
-    here = (lane == lax.axis_index("freq") + slots) & leader
-    live_ref[...] = jnp.where(here, mask_ref[0].astype(jnp.float32), 0.0)
-
-
-def last_kernel(steps, m_ref, beam_ref, weight_ref, before_ref, *refs):
-    *blocks, edge_ref, live_ref, vis_ref, power_ref = refs
-    real, imag = contract(m_ref, beam_ref, blocks, steps)
+def last_kernel(steps, slots, m_ref, mask_ref, left_ref, weight_ref, before_ref, *refs):
+    *blocks, vis_ref, power_ref = refs
+    real, imag = contract(m_ref, left_ref, blocks, steps)
     weight = weight_ref[...]
     real = weigh(real + before_ref[0], weight)
     imag = weigh(imag + before_ref[1], weight)
@@ -110,11 +104,15 @@
     vis_ref[1] = imag
     total = power_of(real, imag)
     lane = lax.broadcasted_iota(jnp.int32, power_ref.shape, 1)
-    here = (lane == lax.axis_index("freq")) & jnp.logical_not(at_edge())
-    power_ref[...] = jnp.where(here, total, 0.0) + edge_ref[...] + live_ref[...]
-
-
-def finish_kernel(slots, modes, mask_ref, total_ref, vis_ref, scaled_ref, power_ref, held_ref, sems):
+    leader = (lax.axis_index("ma") == 0) & (lax.axis_index("pol") == 0)
+    live = jnp.where(leader, mask_ref[0], 0).astype(jnp.float32)
+    channel = lax.axis_index("freq")
+    power_ref[...] = jnp.where(lane == channel, total, 0.0) + jnp.where(
+        lane == channel + slots, live, 0.0
+    )
+
+
+def finish_kernel(slots, modes, mask_ref, total_ref, vis_ref, scaled_ref, power_ref, held_ref, own_ref, sems):
     lane = lax.broadcasted_iota(jnp.int32, (1, 128), 1)
     totals = total_ref[0:1, :]
     powers = totals / modes
@@ -127,8 +125,9 @@
     own = over(lane == lax.axis_index("freq"), powers)
     mask = mask_ref[0].astype(jnp.float32)
     factor = mask / jnp.sqrt(0.5 * own + 0.5 * band + 1e-06)
-    power_ref[...] = jnp.where(lane == 0, own, 0.0)
-    copies = []
+    own_ref[...] = jnp.where(lane == 0, own, 0.0)
+    copies = [pltpu.make_async_copy(own_ref, power_ref, sems.at[0])]
+    copies[0].start()
     parts, rows, _ = vis_ref.shape
     chunk = rows // 4
     for c in range(parts):
@@ -167,7 +166,7 @@
         return pl.pallas_call(
             kernel,
             out_shape=out_shape,
-            in_specs=[SMEM] * len(scalars) + [VMEM] * len(operands),
+            in_specs=more.pop("in_specs", [SMEM] * len(scalars) + [VMEM] * len(operands)),
             out_specs=more.pop("out_specs", jax.tree.map(lambda _: VMEM, out_shape)),
             compiler_params=params,
             cost_estimate=pl.CostEstimate(
@@ -178,56 +177,54 @@
             **more,
         )(*scalars, *operands)
 
-    two, one, three, own = call(
-        functools.partial(split_kernel, (2, 1, 3, 0)),
+    three, one, two, own = call(
+        functools.partial(split_kernel, (3, 1, 2, 0)),
         [slab] * n_ma,
         (),
         (alm[:, 0],),
         0,
         scratch_shapes=[pltpu.VMEM((n_ma, ell, maps), alm.dtype)],
     )
+    three = swap(three, "ma", 3)
+    one = swap(one, "ma", 1)
     two = swap(two, "ma", 2)
-    one = swap(one, "ma", 1)
-    edge = lax.ppermute(three, "ma", [(0, 3), (3, 0)])
-    middle = lax.ppermute(three, "ma", [(1, 2), (2, 1)])
     own_far = swap(own, "pol", 1)
     one_far = swap(one, "pol", 1)
+    three_far = swap(three, "pol", 1)
     two_far = swap(two, "pol", 1)
-    edge_far = swap(edge, "pol", 1)
-    middle_far = swap(middle, "pol", 1)
-    steps = ((0, 0), (0, 1), (1, 0), (1, 1), (2, 0), (2, 1))
-    vis, weight = call(
+    blocks = n_ma * n_pol
+    left, weight = call(
+        load_kernel,
+        (jax.ShapeDtypeStruct((blocks, modes, 2 * ell), beam.dtype), weights),
+        (),
+        (response, noise),
+        0,
+        in_specs=[HBM, VMEM],
+        scratch_shapes=[pltpu.SemaphoreType.DMA((2 * blocks,))],
+    )
+    steps = ((0, 0), (0, 1), (1, 0), (1, 1), (3, 0), (3, 1))
+    vis = call(
         functools.partial(first_kernel, steps),
-        (vis_shape, weights),
+        vis_shape,
         (m_table, chan_mask),
-        (response, noise, own, own_far, one, one_far, two, two_far),
+        (left, own, own_far, one, one_far, three, three_far),
         6,
     )
-    vis, edge_power = call(
-        functools.partial(edge_kernel, ((3, 0), (3, 1))),
+    vis = call(
+        functools.partial(next_kernel, ((2, 0),)), vis_shape, (m_table,), (left, vis, two), 1
+    )
+    vis, total = call(
+        functools.partial(last_kernel, ((2, 1),), n_freq),
         (vis_shape, row),
-        (m_table,),
-        (response, weight, vis, edge, edge_far),
-        2,
-    )
-    edge_power = lax.ppermute(edge_power, "ma", [(0, 1), (3, 2)])
-    live = call(functools.partial(live_kernel, n_freq), row, (chan_mask,), (), 0)
-    vis = call(
-        functools.partial(next_kernel, ((3, 0),)), vis_shape, (m_table,), (response, vis, middle), 1
-    )
-    vis, total = call(
-        functools.partial(last_kernel, ((3, 1),)),
-        (vis_shape, row),
-        (m_table,),
-        (response, weight, vis, middle_far, edge_power, live),
+        (m_table, chan_mask),
+        (left, weight, vis, two_far),
         1,
     )
-    total += swap(total, "pol", 1)
-    total += swap(total, "freq", 1)
-    beyond = lax.ppermute(total, "ma", [(1, 3), (2, 0)])
-    beside = lax.ppermute(total, "ma", [(1, 0), (2, 3)])
-    across = lax.ppermute(total, "ma", [(1, 2), (2, 1)])
-    total = total + beyond + beside + across
+    for name in ("pol", "freq", "ma"):
+        step = 1
+        while step < lax.axis_size(name):
+            total = total + swap(total, name, step)
+            step *= 2
     scaled, own_power = call(
         functools.partial(finish_kernel, n_freq, n_ma * n_pol * modes * maps),
         (
@@ -237,10 +234,11 @@
         (chan_mask,),
         (total, vis),
         0,
-        out_specs=(pl.BlockSpec(memory_space=pltpu.HBM), VMEM),
+        out_specs=(HBM, HBM),
         scratch_shapes=[
             pltpu.VMEM((parts, modes, maps), jnp.bfloat16),
-            pltpu.SemaphoreType.DMA((4 * parts,)),
+            pltpu.VMEM((1, 128), jnp.float32),
+            pltpu.SemaphoreType.DMA((4 * parts + 1,)),
         ],
     )
     return scaled[:, None, None], own_power[0, :1]

time: 57.3 us -> 52.8 us (0.921)
  the two profiles are of different devices: /device:TPU:14 before, /device:TPU:0 now
where the time goes in v2:
time: 52.8 us; the launch traced here: 52.6 us
  waiting for transfers between devices  32.7 us (62%)
  starting transfers between devices  8.97 us (17%)
  Pallas kernels  5.35 us (10%)
  local copies, waits for them, and re-layouts  3.49 us (7%)
  between operations  2.02 us (4%)
    ppermute x11, waiting for transfers between devices, swap(): lax.ppermute(x, name, [(i, i ^ step) for i in range(lax.axis_size(name))])  32.7 us
    ppermute x11, starting transfers between devices, swap(): lax.ppermute(x, name, [(i, i ^ step) for i in range(lax.axis_size(name))])  8.97 us
    pallas_call x6, Pallas kernels, call(): pl.pallas_call(kernel, out_shape=out_shape, in_specs=more.pop('in_specs',...  5.35 us
    unnamed x6, local copies, waits for them, and re-layouts  3.49 us
  transfers between devices with their start and end apart: 11, of which 7 were waited for; matrix products, arithmetic and copies ran while one was open for 0% of the time, Pallas kernels for 6%

profile of v2, /device:TPU:0, one launch (start us, length us, event | category | flops | bytes accessed | tf_op | source)
XLA Modules:
  0.0 52.6 jit_solution(5566786431346180658)
XLA Ops:
  0.6 1.2 %copy-done.1 = bf16[2,1,128,4,512]{4,3,2,1,0:T(4,128)(2,1)S(1)} copy-done((bf16[2,1,128,4,512]{4,3,2,1,0:T(4,128)(2,1)S(1)}, bf16[2,1,128,4,512]{4,3,2,1,0:T(4,128)(2,1)}, u32[]{:S(2)}) %copy-start.1) | copy-done | bytes 1048600
  1.9 0.3 shard_map.69
  2.2 3.1 %collective-permute-start.1 = (bf16[2,128,512]{2,1,0:T(8,128)(2,1)S(1)}, bf16[2,128,512]{2,1,0:T(8,128)(2,1)S(1)}, u32[]{:S(2)}, u32[]{:S(2)}) collective-permute-start(bf16[2,128,512]{2,1,0:T(8,128)(2,1)S(1)} %get-tuple-element.15), channel_id=1, source_target_pairs={{0,4},{4,0},{8,12},{12,8},{1,5},{5,1},{9,13},{13,9},{2,6},{6,2},{1... | collective-permute-start | bytes 786440 | tf_op jit(solution)/shard_map/ppermute | solution.py:151
  5.3 2.5 %collective-permute-start.3 = (bf16[2,128,512]{2,1,0:T(8,128)(2,1)S(1)}, bf16[2,128,512]{2,1,0:T(8,128)(2,1)S(1)}, u32[]{:S(2)}, u32[]{:S(2)}) collective-permute-start(bf16[2,128,512]{2,1,0:T(8,128)(2,1)S(1)} %get-tuple-element.16), channel_id=1, source_target_pairs={{0,12},{4,8},{8,4},{12,0},{1,13},{5,9},{9,5},{13,1},{2,14},{6,10},... | collective-permute-start | bytes 786440 | tf_op jit(solution)/shard_map/ppermute | solution.py:151
  7.7 0.1 collective-permute-start.5
  7.9 0.0 collective-permute-start
  7.9 4.1 %collective-permute-done.1.refs_2_ = bf16[2,128,512]{2,1,0:T(8,128)(2,1)S(1)} collective-permute-done((bf16[2,128,512]{2,1,0:T(8,128)(2,1)S(1)}, bf16[2,128,512]{2,1,0:T(8,128)(2,1)S(1)}, u32[]{:S(2)}, u32[]{:S(2)}) %collective-permute-start.1) | collective-permute-done | bytes 262176 | tf_op jit(solution)/shard_map/ppermute | solution.py:151
  12.0 0.0 collective-permute-start.2
  12.0 8.6 %collective-permute-done.3.refs_4_ = bf16[2,128,512]{2,1,0:T(8,128)(2,1)S(1)} collective-permute-done((bf16[2,128,512]{2,1,0:T(8,128)(2,1)S(1)}, bf16[2,128,512]{2,1,0:T(8,128)(2,1)S(1)}, u32[]{:S(2)}, u32[]{:S(2)}) %collective-permute-start.3) | collective-permute-done | bytes 262176 | tf_op jit(solution)/shard_map/ppermute | solution.py:151
  20.6 0.0 collective-permute-start.4
  20.6 10.1 %collective-permute-done.5.refs_0_ = bf16[2,128,512]{2,1,0:T(8,128)(2,1)S(1)} collective-permute-done((bf16[2,128,512]{2,1,0:T(8,128)(2,1)S(1)}, bf16[2,128,512]{2,1,0:T(8,128)(2,1)S(1)}, u32[]{:S(2)}, u32[]{:S(2)}) %collective-permute-start.5) | collective-permute-done | bytes 262176 | tf_op jit(solution)/shard_map/ppermute | solution.py:151
  30.7 0.0 collective-permute-start.6
  32.0 0.0 copy-start
  32.1 1.6 %copy-done = bf16[1,1,2,512,1024]{4,3,2,1,0:T(8,128)(2,1)S(1)} copy-done((bf16[1,1,2,512,1024]{4,3,2,1,0:T(8,128)(2,1)S(1)}, bf16[1,1,2,512,1024]{4,3,2,1,0:T(8,128)(2,1)}, u32[]{:S(2)}) %copy-start) | copy-done | bytes 2097176
  33.6 0.7 %copy-done.2 = f32[1,512]{1,0:T(1,128)S(1)} copy-done((f32[1,512]{1,0:T(1,128)S(1)}, f32[1,512]{1,0:T(1,128)}, u32[]{:S(2)}) %copy-start.2) | copy-done | bytes 2072
  34.3 0.9 %shard_map.68 = (bf16[8,512,256]{2,1,0:T(8,128)(2,1)S(1)}, f32[512,128]{1,0:T(8,128)S(1)}) custom-call(bf16[2,512,1024]{2,1,0:T(8,128)(2,1)S(1)} %bitcast.7, f32[1,512]{1,0:T(1,128)S(1)} %copy-done.2), custom_call_target="tpu_custom_call" | custom-call | bytes 2097152 | tf_op jit(solution)/shard_map/pallas_call | solution.py:166
  35.2 0.0 collective-permute-done.refs_1_
  35.2 0.0 collective-permute-done.2.refs_3_
  35.2 0.0 collective-permute-done.4.refs_5_
  35.2 1.8 %shard_map.70.before_ref = f32[2,512,512]{2,1,0:T(8,128)S(1)} custom-call(s32[1]{0:T(128)S(6)} %copy.8.m_ref, s32[1]{0:T(128)S(6)} %copy.9.mask_ref, bf16[8,512,256]{2,1,0:T(8,128)(2,1)S(1)} %get-tuple-element.12.left_ref, bf16[2,128,512]{2,1,0:T(8,128)(2,1)S(1)} %get-tuple-element.14.refs_0_, bf16[2,128,512]{2,1,0:T(8,128)(2,1)S(1)} %collective-permute-done.refs_1_, ...), custom_call_target="tpu_custom_call" | custom-call | flops 1610612736 | bytes 5242880 | tf_op jit(solution)/shard_map/pallas_call | solution.py:166
  37.0 0.5 shard_map.71.before_ref
  37.5 0.0 collective-permute-done.6.refs_0_
  37.5 0.7 %shard_map.72 = (f32[2,512,512]{2,1,0:T(8,128)S(1)}, f32[8,128]{1,0:T(8,128)S(1)}) custom-call(s32[1]{0:T(128)S(6)} %copy.8.m_ref, s32[1]{0:T(128)S(6)} %copy.9.mask_ref, bf16[8,512,256]{2,1,0:T(8,128)(2,1)S(1)} %get-tuple-element.12.left_ref, f32[512,128]{1,0:T(8,128)S(1)} %get-tuple-element.13.weight_ref, f32[2,512,512]{2,1,0:T(8,128)S(1)} %shard_map.71.before_ref, ...), custom_call_target="tpu_custom_call" | custom-call | flops 268435456 | bytes 2621440 | tf_op jit(solution)/shard_map/pallas_call | solution.py:166
  38.2 0.6 %collective-permute-start.7 = (f32[8,128]{1,0:T(8,128)S(1)}, f32[8,128]{1,0:T(8,128)S(1)}, u32[]{:S(2)}, u32[]{:S(2)}) collective-permute-start(f32[8,128]{1,0:T(8,128)S(1)} %get-tuple-element.18), channel_id=1, source_target_pairs={{0,1},{1,0},{2,3},{3,2},{4,5},{5,4},{6,7},{7,6},{8,9},{9,8},{10,11... | collective-permute-start | bytes 12296 | tf_op jit(solution)/shard_map/ppermute | solution.py:151
  38.8 0.8 %collective-permute-done.7 = f32[8,128]{1,0:T(8,128)S(1)} collective-permute-done((f32[8,128]{1,0:T(8,128)S(1)}, f32[8,128]{1,0:T(8,128)S(1)}, u32[]{:S(2)}, u32[]{:S(2)}) %collective-permute-start.7) | collective-permute-done | bytes 4128 | tf_op jit(solution)/shard_map/ppermute | solution.py:151
  39.6 1.5 %collective-permute-start.8 = (f32[8,128]{1,0:T(8,128)S(1)}, f32[8,128]{1,0:T(8,128)S(1)}, u32[]{:S(2)}, u32[]{:S(2)}) collective-permute-start(f32[8,128]{1,0:T(8,128)S(1)} %add.12), channel_id=1, source_target_pairs={{0,2},{2,0},{1,3},{3,1},{4,6},{6,4},{5,7},{7,5},{8,10},{10,8},{9,1... | collective-permute-start | bytes 12296 | tf_op jit(solution)/shard_map/ppermute | solution.py:151
  41.1 2.1 %collective-permute-done.8 = f32[8,128]{1,0:T(8,128)S(1)} collective-permute-done((f32[8,128]{1,0:T(8,128)S(1)}, f32[8,128]{1,0:T(8,128)S(1)}, u32[]{:S(2)}, u32[]{:S(2)}) %collective-permute-start.8) | collective-permute-done | bytes 4128 | tf_op jit(solution)/shard_map/ppermute | solution.py:151
  43.2 0.0 collective-permute-start.9
  43.2 3.6 %collective-permute-done.9 = f32[8,128]{1,0:T(8,128)S(1)} collective-permute-done((f32[8,128]{1,0:T(8,128)S(1)}, f32[8,128]{1,0:T(8,128)S(1)}, u32[]{:S(2)}, u32[]{:S(2)}) %collective-permute-start.9) | collective-permute-done | bytes 4128 | tf_op jit(solution)/shard_map/ppermute | solution.py:151
  46.8 1.2 %collective-permute-start.10 = (f32[8,128]{1,0:T(8,128)S(1)}, f32[8,128]{1,0:T(8,128)S(1)}, u32[]{:S(2)}, u32[]{:S(2)}) collective-permute-start(f32[8,128]{1,0:T(8,128)S(1)} %add.14), channel_id=1, source_target_pairs={{0,8},{4,12},{8,0},{12,4},{1,9},{5,13},{9,1},{13,5},{2,10},{6,14},... | collective-permute-start | bytes 12296 | tf_op jit(solution)/shard_map/ppermute | solution.py:151
  48.0 3.3 %collective-permute-done.10 = f32[8,128]{1,0:T(8,128)S(1)} collective-permute-done((f32[8,128]{1,0:T(8,128)S(1)}, f32[8,128]{1,0:T(8,128)S(1)}, u32[]{:S(2)}, u32[]{:S(2)}) %collective-permute-start.10) | collective-permute-done | bytes 4128 | tf_op jit(solution)/shard_map/ppermute | solution.py:151
  51.3 1.2 %shard_map.73 = (bf16[2,512,512]{2,1,0:T(8,128)(2,1)}, f32[1,128]{1,0:T(1,128)}) custom-call(s32[1]{0:T(128)S(6)} %copy.9.mask_ref, f32[8,128]{1,0:T(8,128)S(1)} %add.15.total_ref, f32[2,512,512]{2,1,0:T(8,128)S(1)} %get-tuple-element.19.vis_ref), custom_call_target="tpu_custom_call" | custom-call | bytes 2097152 | tf_op jit(solution)/shard_map/pallas_call | solution.py:166
  (6 shorter events, 0.0 us)
Async XLA Ops:
  0.6 1.2 %copy-start.1 = (bf16[2,1,128,4,512]{4,3,2,1,0:T(4,128)(2,1)S(1)}, bf16[2,1,128,4,512]{4,3,2,1,0:T(4,128)(2,1)}, u32[]{:S(2)}) copy-start(bf16[2,1,128,4,512]{4,3,2,1,0:T(4,128)(2,1)} %param.5) | copy-start | bytes 3145732
  2.2 9.8 %collective-permute-start.1 = (bf16[2,128,512]{2,1,0:T(8,128)(2,1)S(1)}, bf16[2,128,512]{2,1,0:T(8,128)(2,1)S(1)}, u32[]{:S(2)}, u32[]{:S(2)}) collective-permute-start(bf16[2,128,512]{2,1,0:T(8,128)(2,1)S(1)} %get-tuple-element.15), channel_id=1, source_target_pairs={{0,4},{4,0},{8,12},{12,8},{1,5},{5,1},{9,13},{13,9},{2,6},{6,2},{1... | collective-permute-start | bytes 786440 | tf_op jit(solution)/shard_map/ppermute | solution.py:151
  5.3 15.3 %collective-permute-start.3 = (bf16[2,128,512]{2,1,0:T(8,128)(2,1)S(1)}, bf16[2,128,512]{2,1,0:T(8,128)(2,1)S(1)}, u32[]{:S(2)}, u32[]{:S(2)}) collective-permute-start(bf16[2,128,512]{2,1,0:T(8,128)(2,1)S(1)} %get-tuple-element.16), channel_id=1, source_target_pairs={{0,12},{4,8},{8,4},{12,0},{1,13},{5,9},{9,5},{13,1},{2,14},{6,10},... | collective-permute-start | bytes 786440 | tf_op jit(solution)/shard_map/ppermute | solution.py:151
  7.7 23.0 %collective-permute-start.5 = (bf16[2,128,512]{2,1,0:T(8,128)(2,1)S(1)}, bf16[2,128,512]{2,1,0:T(8,128)(2,1)S(1)}, u32[]{:S(2)}, u32[]{:S(2)}) collective-permute-start(bf16[2,128,512]{2,1,0:T(8,128)(2,1)S(1)} %get-tuple-element.17), channel_id=1, source_target_pairs={{0,8},{4,12},{8,0},{12,4},{1,9},{5,13},{9,1},{13,5},{2,10},{6,14},... | collective-permute-start | bytes 786440 | tf_op jit(solution)/shard_map/ppermute | solution.py:151
  7.9 27.3 %collective-permute-start = (bf16[2,128,512]{2,1,0:T(8,128)(2,1)S(1)}, bf16[2,128,512]{2,1,0:T(8,128)(2,1)S(1)}, u32[]{:S(2)}, u32[]{:S(2)}) collective-permute-start(bf16[2,128,512]{2,1,0:T(8,128)(2,1)S(1)} %get-tuple-element.14.refs_0_), channel_id=1, source_target_pairs={{0,1},{1,0},{2,3},{3,2},{4,5},{5,4},{6,7},{7,6},{8,9},{9,8},{10,11... | collective-permute-start | bytes 786440 | tf_op jit(solution)/shard_map/ppermute | solution.py:151
  12.0 23.2 %collective-permute-start.2 = (bf16[2,128,512]{2,1,0:T(8,128)(2,1)S(1)}, bf16[2,128,512]{2,1,0:T(8,128)(2,1)S(1)}, u32[]{:S(2)}, u32[]{:S(2)}) collective-permute-start(bf16[2,128,512]{2,1,0:T(8,128)(2,1)S(1)} %collective-permute-done.1.refs_2_), channel_id=1, source_target_pairs={{0,1},{1,0},{2,3},{3,2},{4,5},{5,4},{6,7},{7,6},{8,9},{9,8},{10,11... | collective-permute-start | bytes 786440 | tf_op jit(solution)/shard_map/ppermute | solution.py:151
  20.6 14.6 %collective-permute-start.4 = (bf16[2,128,512]{2,1,0:T(8,128)(2,1)S(1)}, bf16[2,128,512]{2,1,0:T(8,128)(2,1)S(1)}, u32[]{:S(2)}, u32[]{:S(2)}) collective-permute-start(bf16[2,128,512]{2,1,0:T(8,128)(2,1)S(1)} %collective-permute-done.3.refs_4_), channel_id=1, source_target_pairs={{0,1},{1,0},{2,3},{3,2},{4,5},{5,4},{6,7},{7,6},{8,9},{9,8},{10,11... | collective-permute-start | bytes 786440 | tf_op jit(solution)/shard_map/ppermute | solution.py:151
  30.7 6.8 %collective-permute-start.6 = (bf16[2,128,512]{2,1,0:T(8,128)(2,1)S(1)}, bf16[2,128,512]{2,1,0:T(8,128)(2,1)S(1)}, u32[]{:S(2)}, u32[]{:S(2)}) collective-permute-start(bf16[2,128,512]{2,1,0:T(8,128)(2,1)S(1)} %collective-permute-done.5.refs_0_), channel_id=1, source_target_pairs={{0,1},{1,0},{2,3},{3,2},{4,5},{5,4},{6,7},{7,6},{8,9},{9,8},{10,11... | collective-permute-start | bytes 786440 | tf_op jit(solution)/shard_map/ppermute | solution.py:151
  32.0 1.6 %copy-start = (bf16[1,1,2,512,1024]{4,3,2,1,0:T(8,128)(2,1)S(1)}, bf16[1,1,2,512,1024]{4,3,2,1,0:T(8,128)(2,1)}, u32[]{:S(2)}) copy-start(bf16[1,1,2,512,1024]{4,3,2,1,0:T(8,128)(2,1)} %param.6) | copy-start | bytes 6291460
  33.6 0.7 %copy-start.2 = (f32[1,512]{1,0:T(1,128)S(1)}, f32[1,512]{1,0:T(1,128)}, u32[]{:S(2)}) copy-start(f32[1,512]{1,0:T(1,128)} %noise_ref.1) | copy-start | bytes 6148
  38.2 1.4 %collective-permute-start.7 = (f32[8,128]{1,0:T(8,128)S(1)}, f32[8,128]{1,0:T(8,128)S(1)}, u32[]{:S(2)}, u32[]{:S(2)}) collective-permute-start(f32[8,128]{1,0:T(8,128)S(1)} %get-tuple-element.18), channel_id=1, source_target_pairs={{0,1},{1,0},{2,3},{3,2},{4,5},{5,4},{6,7},{7,6},{8,9},{9,8},{10,11... | collective-permute-start | bytes 12296 | tf_op jit(solution)/shard_map/ppermute | solution.py:151
  39.6 3.6 %collective-permute-start.8 = (f32[8,128]{1,0:T(8,128)S(1)}, f32[8,128]{1,0:T(8,128)S(1)}, u32[]{:S(2)}, u32[]{:S(2)}) collective-permute-start(f32[8,128]{1,0:T(8,128)S(1)} %add.12), channel_id=1, source_target_pairs={{0,2},{2,0},{1,3},{3,1},{4,6},{6,4},{5,7},{7,5},{8,10},{10,8},{9,1... | collective-permute-start | bytes 12296 | tf_op jit(solution)/shard_map/ppermute | solution.py:151
  43.2 3.6 %collective-permute-start.9 = (f32[8,128]{1,0:T(8,128)S(1)}, f32[8,128]{1,0:T(8,128)S(1)}, u32[]{:S(2)}, u32[]{:S(2)}) collective-permute-start(f32[8,128]{1,0:T(8,128)S(1)} %add.13), channel_id=1, source_target_pairs={{0,4},{4,0},{8,12},{12,8},{1,5},{5,1},{9,13},{13,9},{2,6},{6,2},{1... | collective-permute-start | bytes 12296 | tf_op jit(solution)/shard_map/ppermute | solution.py:151
  46.8 4.5 %collective-permute-start.10 = (f32[8,128]{1,0:T(8,128)S(1)}, f32[8,128]{1,0:T(8,128)S(1)}, u32[]{:S(2)}, u32[]{:S(2)}) collective-permute-start(f32[8,128]{1,0:T(8,128)S(1)} %add.14), channel_id=1, source_target_pairs={{0,8},{4,12},{8,0},{12,4},{1,9},{5,13},{9,1},{13,5},{2,10},{6,14},... | collective-permute-start | bytes 12296 | tf_op jit(solution)/shard_map/ppermute | solution.py:151

commit v3 on v2

--- a/solution.py
+++ b/solution.py
@@ -148,7 +148,9 @@
 
 
 def swap(x, name, step):
-    return lax.ppermute(x, name, [(i, i ^ step) for i in range(lax.axis_size(name))])
+    names, flip = ("pol", step) if name == "pol" else ((name, "pol"), 2 * step + 1)
+    size = lax.axis_size(names)
+    return lax.ppermute(x, names, [(i, i ^ flip) for i in range(size)])
 
 
 def on_device(alm, beam, m_table, chan_mask, noise):
@@ -202,7 +204,7 @@
         in_specs=[HBM, VMEM],
         scratch_shapes=[pltpu.SemaphoreType.DMA((2 * blocks,))],
     )
-    steps = ((0, 0), (0, 1), (1, 0), (1, 1), (3, 0), (3, 1))
+    steps = ((0, 0), (0, 1), (1, 1), (1, 0), (3, 1), (3, 0))
     vis = call(
         functools.partial(first_kernel, steps),
         vis_shape,
@@ -211,10 +213,10 @@
         6,
     )
     vis = call(
-        functools.partial(next_kernel, ((2, 0),)), vis_shape, (m_table,), (left, vis, two), 1
+        functools.partial(next_kernel, ((2, 1),)), vis_shape, (m_table,), (left, vis, two), 1
     )
     vis, total = call(
-        functools.partial(last_kernel, ((2, 1),), n_freq),
+        functools.partial(last_kernel, ((2, 0),), n_freq),
         (vis_shape, row),
         (m_table, chan_mask),
         (left, weight, vis, two_far),

time: 52.8 us -> 51.6 us (0.977)
  starting transfers between devices: 8.97 us -> 8.19 us
    ppermute x11, starting transfers between devices: 8.97 us -> 8.19 us  [swap(): return lax.ppermute(x, names, [(i, i ^ flip) for i in range(size)])]
where the time goes in v3:
time: 51.6 us; the launch traced here: 51.4 us
  waiting for transfers between devices  32.4 us (63%)
  starting transfers between devices  8.19 us (16%)
  Pallas kernels  5.35 us (10%)
  local copies, waits for them, and re-layouts  3.49 us (7%)
  between operations  2.02 us (4%)
    ppermute x11, waiting for transfers between devices, swap(): return lax.ppermute(x, names, [(i, i ^ flip) for i in range(size)])  32.4 us
    ppermute x11, starting transfers between devices, swap(): return lax.ppermute(x, names, [(i, i ^ flip) for i in range(size)])  8.19 us
    pallas_call x6, Pallas kernels, call(): pl.pallas_call(kernel, out_shape=out_shape, in_specs=more.pop('in_specs',...  5.35 us
    unnamed x6, local copies, waits for them, and re-layouts  3.49 us
  transfers between devices with their start and end apart: 11, of which 7 were waited for; matrix products, arithmetic and copies ran while one was open for 0% of the time, Pallas kernels for 6%

profile of v3, /device:TPU:0, one launch (start us, length us, event | category | flops | bytes accessed | tf_op | source)
XLA Modules:
  0.0 51.4 jit_solution(4405497153997631892)
XLA Ops:
  0.6 1.2 %copy-done.1 = bf16[2,1,128,4,512]{4,3,2,1,0:T(4,128)(2,1)S(1)} copy-done((bf16[2,1,128,4,512]{4,3,2,1,0:T(4,128)(2,1)S(1)}, bf16[2,1,128,4,512]{4,3,2,1,0:T(4,128)(2,1)}, u32[]{:S(2)}) %copy-start.1) | copy-done | bytes 1048600
  1.9 0.3 shard_map.69
  2.2 2.6 %collective-permute-start.1 = (bf16[2,128,512]{2,1,0:T(8,128)(2,1)S(1)}, bf16[2,128,512]{2,1,0:T(8,128)(2,1)S(1)}, u32[]{:S(2)}, u32[]{:S(2)}) collective-permute-start(bf16[2,128,512]{2,1,0:T(8,128)(2,1)S(1)} %get-tuple-element.15), channel_id=1, source_target_pairs={{0,5},{1,4},{4,1},{5,0},{8,13},{9,12},{12,9},{13,8},{2,7},{3,6},{6... | collective-permute-start | bytes 786440 | tf_op jit(solution)/shard_map/ppermute | solution.py:153
  4.7 2.8 %collective-permute-start.3 = (bf16[2,128,512]{2,1,0:T(8,128)(2,1)S(1)}, bf16[2,128,512]{2,1,0:T(8,128)(2,1)S(1)}, u32[]{:S(2)}, u32[]{:S(2)}) collective-permute-start(bf16[2,128,512]{2,1,0:T(8,128)(2,1)S(1)} %get-tuple-element.16), channel_id=1, source_target_pairs={{0,13},{1,12},{4,9},{5,8},{8,5},{9,4},{12,1},{13,0},{2,15},{3,14},... | collective-permute-start | bytes 786440 | tf_op jit(solution)/shard_map/ppermute | solution.py:153
  7.5 0.1 collective-permute-start.5
  7.6 0.0 collective-permute-start
  7.6 3.8 %collective-permute-done.1.refs_2_ = bf16[2,128,512]{2,1,0:T(8,128)(2,1)S(1)} collective-permute-done((bf16[2,128,512]{2,1,0:T(8,128)(2,1)S(1)}, bf16[2,128,512]{2,1,0:T(8,128)(2,1)S(1)}, u32[]{:S(2)}, u32[]{:S(2)}) %collective-permute-start.1) | collective-permute-done | bytes 262176 | tf_op jit(solution)/shard_map/ppermute | solution.py:153
  11.4 0.1 collective-permute-start.2
  11.5 8.4 %collective-permute-done.3.refs_4_ = bf16[2,128,512]{2,1,0:T(8,128)(2,1)S(1)} collective-permute-done((bf16[2,128,512]{2,1,0:T(8,128)(2,1)S(1)}, bf16[2,128,512]{2,1,0:T(8,128)(2,1)S(1)}, u32[]{:S(2)}, u32[]{:S(2)}) %collective-permute-start.3) | collective-permute-done | bytes 262176 | tf_op jit(solution)/shard_map/ppermute | solution.py:153
  19.9 0.1 collective-permute-start.4
  20.0 11.3 %collective-permute-done.5.refs_0_ = bf16[2,128,512]{2,1,0:T(8,128)(2,1)S(1)} collective-permute-done((bf16[2,128,512]{2,1,0:T(8,128)(2,1)S(1)}, bf16[2,128,512]{2,1,0:T(8,128)(2,1)S(1)}, u32[]{:S(2)}, u32[]{:S(2)}) %collective-permute-start.5) | collective-permute-done | bytes 262176 | tf_op jit(solution)/shard_map/ppermute | solution.py:153
  31.3 0.1 collective-permute-start.6
  32.7 0.0 copy-start
  32.7 1.6 %copy-done = bf16[1,1,2,512,1024]{4,3,2,1,0:T(8,128)(2,1)S(1)} copy-done((bf16[1,1,2,512,1024]{4,3,2,1,0:T(8,128)(2,1)S(1)}, bf16[1,1,2,512,1024]{4,3,2,1,0:T(8,128)(2,1)}, u32[]{:S(2)}) %copy-start) | copy-done | bytes 2097176
  34.3 0.7 %copy-done.2 = f32[1,512]{1,0:T(1,128)S(1)} copy-done((f32[1,512]{1,0:T(1,128)S(1)}, f32[1,512]{1,0:T(1,128)}, u32[]{:S(2)}) %copy-start.2) | copy-done | bytes 2072
  35.0 0.9 %shard_map.68 = (bf16[8,512,256]{2,1,0:T(8,128)(2,1)S(1)}, f32[512,128]{1,0:T(8,128)S(1)}) custom-call(bf16[2,512,1024]{2,1,0:T(8,128)(2,1)S(1)} %bitcast.7, f32[1,512]{1,0:T(1,128)S(1)} %copy-done.2), custom_call_target="tpu_custom_call" | custom-call | bytes 2097152 | tf_op jit(solution)/shard_map/pallas_call | solution.py:168
  35.8 0.0 collective-permute-done.refs_1_
  35.8 0.0 collective-permute-done.2.refs_3_
  35.9 0.0 collective-permute-done.4.refs_5_
  35.9 1.8 %shard_map.70.before_ref = f32[2,512,512]{2,1,0:T(8,128)S(1)} custom-call(s32[1]{0:T(128)S(6)} %copy.8.m_ref, s32[1]{0:T(128)S(6)} %copy.9.mask_ref, bf16[8,512,256]{2,1,0:T(8,128)(2,1)S(1)} %get-tuple-element.12.left_ref, bf16[2,128,512]{2,1,0:T(8,128)(2,1)S(1)} %get-tuple-element.14.refs_0_, bf16[2,128,512]{2,1,0:T(8,128)(2,1)S(1)} %collective-permute-done.refs_1_, ...), custom_call_target="tpu_custom_call" | custom-call | flops 1610612736 | bytes 5242880 | tf_op jit(solution)/shard_map/pallas_call | solution.py:168
  37.7 0.5 shard_map.71.before_ref
  38.2 0.0 collective-permute-done.6.refs_0_
  38.2 0.7 %shard_map.72 = (f32[2,512,512]{2,1,0:T(8,128)S(1)}, f32[8,128]{1,0:T(8,128)S(1)}) custom-call(s32[1]{0:T(128)S(6)} %copy.8.m_ref, s32[1]{0:T(128)S(6)} %copy.9.mask_ref, bf16[8,512,256]{2,1,0:T(8,128)(2,1)S(1)} %get-tuple-element.12.left_ref, f32[512,128]{1,0:T(8,128)S(1)} %get-tuple-element.13.weight_ref, f32[2,512,512]{2,1,0:T(8,128)S(1)} %shard_map.71.before_ref, ...), custom_call_target="tpu_custom_call" | custom-call | flops 268435456 | bytes 2621440 | tf_op jit(solution)/shard_map/pallas_call | solution.py:168
  38.9 0.5 collective-permute-start.7
  39.3 0.8 %collective-permute-done.7 = f32[8,128]{1,0:T(8,128)S(1)} collective-permute-done((f32[8,128]{1,0:T(8,128)S(1)}, f32[8,128]{1,0:T(8,128)S(1)}, u32[]{:S(2)}, u32[]{:S(2)}) %collective-permute-start.7) | collective-permute-done | bytes 4128 | tf_op jit(solution)/shard_map/ppermute | solution.py:153
  40.2 1.4 %collective-permute-start.8 = (f32[8,128]{1,0:T(8,128)S(1)}, f32[8,128]{1,0:T(8,128)S(1)}, u32[]{:S(2)}, u32[]{:S(2)}) collective-permute-start(f32[8,128]{1,0:T(8,128)S(1)} %add.12), channel_id=1, source_target_pairs={{0,3},{1,2},{2,1},{3,0},{4,7},{5,6},{6,5},{7,4},{8,11},{9,10},{10,... | collective-permute-start | bytes 12296 | tf_op jit(solution)/shard_map/ppermute | solution.py:153
  41.6 1.6 %collective-permute-done.8 = f32[8,128]{1,0:T(8,128)S(1)} collective-permute-done((f32[8,128]{1,0:T(8,128)S(1)}, f32[8,128]{1,0:T(8,128)S(1)}, u32[]{:S(2)}, u32[]{:S(2)}) %collective-permute-start.8) | collective-permute-done | bytes 4128 | tf_op jit(solution)/shard_map/ppermute | solution.py:153
  43.2 0.0 collective-permute-start.9
  43.2 3.0 %collective-permute-done.9 = f32[8,128]{1,0:T(8,128)S(1)} collective-permute-done((f32[8,128]{1,0:T(8,128)S(1)}, f32[8,128]{1,0:T(8,128)S(1)}, u32[]{:S(2)}, u32[]{:S(2)}) %collective-permute-start.9) | collective-permute-done | bytes 4128 | tf_op jit(solution)/shard_map/ppermute | solution.py:153
  46.2 0.6 %collective-permute-start.10 = (f32[8,128]{1,0:T(8,128)S(1)}, f32[8,128]{1,0:T(8,128)S(1)}, u32[]{:S(2)}, u32[]{:S(2)}) collective-permute-start(f32[8,128]{1,0:T(8,128)S(1)} %add.14), channel_id=1, source_target_pairs={{0,9},{1,8},{4,13},{5,12},{8,1},{9,0},{12,5},{13,4},{2,11},{3,10},... | collective-permute-start | bytes 12296 | tf_op jit(solution)/shard_map/ppermute | solution.py:153
  46.8 3.4 %collective-permute-done.10 = f32[8,128]{1,0:T(8,128)S(1)} collective-permute-done((f32[8,128]{1,0:T(8,128)S(1)}, f32[8,128]{1,0:T(8,128)S(1)}, u32[]{:S(2)}, u32[]{:S(2)}) %collective-permute-start.10) | collective-permute-done | bytes 4128 | tf_op jit(solution)/shard_map/ppermute | solution.py:153
  50.2 1.2 %shard_map.73 = (bf16[2,512,512]{2,1,0:T(8,128)(2,1)}, f32[1,128]{1,0:T(1,128)}) custom-call(s32[1]{0:T(128)S(6)} %copy.9.mask_ref, f32[8,128]{1,0:T(8,128)S(1)} %add.15.total_ref, f32[2,512,512]{2,1,0:T(8,128)S(1)} %get-tuple-element.19.vis_ref), custom_call_target="tpu_custom_call" | custom-call | bytes 2097152 | tf_op jit(solution)/shard_map/pallas_call | solution.py:168
  (6 shorter events, 0.0 us)
Async XLA Ops:
  0.6 1.2 %copy-start.1 = (bf16[2,1,128,4,512]{4,3,2,1,0:T(4,128)(2,1)S(1)}, bf16[2,1,128,4,512]{4,3,2,1,0:T(4,128)(2,1)}, u32[]{:S(2)}) copy-start(bf16[2,1,128,4,512]{4,3,2,1,0:T(4,128)(2,1)} %param.5) | copy-start | bytes 3145732
  2.2 9.3 %collective-permute-start.1 = (bf16[2,128,512]{2,1,0:T(8,128)(2,1)S(1)}, bf16[2,128,512]{2,1,0:T(8,128)(2,1)S(1)}, u32[]{:S(2)}, u32[]{:S(2)}) collective-permute-start(bf16[2,128,512]{2,1,0:T(8,128)(2,1)S(1)} %get-tuple-element.15), channel_id=1, source_target_pairs={{0,5},{1,4},{4,1},{5,0},{8,13},{9,12},{12,9},{13,8},{2,7},{3,6},{6... | collective-permute-start | bytes 786440 | tf_op jit(solution)/shard_map/ppermute | solution.py:153
  4.7 15.2 %collective-permute-start.3 = (bf16[2,128,512]{2,1,0:T(8,128)(2,1)S(1)}, bf16[2,128,512]{2,1,0:T(8,128)(2,1)S(1)}, u32[]{:S(2)}, u32[]{:S(2)}) collective-permute-start(bf16[2,128,512]{2,1,0:T(8,128)(2,1)S(1)} %get-tuple-element.16), channel_id=1, source_target_pairs={{0,13},{1,12},{4,9},{5,8},{8,5},{9,4},{12,1},{13,0},{2,15},{3,14},... | collective-permute-start | bytes 786440 | tf_op jit(solution)/shard_map/ppermute | solution.py:153
  7.5 23.8 %collective-permute-start.5 = (bf16[2,128,512]{2,1,0:T(8,128)(2,1)S(1)}, bf16[2,128,512]{2,1,0:T(8,128)(2,1)S(1)}, u32[]{:S(2)}, u32[]{:S(2)}) collective-permute-start(bf16[2,128,512]{2,1,0:T(8,128)(2,1)S(1)} %get-tuple-element.17), channel_id=1, source_target_pairs={{0,9},{1,8},{4,13},{5,12},{8,1},{9,0},{12,5},{13,4},{2,11},{3,10},... | collective-permute-start | bytes 786440 | tf_op jit(solution)/shard_map/ppermute | solution.py:153
  7.6 28.3 %collective-permute-start = (bf16[2,128,512]{2,1,0:T(8,128)(2,1)S(1)}, bf16[2,128,512]{2,1,0:T(8,128)(2,1)S(1)}, u32[]{:S(2)}, u32[]{:S(2)}) collective-permute-start(bf16[2,128,512]{2,1,0:T(8,128)(2,1)S(1)} %get-tuple-element.14.refs_0_), channel_id=1, source_target_pairs={{0,1},{1,0},{2,3},{3,2},{4,5},{5,4},{6,7},{7,6},{8,9},{9,8},{10,11... | collective-permute-start | bytes 786440 | tf_op jit(solution)/shard_map/ppermute | solution.py:153
  11.4 24.4 %collective-permute-start.2 = (bf16[2,128,512]{2,1,0:T(8,128)(2,1)S(1)}, bf16[2,128,512]{2,1,0:T(8,128)(2,1)S(1)}, u32[]{:S(2)}, u32[]{:S(2)}) collective-permute-start(bf16[2,128,512]{2,1,0:T(8,128)(2,1)S(1)} %collective-permute-done.1.refs_2_), channel_id=1, source_target_pairs={{0,1},{1,0},{2,3},{3,2},{4,5},{5,4},{6,7},{7,6},{8,9},{9,8},{10,11... | collective-permute-start | bytes 786440 | tf_op jit(solution)/shard_map/ppermute | solution.py:153
  19.9 15.9 %collective-permute-start.4 = (bf16[2,128,512]{2,1,0:T(8,128)(2,1)S(1)}, bf16[2,128,512]{2,1,0:T(8,128)(2,1)S(1)}, u32[]{:S(2)}, u32[]{:S(2)}) collective-permute-start(bf16[2,128,512]{2,1,0:T(8,128)(2,1)S(1)} %collective-permute-done.3.refs_4_), channel_id=1, source_target_pairs={{0,1},{1,0},{2,3},{3,2},{4,5},{5,4},{6,7},{7,6},{8,9},{9,8},{10,11... | collective-permute-start | bytes 786440 | tf_op jit(solution)/shard_map/ppermute | solution.py:153
  31.3 6.9 %collective-permute-start.6 = (bf16[2,128,512]{2,1,0:T(8,128)(2,1)S(1)}, bf16[2,128,512]{2,1,0:T(8,128)(2,1)S(1)}, u32[]{:S(2)}, u32[]{:S(2)}) collective-permute-start(bf16[2,128,512]{2,1,0:T(8,128)(2,1)S(1)} %collective-permute-done.5.refs_0_), channel_id=1, source_target_pairs={{0,1},{1,0},{2,3},{3,2},{4,5},{5,4},{6,7},{7,6},{8,9},{9,8},{10,11... | collective-permute-start | bytes 786440 | tf_op jit(solution)/shard_map/ppermute | solution.py:153
  32.7 1.6 %copy-start = (bf16[1,1,2,512,1024]{4,3,2,1,0:T(8,128)(2,1)S(1)}, bf16[1,1,2,512,1024]{4,3,2,1,0:T(8,128)(2,1)}, u32[]{:S(2)}) copy-start(bf16[1,1,2,512,1024]{4,3,2,1,0:T(8,128)(2,1)} %param.6) | copy-start | bytes 6291460
  34.3 0.7 %copy-start.2 = (f32[1,512]{1,0:T(1,128)S(1)}, f32[1,512]{1,0:T(1,128)}, u32[]{:S(2)}) copy-start(f32[1,512]{1,0:T(1,128)} %noise_ref.1) | copy-start | bytes 6148
  38.9 1.3 %collective-permute-start.7 = (f32[8,128]{1,0:T(8,128)S(1)}, f32[8,128]{1,0:T(8,128)S(1)}, u32[]{:S(2)}, u32[]{:S(2)}) collective-permute-start(f32[8,128]{1,0:T(8,128)S(1)} %get-tuple-element.18), channel_id=1, source_target_pairs={{0,1},{1,0},{2,3},{3,2},{4,5},{5,4},{6,7},{7,6},{8,9},{9,8},{10,11... | collective-permute-start | bytes 12296 | tf_op jit(solution)/shard_map/ppermute | solution.py:153
  40.2 3.0 %collective-permute-start.8 = (f32[8,128]{1,0:T(8,128)S(1)}, f32[8,128]{1,0:T(8,128)S(1)}, u32[]{:S(2)}, u32[]{:S(2)}) collective-permute-start(f32[8,128]{1,0:T(8,128)S(1)} %add.12), channel_id=1, source_target_pairs={{0,3},{1,2},{2,1},{3,0},{4,7},{5,6},{6,5},{7,4},{8,11},{9,10},{10,... | collective-permute-start | bytes 12296 | tf_op jit(solution)/shard_map/ppermute | solution.py:153
  43.2 3.0 %collective-permute-start.9 = (f32[8,128]{1,0:T(8,128)S(1)}, f32[8,128]{1,0:T(8,128)S(1)}, u32[]{:S(2)}, u32[]{:S(2)}) collective-permute-start(f32[8,128]{1,0:T(8,128)S(1)} %add.13), channel_id=1, source_target_pairs={{0,5},{1,4},{4,1},{5,0},{8,13},{9,12},{12,9},{13,8},{2,7},{3,6},{6... | collective-permute-start | bytes 12296 | tf_op jit(solution)/shard_map/ppermute | solution.py:153
  46.2 3.9 %collective-permute-start.10 = (f32[8,128]{1,0:T(8,128)S(1)}, f32[8,128]{1,0:T(8,128)S(1)}, u32[]{:S(2)}, u32[]{:S(2)}) collective-permute-start(f32[8,128]{1,0:T(8,128)S(1)} %add.14), channel_id=1, source_target_pairs={{0,9},{1,8},{4,13},{5,12},{8,1},{9,0},{12,5},{13,4},{2,11},{3,10},... | collective-permute-start | bytes 12296 | tf_op jit(solution)/shard_map/ppermute | solution.py:153

commit v4 on v3

--- a/solution.py
+++ b/solution.py
@@ -147,6 +147,11 @@
         copy.wait()
 
 
+def straight(x, name, step):
+    size = lax.axis_size(name)
+    return lax.ppermute(x, name, [(i, i ^ step) for i in range(size)])
+
+
 def swap(x, name, step):
     names, flip = ("pol", step) if name == "pol" else ((name, "pol"), 2 * step + 1)
     size = lax.axis_size(names)
@@ -187,9 +192,9 @@
         0,
         scratch_shapes=[pltpu.VMEM((n_ma, ell, maps), alm.dtype)],
     )
-    three = swap(three, "ma", 3)
-    one = swap(one, "ma", 1)
-    two = swap(two, "ma", 2)
+    three = straight(three, "ma", 3)
+    one = straight(one, "ma", 1)
+    two = straight(two, "ma", 2)
     own_far = swap(own, "pol", 1)
     one_far = swap(one, "pol", 1)
     three_far = swap(three, "pol", 1)
@@ -204,29 +209,26 @@
         in_specs=[HBM, VMEM],
         scratch_shapes=[pltpu.SemaphoreType.DMA((2 * blocks,))],
     )
-    steps = ((0, 0), (0, 1), (1, 1), (1, 0), (3, 1), (3, 0))
+    steps = ((0, 0), (0, 1), (1, 0), (1, 1), (2, 0), (2, 1))
     vis = call(
         functools.partial(first_kernel, steps),
         vis_shape,
         (m_table, chan_mask),
-        (left, own, own_far, one, one_far, three, three_far),
+        (left, own, own_far, one, one_far, two, two_far),
         6,
     )
     vis = call(
-        functools.partial(next_kernel, ((2, 1),)), vis_shape, (m_table,), (left, vis, two), 1
+        functools.partial(next_kernel, ((3, 0),)), vis_shape, (m_table,), (left, vis, three), 1
     )
     vis, total = call(
-        functools.partial(last_kernel, ((2, 0),), n_freq),
+        functools.partial(last_kernel, ((3, 1),), n_freq),
         (vis_shape, row),
         (m_table, chan_mask),
-        (left, weight, vis, two_far),
+        (left, weight, vis, three_far),
         1,
     )
-    for name in ("pol", "freq", "ma"):
-        step = 1
-        while step < lax.axis_size(name):
-            total = total + swap(total, name, step)
-            step *= 2
+    for name, step in (('pol', 1), ('freq', 1), ('ma', 3), ('ma', 1)):
+        total = total + swap(total, name, step)
     scaled, own_power = call(
         functools.partial(finish_kernel, n_freq, n_ma * n_pol * modes * maps),
         (

time: 51.6 us -> 49.1 us (0.952)
  waiting for transfers between devices: 32.4 us -> 25.6 us
  starting transfers between devices: 8.19 us -> 12.4 us
    ppermute x11 -> x8, waiting for transfers between devices: 32.4 us -> 6.85 us  [swap(): return lax.ppermute(x, names, [(i, i ^ flip) for i in range(size)])]
    ppermute x0 -> x3, waiting for transfers between devices: none -> 18.7 us  [straight(): return lax.ppermute(x, name, [(i, i ^ step) for i in range(size)])]
    ppermute x0 -> x3, starting transfers between devices: none -> 5.71 us  [straight(): return lax.ppermute(x, name, [(i, i ^ step) for i in range(size)])]
    ppermute x11 -> x8, starting transfers between devices: 8.19 us -> 6.71 us  [swap(): return lax.ppermute(x, names, [(i, i ^ flip) for i in range(size)])]
  transfers between devices with their start and end apart: 11 -> 11, of which waited for: 7 -> 6; matrix products, arithmetic and copies ran while one was open for 0% -> 0% of each run, Pallas kernels for 6% -> 6%
where the time goes in v4:
time: 49.1 us; the launch traced here: 48.9 us
  waiting for transfers between devices  25.6 us (52%)
  starting transfers between devices  12.4 us (25%)
  Pallas kernels  5.34 us (11%)
  local copies, waits for them, and re-layouts  3.49 us (7%)
  between operations  2.02 us (4%)
    ppermute x3, waiting for transfers between devices, straight(): return lax.ppermute(x, name, [(i, i ^ step) for i in range(size)])  18.7 us
    ppermute x8, waiting for transfers between devices, swap(): return lax.ppermute(x, names, [(i, i ^ flip) for i in range(size)])  6.85 us
    ppermute x8, starting transfers between devices, swap(): return lax.ppermute(x, names, [(i, i ^ flip) for i in range(size)])  6.71 us
    ppermute x3, starting transfers between devices, straight(): return lax.ppermute(x, name, [(i, i ^ step) for i in range(size)])  5.71 us
    pallas_call x6, Pallas kernels, call(): pl.pallas_call(kernel, out_shape=out_shape, in_specs=more.pop('in_specs',...  5.34 us
    unnamed x6, local copies, waits for them, and re-layouts  3.49 us
  transfers between devices with their start and end apart: 11, of which 6 were waited for; matrix products, arithmetic and copies ran while one was open for 0% of the time, Pallas kernels for 6%

profile of v4, /device:TPU:0, one launch (start us, length us, event | category | flops | bytes accessed | tf_op | source)
XLA Modules:
  0.0 48.9 jit_solution(643454850363537028)
XLA Ops:
  0.6 1.2 %copy-done.1 = bf16[2,1,128,4,512]{4,3,2,1,0:T(4,128)(2,1)S(1)} copy-done((bf16[2,1,128,4,512]{4,3,2,1,0:T(4,128)(2,1)S(1)}, bf16[2,1,128,4,512]{4,3,2,1,0:T(4,128)(2,1)}, u32[]{:S(2)}) %copy-start.1) | copy-done | bytes 1048600
  1.9 0.3 shard_map.69
  2.2 3.1 %collective-permute-start.1 = (bf16[2,128,512]{2,1,0:T(8,128)(2,1)S(1)}, bf16[2,128,512]{2,1,0:T(8,128)(2,1)S(1)}, u32[]{:S(2)}, u32[]{:S(2)}) collective-permute-start(bf16[2,128,512]{2,1,0:T(8,128)(2,1)S(1)} %get-tuple-element.15), channel_id=1, source_target_pairs={{0,4},{4,0},{8,12},{12,8},{1,5},{5,1},{9,13},{13,9},{2,6},{6,2},{1... | collective-permute-start | bytes 786440 | tf_op jit(solution)/shard_map/ppermute | solution.py:152
  5.3 2.6 %collective-permute-start.3 = (bf16[2,128,512]{2,1,0:T(8,128)(2,1)S(1)}, bf16[2,128,512]{2,1,0:T(8,128)(2,1)S(1)}, u32[]{:S(2)}, u32[]{:S(2)}) collective-permute-start(bf16[2,128,512]{2,1,0:T(8,128)(2,1)S(1)} %get-tuple-element.16), channel_id=1, source_target_pairs={{0,8},{4,12},{8,0},{12,4},{1,9},{5,13},{9,1},{13,5},{2,10},{6,14},... | collective-permute-start | bytes 786440 | tf_op jit(solution)/shard_map/ppermute | solution.py:152
  7.9 0.0 collective-permute-start.5
  7.9 0.0 collective-permute-start
  7.9 8.6 %collective-permute-done.1.refs_2_ = bf16[2,128,512]{2,1,0:T(8,128)(2,1)S(1)} collective-permute-done((bf16[2,128,512]{2,1,0:T(8,128)(2,1)S(1)}, bf16[2,128,512]{2,1,0:T(8,128)(2,1)S(1)}, u32[]{:S(2)}, u32[]{:S(2)}) %collective-permute-start.1) | collective-permute-done | bytes 262176 | tf_op jit(solution)/shard_map/ppermute | solution.py:152
  16.5 0.0 collective-permute-start.2
  16.5 10.1 %collective-permute-done.3.refs_4_ = bf16[2,128,512]{2,1,0:T(8,128)(2,1)S(1)} collective-permute-done((bf16[2,128,512]{2,1,0:T(8,128)(2,1)S(1)}, bf16[2,128,512]{2,1,0:T(8,128)(2,1)S(1)}, u32[]{:S(2)}, u32[]{:S(2)}) %collective-permute-start.3) | collective-permute-done | bytes 262176 | tf_op jit(solution)/shard_map/ppermute | solution.py:152
  26.6 0.0 collective-permute-start.4
  26.6 0.0 collective-permute-done.5.refs_0_
  26.6 0.5 %collective-permute-start.6 = (bf16[2,128,512]{2,1,0:T(8,128)(2,1)S(1)}, bf16[2,128,512]{2,1,0:T(8,128)(2,1)S(1)}, u32[]{:S(2)}, u32[]{:S(2)}) collective-permute-start(bf16[2,128,512]{2,1,0:T(8,128)(2,1)S(1)} %collective-permute-done.5.refs_0_), channel_id=1, source_target_pairs={{0,1},{1,0},{2,3},{3,2},{4,5},{5,4},{6,7},{7,6},{8,9},{9,8},{10,11... | collective-permute-start | bytes 786440 | tf_op jit(solution)/shard_map/ppermute | solution.py:158
  28.4 0.0 copy-start
  28.4 1.6 %copy-done = bf16[1,1,2,512,1024]{4,3,2,1,0:T(8,128)(2,1)S(1)} copy-done((bf16[1,1,2,512,1024]{4,3,2,1,0:T(8,128)(2,1)S(1)}, bf16[1,1,2,512,1024]{4,3,2,1,0:T(8,128)(2,1)}, u32[]{:S(2)}) %copy-start) | copy-done | bytes 2097176
  30.0 0.7 %copy-done.2 = f32[1,512]{1,0:T(1,128)S(1)} copy-done((f32[1,512]{1,0:T(1,128)S(1)}, f32[1,512]{1,0:T(1,128)}, u32[]{:S(2)}) %copy-start.2) | copy-done | bytes 2072
  30.7 0.9 %shard_map.68 = (bf16[8,512,256]{2,1,0:T(8,128)(2,1)S(1)}, f32[512,128]{1,0:T(8,128)S(1)}) custom-call(bf16[2,512,1024]{2,1,0:T(8,128)(2,1)S(1)} %bitcast.7, f32[1,512]{1,0:T(1,128)S(1)} %copy-done.2), custom_call_target="tpu_custom_call" | custom-call | bytes 2097152 | tf_op jit(solution)/shard_map/pallas_call | solution.py:173
  31.5 0.0 collective-permute-done.refs_1_
  31.5 0.0 collective-permute-done.2.refs_3_
  31.6 0.0 collective-permute-done.4.refs_5_
  31.6 1.8 %shard_map.70.before_ref = f32[2,512,512]{2,1,0:T(8,128)S(1)} custom-call(s32[1]{0:T(128)S(6)} %copy.8.m_ref, s32[1]{0:T(128)S(6)} %copy.9.mask_ref, bf16[8,512,256]{2,1,0:T(8,128)(2,1)S(1)} %get-tuple-element.12.left_ref, bf16[2,128,512]{2,1,0:T(8,128)(2,1)S(1)} %get-tuple-element.14.refs_0_, bf16[2,128,512]{2,1,0:T(8,128)(2,1)S(1)} %collective-permute-done.refs_1_, ...), custom_call_target="tpu_custom_call" | custom-call | flops 1610612736 | bytes 5242880 | tf_op jit(solution)/shard_map/pallas_call | solution.py:173
  33.4 0.5 shard_map.71.before_ref
  33.9 0.0 collective-permute-done.6.refs_0_
  33.9 0.7 %shard_map.72 = (f32[2,512,512]{2,1,0:T(8,128)S(1)}, f32[8,128]{1,0:T(8,128)S(1)}) custom-call(s32[1]{0:T(128)S(6)} %copy.8.m_ref, s32[1]{0:T(128)S(6)} %copy.9.mask_ref, bf16[8,512,256]{2,1,0:T(8,128)(2,1)S(1)} %get-tuple-element.12.left_ref, f32[512,128]{1,0:T(8,128)S(1)} %get-tuple-element.13.weight_ref, f32[2,512,512]{2,1,0:T(8,128)S(1)} %shard_map.71.before_ref, ...), custom_call_target="tpu_custom_call" | custom-call | flops 268435456 | bytes 2621440 | tf_op jit(solution)/shard_map/pallas_call | solution.py:173
  34.6 0.1 collective-permute-start.7
  34.6 1.2 %collective-permute-done.7 = f32[8,128]{1,0:T(8,128)S(1)} collective-permute-done((f32[8,128]{1,0:T(8,128)S(1)}, f32[8,128]{1,0:T(8,128)S(1)}, u32[]{:S(2)}, u32[]{:S(2)}) %collective-permute-start.7) | collective-permute-done | bytes 4128 | tf_op jit(solution)/shard_map/ppermute | solution.py:158
  35.8 1.3 %collective-permute-start.8 = (f32[8,128]{1,0:T(8,128)S(1)}, f32[8,128]{1,0:T(8,128)S(1)}, u32[]{:S(2)}, u32[]{:S(2)}) collective-permute-start(f32[8,128]{1,0:T(8,128)S(1)} %add.12), channel_id=1, source_target_pairs={{0,3},{1,2},{2,1},{3,0},{4,7},{5,6},{6,5},{7,4},{8,11},{9,10},{10,... | collective-permute-start | bytes 12296 | tf_op jit(solution)/shard_map/ppermute | solution.py:158
  37.1 1.8 %collective-permute-done.8 = f32[8,128]{1,0:T(8,128)S(1)} collective-permute-done((f32[8,128]{1,0:T(8,128)S(1)}, f32[8,128]{1,0:T(8,128)S(1)}, u32[]{:S(2)}, u32[]{:S(2)}) %collective-permute-start.8) | collective-permute-done | bytes 4128 | tf_op jit(solution)/shard_map/ppermute | solution.py:158
  38.8 2.2 %collective-permute-start.9 = (f32[8,128]{1,0:T(8,128)S(1)}, f32[8,128]{1,0:T(8,128)S(1)}, u32[]{:S(2)}, u32[]{:S(2)}) collective-permute-start(f32[8,128]{1,0:T(8,128)S(1)} %add.13), channel_id=1, source_target_pairs={{0,13},{1,12},{4,9},{5,8},{8,5},{9,4},{12,1},{13,0},{2,15},{3,14},... | collective-permute-start | bytes 12296 | tf_op jit(solution)/shard_map/ppermute | solution.py:158
  41.1 2.6 %collective-permute-done.9 = f32[8,128]{1,0:T(8,128)S(1)} collective-permute-done((f32[8,128]{1,0:T(8,128)S(1)}, f32[8,128]{1,0:T(8,128)S(1)}, u32[]{:S(2)}, u32[]{:S(2)}) %collective-permute-start.9) | collective-permute-done | bytes 4128 | tf_op jit(solution)/shard_map/ppermute | solution.py:158
  43.7 2.6 %collective-permute-start.10 = (f32[8,128]{1,0:T(8,128)S(1)}, f32[8,128]{1,0:T(8,128)S(1)}, u32[]{:S(2)}, u32[]{:S(2)}) collective-permute-start(f32[8,128]{1,0:T(8,128)S(1)} %add.14), channel_id=1, source_target_pairs={{0,5},{1,4},{4,1},{5,0},{8,13},{9,12},{12,9},{13,8},{2,7},{3,6},{6... | collective-permute-start | bytes 12296 | tf_op jit(solution)/shard_map/ppermute | solution.py:158
  46.3 1.3 %collective-permute-done.10 = f32[8,128]{1,0:T(8,128)S(1)} collective-permute-done((f32[8,128]{1,0:T(8,128)S(1)}, f32[8,128]{1,0:T(8,128)S(1)}, u32[]{:S(2)}, u32[]{:S(2)}) %collective-permute-start.10) | collective-permute-done | bytes 4128 | tf_op jit(solution)/shard_map/ppermute | solution.py:158
  47.6 1.2 %shard_map.73 = (bf16[2,512,512]{2,1,0:T(8,128)(2,1)}, f32[1,128]{1,0:T(1,128)}) custom-call(s32[1]{0:T(128)S(6)} %copy.9.mask_ref, f32[8,128]{1,0:T(8,128)S(1)} %add.15.total_ref, f32[2,512,512]{2,1,0:T(8,128)S(1)} %get-tuple-element.19.vis_ref), custom_call_target="tpu_custom_call" | custom-call | bytes 2097152 | tf_op jit(solution)/shard_map/pallas_call | solution.py:173
  (6 shorter events, 0.0 us)
Async XLA Ops:
  0.6 1.2 %copy-start.1 = (bf16[2,1,128,4,512]{4,3,2,1,0:T(4,128)(2,1)S(1)}, bf16[2,1,128,4,512]{4,3,2,1,0:T(4,128)(2,1)}, u32[]{:S(2)}) copy-start(bf16[2,1,128,4,512]{4,3,2,1,0:T(4,128)(2,1)} %param.5) | copy-start | bytes 3145732
  2.2 14.3 %collective-permute-start.1 = (bf16[2,128,512]{2,1,0:T(8,128)(2,1)S(1)}, bf16[2,128,512]{2,1,0:T(8,128)(2,1)S(1)}, u32[]{:S(2)}, u32[]{:S(2)}) collective-permute-start(bf16[2,128,512]{2,1,0:T(8,128)(2,1)S(1)} %get-tuple-element.15), channel_id=1, source_target_pairs={{0,4},{4,0},{8,12},{12,8},{1,5},{5,1},{9,13},{13,9},{2,6},{6,2},{1... | collective-permute-start | bytes 786440 | tf_op jit(solution)/shard_map/ppermute | solution.py:152
  5.3 21.3 %collective-permute-start.3 = (bf16[2,128,512]{2,1,0:T(8,128)(2,1)S(1)}, bf16[2,128,512]{2,1,0:T(8,128)(2,1)S(1)}, u32[]{:S(2)}, u32[]{:S(2)}) collective-permute-start(bf16[2,128,512]{2,1,0:T(8,128)(2,1)S(1)} %get-tuple-element.16), channel_id=1, source_target_pairs={{0,8},{4,12},{8,0},{12,4},{1,9},{5,13},{9,1},{13,5},{2,10},{6,14},... | collective-permute-start | bytes 786440 | tf_op jit(solution)/shard_map/ppermute | solution.py:152
  7.9 18.7 %collective-permute-start.5 = (bf16[2,128,512]{2,1,0:T(8,128)(2,1)S(1)}, bf16[2,128,512]{2,1,0:T(8,128)(2,1)S(1)}, u32[]{:S(2)}, u32[]{:S(2)}) collective-permute-start(bf16[2,128,512]{2,1,0:T(8,128)(2,1)S(1)} %get-tuple-element.17), channel_id=1, source_target_pairs={{0,12},{4,8},{8,4},{12,0},{1,13},{5,9},{9,5},{13,1},{2,14},{6,10},... | collective-permute-start | bytes 786440 | tf_op jit(solution)/shard_map/ppermute | solution.py:152
  7.9 23.7 %collective-permute-start = (bf16[2,128,512]{2,1,0:T(8,128)(2,1)S(1)}, bf16[2,128,512]{2,1,0:T(8,128)(2,1)S(1)}, u32[]{:S(2)}, u32[]{:S(2)}) collective-permute-start(bf16[2,128,512]{2,1,0:T(8,128)(2,1)S(1)} %get-tuple-element.14.refs_0_), channel_id=1, source_target_pairs={{0,1},{1,0},{2,3},{3,2},{4,5},{5,4},{6,7},{7,6},{8,9},{9,8},{10,11... | collective-permute-start | bytes 786440 | tf_op jit(solution)/shard_map/ppermute | solution.py:158
  16.5 15.1 %collective-permute-start.2 = (bf16[2,128,512]{2,1,0:T(8,128)(2,1)S(1)}, bf16[2,128,512]{2,1,0:T(8,128)(2,1)S(1)}, u32[]{:S(2)}, u32[]{:S(2)}) collective-permute-start(bf16[2,128,512]{2,1,0:T(8,128)(2,1)S(1)} %collective-permute-done.1.refs_2_), channel_id=1, source_target_pairs={{0,1},{1,0},{2,3},{3,2},{4,5},{5,4},{6,7},{7,6},{8,9},{9,8},{10,11... | collective-permute-start | bytes 786440 | tf_op jit(solution)/shard_map/ppermute | solution.py:158
  26.6 5.0 %collective-permute-start.4 = (bf16[2,128,512]{2,1,0:T(8,128)(2,1)S(1)}, bf16[2,128,512]{2,1,0:T(8,128)(2,1)S(1)}, u32[]{:S(2)}, u32[]{:S(2)}) collective-permute-start(bf16[2,128,512]{2,1,0:T(8,128)(2,1)S(1)} %collective-permute-done.3.refs_4_), channel_id=1, source_target_pairs={{0,1},{1,0},{2,3},{3,2},{4,5},{5,4},{6,7},{7,6},{8,9},{9,8},{10,11... | collective-permute-start | bytes 786440 | tf_op jit(solution)/shard_map/ppermute | solution.py:158
  26.6 7.3 %collective-permute-start.6 = (bf16[2,128,512]{2,1,0:T(8,128)(2,1)S(1)}, bf16[2,128,512]{2,1,0:T(8,128)(2,1)S(1)}, u32[]{:S(2)}, u32[]{:S(2)}) collective-permute-start(bf16[2,128,512]{2,1,0:T(8,128)(2,1)S(1)} %collective-permute-done.5.refs_0_), channel_id=1, source_target_pairs={{0,1},{1,0},{2,3},{3,2},{4,5},{5,4},{6,7},{7,6},{8,9},{9,8},{10,11... | collective-permute-start | bytes 786440 | tf_op jit(solution)/shard_map/ppermute | solution.py:158
  28.4 1.6 %copy-start = (bf16[1,1,2,512,1024]{4,3,2,1,0:T(8,128)(2,1)S(1)}, bf16[1,1,2,512,1024]{4,3,2,1,0:T(8,128)(2,1)}, u32[]{:S(2)}) copy-start(bf16[1,1,2,512,1024]{4,3,2,1,0:T(8,128)(2,1)} %param.6) | copy-start | bytes 6291460
  30.0 0.7 %copy-start.2 = (f32[1,512]{1,0:T(1,128)S(1)}, f32[1,512]{1,0:T(1,128)}, u32[]{:S(2)}) copy-start(f32[1,512]{1,0:T(1,128)} %noise_ref.1) | copy-start | bytes 6148
  34.6 1.2 %collective-permute-start.7 = (f32[8,128]{1,0:T(8,128)S(1)}, f32[8,128]{1,0:T(8,128)S(1)}, u32[]{:S(2)}, u32[]{:S(2)}) collective-permute-start(f32[8,128]{1,0:T(8,128)S(1)} %get-tuple-element.18), channel_id=1, source_target_pairs={{0,1},{1,0},{2,3},{3,2},{4,5},{5,4},{6,7},{7,6},{8,9},{9,8},{10,11... | collective-permute-start | bytes 12296 | tf_op jit(solution)/shard_map/ppermute | solution.py:158
  35.8 3.0 %collective-permute-start.8 = (f32[8,128]{1,0:T(8,128)S(1)}, f32[8,128]{1,0:T(8,128)S(1)}, u32[]{:S(2)}, u32[]{:S(2)}) collective-permute-start(f32[8,128]{1,0:T(8,128)S(1)} %add.12), channel_id=1, source_target_pairs={{0,3},{1,2},{2,1},{3,0},{4,7},{5,6},{6,5},{7,4},{8,11},{9,10},{10,... | collective-permute-start | bytes 12296 | tf_op jit(solution)/shard_map/ppermute | solution.py:158
  38.8 4.8 %collective-permute-start.9 = (f32[8,128]{1,0:T(8,128)S(1)}, f32[8,128]{1,0:T(8,128)S(1)}, u32[]{:S(2)}, u32[]{:S(2)}) collective-permute-start(f32[8,128]{1,0:T(8,128)S(1)} %add.13), channel_id=1, source_target_pairs={{0,13},{1,12},{4,9},{5,8},{8,5},{9,4},{12,1},{13,0},{2,15},{3,14},... | collective-permute-start | bytes 12296 | tf_op jit(solution)/shard_map/ppermute | solution.py:158
  43.7 3.9 %collective-permute-start.10 = (f32[8,128]{1,0:T(8,128)S(1)}, f32[8,128]{1,0:T(8,128)S(1)}, u32[]{:S(2)}, u32[]{:S(2)}) collective-permute-start(f32[8,128]{1,0:T(8,128)S(1)} %add.14), channel_id=1, source_target_pairs={{0,5},{1,4},{4,1},{5,0},{8,13},{9,12},{12,9},{13,8},{2,7},{3,6},{6... | collective-permute-start | bytes 12296 | tf_op jit(solution)/shard_map/ppermute | solution.py:158

commit v5 on v4

--- a/solution.py
+++ b/solution.py
@@ -16,19 +16,38 @@
     return jnp.transpose(jnp.broadcast_to(row, (128, row.shape[1])))
 
 
-def split_kernel(steps, alm_ref, *refs):
-    *slab_refs, modes_ref = refs
-    place = lax.axis_index("ma")
-    for c in range(alm_ref.shape[0]):
-        modes_ref[...] = pltpu.einshape("lms->mls", alm_ref[c])
-        for ref, step in zip(slab_refs, steps, strict=True):
-            ref[c] = modes_ref[place ^ step]
-
-
-def load_kernel(beam_ref, noise_ref, left_ref, weight_ref, sems):
-    _, _, total = beam_ref.shape
+def maps_of(pol, count):
+    return pl.ds(pl.multiple_of(pol * count, count), count)
+
+
+def split_kernel(pieces, alm_ref, *refs):
+    *slab_refs, held_ref, modes_ref, sems = refs
+    place, pol = lax.axis_index("ma"), lax.axis_index("pol")
+    parts, ell = alm_ref.shape[:2]
+    chunks = 2
+    size = ell // chunks
+    copies = {}
+    for c in range(parts):
+        for j in range(chunks):
+            rows = pl.ds(j * size, size)
+            copies[c, j] = pltpu.make_async_copy(
+                alm_ref.at[c, rows], held_ref.at[c, rows], sems.at[c * chunks + j]
+            )
+            copies[c, j].start()
+    for (c, j), copy in copies.items():
+        copy.wait()
+        rows = slice(j * size, (j + 1) * size)
+        modes_ref[...] = pltpu.einshape("lms->mls", held_ref[c, rows])
+        for ref, (step, other) in zip(slab_refs, pieces, strict=True):
+            if other is None:
+                ref[c, rows] = modes_ref[place ^ step]
+            else:
+                ref[c, rows] = modes_ref[place ^ step, :, maps_of(pol ^ other, ref.shape[2])]
+
+
+def load_kernel(step, beam_ref, noise_ref, left_ref, share_ref, weight_ref, sems):
     blocks = left_ref.shape[0]
-    ell = total // blocks
+    ell = beam_ref.shape[2] // blocks
     copies = []
     for block in range(blocks):
         for c in range(2):
@@ -43,34 +62,48 @@
     weight_ref[...] = column(lax.rsqrt(noise_ref[...]))
     for copy in copies:
         copy.wait()
-
-
-def contract(m_ref, left_ref, block_refs, steps):
+    for half in range(share_ref.shape[0]):
+        share_ref[half] = left_ref[(lax.axis_index("ma") ^ step) * lax.axis_size("pol") + half]
+
+
+def operands(m_ref, block_refs, steps, maps):
     ell = block_refs[0].shape[1]
-    left, right_real, right_imag = [], [], []
+    blocks, right_real, right_imag = [], [], []
     for ref, (step, other) in zip(block_refs, steps, strict=True):
         owner = lax.axis_index("ma") ^ step
         half = lax.axis_index("pol") ^ other
         block = owner * lax.axis_size("pol") + half
-        degree = block * ell + lax.broadcasted_iota(jnp.int32, (ell, ref.shape[2]), 0)
+        real, imag = ref[0, :, maps], ref[1, :, maps]
+        degree = block * ell + lax.broadcasted_iota(jnp.int32, real.shape, 0)
         keep = degree >= m_ref[0]
-        real = jnp.where(keep, ref[0], jnp.zeros((), ref.dtype))
-        imag = jnp.where(keep, ref[1], jnp.zeros((), ref.dtype))
-        left.append(left_ref[block])
+        real = jnp.where(keep, real, jnp.zeros((), ref.dtype))
+        imag = jnp.where(keep, imag, jnp.zeros((), ref.dtype))
+        blocks.append(block)
         right_real += [real, -imag]
         right_imag += [imag, real]
-    left = jnp.concatenate(left, axis=1)
-    dot = functools.partial(jnp.dot, preferred_element_type=jnp.float32)
-    return (
-        dot(left, jnp.concatenate(right_real, axis=0)),
-        dot(left, jnp.concatenate(right_imag, axis=0)),
-    )
+    return blocks, jnp.concatenate(right_real, axis=0), jnp.concatenate(right_imag, axis=0)
+
+
+dot = functools.partial(jnp.dot, preferred_element_type=jnp.float32)
 
 
 def first_kernel(steps, m_ref, mask_ref, left_ref, *refs):
     del mask_ref
-    *blocks, vis_ref = refs
-    vis_ref[0], vis_ref[1] = contract(m_ref, left_ref, blocks, steps)
+    *block_refs, mine_ref, give_ref = refs
+    pol, count = lax.axis_index("pol"), mine_ref.shape[2]
+    for ref, owner in ((mine_ref, pol), (give_ref, pol ^ 1)):
+        blocks, *rights = operands(m_ref, block_refs, steps, maps_of(owner, count))
+        left = jnp.concatenate([left_ref[block] for block in blocks], axis=1)
+        for c, right in enumerate(rights):
+            ref[c] = dot(left, right)
+
+
+def same_kernel(step, m_ref, left_ref, share_ref, mine_ref, got_ref, block_ref, near_ref, far_ref):
+    (block,), *rights = operands(m_ref, [block_ref], [(step, 0)], slice(None))
+    shared = share_ref[lax.axis_index("pol")]
+    for c, right in enumerate(rights):
+        near_ref[c] = mine_ref[c] + dot(left_ref[block], right)
+        far_ref[c] = got_ref[c] + dot(shared, right)
 
 
 def weigh(vis, weight):
@@ -79,30 +112,35 @@
     )
 
 
-def power_of(real, imag):
-    squares = real * real + imag * imag
-    folded = functools.reduce(
-        jnp.add, [squares[:, i : i + 128] for i in range(0, squares.shape[1], 128)]
-    )
-    return jnp.sum(folded)
-
-
-def next_kernel(steps, m_ref, left_ref, before_ref, *refs):
-    *blocks, vis_ref = refs
-    real, imag = contract(m_ref, left_ref, blocks, steps)
-    vis_ref[0] = real + before_ref[0]
-    vis_ref[1] = imag + before_ref[1]
-
-
-def last_kernel(steps, slots, m_ref, mask_ref, left_ref, weight_ref, before_ref, *refs):
-    *blocks, vis_ref, power_ref = refs
-    real, imag = contract(m_ref, left_ref, blocks, steps)
-    weight = weight_ref[...]
-    real = weigh(real + before_ref[0], weight)
-    imag = weigh(imag + before_ref[1], weight)
-    vis_ref[0] = real
-    vis_ref[1] = imag
-    total = power_of(real, imag)
+def last_kernel(
+    step,
+    slots,
+    m_ref,
+    mask_ref,
+    left_ref,
+    share_ref,
+    weight_ref,
+    other_ref,
+    mine_ref,
+    got_ref,
+    block_ref,
+    near_ref,
+    far_ref,
+    power_ref,
+):
+    (block,), *rights = operands(m_ref, [block_ref], [(step, 1)], slice(None))
+    sums = jnp.zeros(weight_ref.shape, jnp.float32)
+    for left, before_ref, weights_ref, ref in (
+        (share_ref[lax.axis_index("pol") ^ 1], got_ref, other_ref, far_ref),
+        (left_ref[block], mine_ref, weight_ref, near_ref),
+    ):
+        weight = weights_ref[...]
+        for c, right in enumerate(rights):
+            vis = weigh(before_ref[c] + dot(left, right), weight)
+            ref[c] = vis
+            for i in range(0, vis.shape[1], 128):
+                sums += vis[:, i : i + 128] * vis[:, i : i + 128]
+    total = jnp.sum(sums)
     lane = lax.broadcasted_iota(jnp.int32, power_ref.shape, 1)
     leader = (lax.axis_index("ma") == 0) & (lax.axis_index("pol") == 0)
     live = jnp.where(leader, mask_ref[0], 0).astype(jnp.float32)
@@ -112,7 +150,7 @@
     )
 
 
-def finish_kernel(slots, modes, mask_ref, total_ref, vis_ref, scaled_ref, power_ref, held_ref, own_ref, sems):
+def finish_kernel(slots, modes, mask_ref, total_ref, near_ref, got_ref, scaled_ref, power_ref, held_ref, own_ref, sems):
     lane = lax.broadcasted_iota(jnp.int32, (1, 128), 1)
     totals = total_ref[0:1, :]
     powers = totals / modes
@@ -128,21 +166,23 @@
     own_ref[...] = jnp.where(lane == 0, own, 0.0)
     copies = [pltpu.make_async_copy(own_ref, power_ref, sems.at[0])]
     copies[0].start()
-    parts, rows, _ = vis_ref.shape
-    chunk = rows // 4
+    parts, rows, count = near_ref.shape
+    pol = lax.axis_index("pol")
+    chunk = rows // 2
     for c in range(parts):
         for j in range(0, rows, chunk):
-            held_ref[c, j : j + chunk] = (vis_ref[c, j : j + chunk] * factor).astype(
-                scaled_ref.dtype
-            )
-            copies.append(
-                pltpu.make_async_copy(
-                    held_ref.at[c, pl.ds(j, chunk)],
-                    scaled_ref.at[c, pl.ds(j, chunk)],
-                    sems.at[len(copies)],
+            for half, (ref, owner) in enumerate(((near_ref, pol), (got_ref, pol ^ 1))):
+                held_ref[half, c, j : j + chunk] = (ref[c, j : j + chunk] * factor).astype(
+                    scaled_ref.dtype
                 )
-            )
-            copies[-1].start()
+                copies.append(
+                    pltpu.make_async_copy(
+                        held_ref.at[half, c, pl.ds(j, chunk)],
+                        scaled_ref.at[c, pl.ds(j, chunk), maps_of(owner, count)],
+                        sems.at[len(copies)],
+                    )
+                )
+                copies[-1].start()
     for copy in copies:
         copy.wait()
 
@@ -164,8 +204,13 @@
     modes = beam.shape[3]
     response = beam[0, 0]
     params = pltpu.CompilerParams(vmem_limit_bytes=24 << 20)
-    vis_shape = jax.ShapeDtypeStruct((parts, modes, maps), jnp.float32)
-    slab = jax.ShapeDtypeStruct((parts, ell, maps), alm.dtype)
+
+    def visible(count):
+        return jax.ShapeDtypeStruct((parts, modes, count), jnp.float32)
+
+    def slab(count):
+        return jax.ShapeDtypeStruct((parts, ell, count), alm.dtype)
+
     row = jax.ShapeDtypeStruct((8, 128), jnp.float32)
     weights = jax.ShapeDtypeStruct((modes, 128), jnp.float32)
 
@@ -175,7 +220,7 @@
             out_shape=out_shape,
             in_specs=more.pop("in_specs", [SMEM] * len(scalars) + [VMEM] * len(operands)),
             out_specs=more.pop("out_specs", jax.tree.map(lambda _: VMEM, out_shape)),
-            compiler_params=params,
+            compiler_params=more.pop("compiler_params", params),
             cost_estimate=pl.CostEstimate(
                 flops=blocks * 2 * 4 * modes * maps * ell,
                 bytes_accessed=(blocks + 4) * parts * ell * (maps + modes) * 2,
@@ -184,50 +229,69 @@
             **more,
         )(*scalars, *operands)
 
-    three, one, two, own = call(
-        functools.partial(split_kernel, (3, 1, 2, 0)),
-        [slab] * n_ma,
+    half = maps // n_pol
+    pieces = ((2, None), (1, None), (3, 0), (3, 1), (0, None))
+    two, one, same, cross, own = call(
+        functools.partial(split_kernel, pieces),
+        [slab(maps if other is None else half) for _, other in pieces],
         (),
-        (alm[:, 0],),
+        (pltpu.with_memory_space_constraint(alm[:, 0], pltpu.HBM),),
         0,
-        scratch_shapes=[pltpu.VMEM((n_ma, ell, maps), alm.dtype)],
-    )
-    three = straight(three, "ma", 3)
+        in_specs=[HBM],
+        scratch_shapes=[
+            pltpu.VMEM((parts, ell, n_ma, maps), alm.dtype),
+            pltpu.VMEM((n_ma, ell // 2, maps), alm.dtype),
+            pltpu.SemaphoreType.DMA((2 * parts,)),
+        ],
+    )
+    two = straight(two, "ma", 2)
     one = straight(one, "ma", 1)
-    two = straight(two, "ma", 2)
+    same = straight(same, "ma", 3)
+    cross = swap(cross, "ma", 3)
     own_far = swap(own, "pol", 1)
     one_far = swap(one, "pol", 1)
-    three_far = swap(three, "pol", 1)
     two_far = swap(two, "pol", 1)
     blocks = n_ma * n_pol
-    left, weight = call(
-        load_kernel,
-        (jax.ShapeDtypeStruct((blocks, modes, 2 * ell), beam.dtype), weights),
+    left, share, weight = call(
+        functools.partial(load_kernel, 3),
+        (
+            jax.ShapeDtypeStruct((blocks, modes, 2 * ell), beam.dtype),
+            jax.ShapeDtypeStruct((n_pol, modes, 2 * ell), beam.dtype),
+            weights,
+        ),
         (),
-        (response, noise),
+        (pltpu.with_memory_space_constraint(response, pltpu.HBM), noise),
         0,
         in_specs=[HBM, VMEM],
         scratch_shapes=[pltpu.SemaphoreType.DMA((2 * blocks,))],
     )
+    share = swap(share, "pol", 1)
+    other_weight = swap(weight, "pol", 1)
     steps = ((0, 0), (0, 1), (1, 0), (1, 1), (2, 0), (2, 1))
-    vis = call(
+    mine, give = call(
         functools.partial(first_kernel, steps),
-        vis_shape,
+        (visible(half), visible(half)),
         (m_table, chan_mask),
         (left, own, own_far, one, one_far, two, two_far),
         6,
     )
-    vis = call(
-        functools.partial(next_kernel, ((3, 0),)), vis_shape, (m_table,), (left, vis, three), 1
-    )
-    vis, total = call(
-        functools.partial(last_kernel, ((3, 1),), n_freq),
-        (vis_shape, row),
+    got = swap(give, "pol", 1)
+    mine, got = call(
+        functools.partial(same_kernel, 3),
+        (visible(half), visible(half)),
+        (m_table,),
+        (left, share, mine, got, same),
+        1,
+    )
+    near, far, total = call(
+        functools.partial(last_kernel, 3, n_freq),
+        (visible(half), visible(half), row),
         (m_table, chan_mask),
-        (left, weight, vis, three_far),
+        (left, share, weight, other_weight, mine, got, cross),
         1,
     )
-    for name, step in (('pol', 1), ('freq', 1), ('ma', 3), ('ma', 1)):
+    far = swap(far, "pol", 1)
+    for name, step in (("pol", 1), ("freq", 1), ("ma", 3), ("ma", 1)):
         total = total + swap(total, name, step)
     scaled, own_power = call(
         functools.partial(finish_kernel, n_freq, n_ma * n_pol * modes * maps),
@@ -236,11 +300,11 @@
             jax.ShapeDtypeStruct((1, 128), jnp.float32),
         ),
         (chan_mask,),
-        (total, vis),
+        (total, near, far),
         0,
         out_specs=(HBM, HBM),
         scratch_shapes=[
-            pltpu.VMEM((parts, modes, maps), jnp.bfloat16),
+            pltpu.VMEM((n_pol, parts, modes, half), jnp.bfloat16),
             pltpu.VMEM((1, 128), jnp.float32),
             pltpu.SemaphoreType.DMA((4 * parts + 1,)),
         ],

time: 49.1 us -> 52.1 us (1.061)
  starting transfers between devices: 12.4 us -> 15.7 us
  local copies, waits for them, and re-layouts: 3.49 us -> 0.68 us
  Pallas kernels: 5.34 us -> 7.23 us
  waiting for transfers between devices: 25.6 us -> 26.3 us
    ppermute x8 -> x12, waiting for transfers between devices: 6.85 us -> 10.4 us  [swap(): return lax.ppermute(x, names, [(i, i ^ flip) for i in range(size)])]
    unnamed x6 -> x2, local copies, waits for them, and re-layouts: 3.49 us -> 0.68 us
    ppermute x3, waiting for transfers between devices: 18.7 us -> 15.9 us  [straight(): return lax.ppermute(x, name, [(i, i ^ step) for i in range(size)])]
    ppermute x3, starting transfers between devices: 5.71 us -> 8.18 us  [straight(): return lax.ppermute(x, name, [(i, i ^ step) for i in range(size)])]
    pallas_call x6, Pallas kernels: 5.34 us -> 7.23 us  [call(): pl.pallas_call(kernel, out_shape=out_shape, in_specs=more.pop('in_specs',...]
    ppermute x8 -> x12, starting transfers between devices: 6.71 us -> 7.47 us  [swap(): return lax.ppermute(x, names, [(i, i ^ flip) for i in range(size)])]
  transfers between devices with their start and end apart: 11 -> 15, of which waited for: 6 -> 8; matrix products, arithmetic and copies ran while one was open for 0% -> 0% of each run, Pallas kernels for 6% -> 4%
where the time goes in v5:
time: 52.1 us; the launch traced here: 51.9 us
  waiting for transfers between devices  26.3 us (50%)
  starting transfers between devices  15.7 us (30%)
  Pallas kernels  7.23 us (14%)
  between operations  2.01 us (4%)
  local copies, waits for them, and re-layouts  0.68 us (1%)
    ppermute x3, waiting for transfers between devices, straight(): return lax.ppermute(x, name, [(i, i ^ step) for i in range(size)])  15.9 us
    ppermute x12, waiting for transfers between devices, swap(): return lax.ppermute(x, names, [(i, i ^ flip) for i in range(size)])  10.4 us
    ppermute x3, starting transfers between devices, straight(): return lax.ppermute(x, name, [(i, i ^ step) for i in range(size)])  8.18 us
    ppermute x12, starting transfers between devices, swap(): return lax.ppermute(x, names, [(i, i ^ flip) for i in range(size)])  7.47 us
    pallas_call x6, Pallas kernels, call(): pl.pallas_call(kernel, out_shape=out_shape, in_specs=more.pop('in_specs',...  7.23 us
  transfers between devices with their start and end apart: 15, of which 8 were waited for; matrix products, arithmetic and copies ran while one was open for 0% of the time, Pallas kernels for 4%

profile of v5, /device:TPU:0, one launch (start us, length us, event | category | flops | bytes accessed | tf_op | source)
XLA Modules:
  0.0 51.9 jit_solution(16774086377221158379)
XLA Ops:
  0.6 1.3 %shard_map.69 = (bf16[2,128,512]{2,1,0:T(8,128)(2,1)S(1)}, bf16[2,128,512]{2,1,0:T(8,128)(2,1)S(1)}, bf16[2,128,256]{2,1,0:T(8,128)(2,1)S(1)}, bf16[2,128,256]{2,1,0:T(8,128)(2,1)S(1)}, bf16[2,128,512]{2,1,0:T(8,128)(2,1)S(1)}) custom-call(bf16[2,128,4,512]{3,2,1,0:T(4,128)(2,1)} %bitcast.8), custom_call_target="tpu_custom_call" | custom-call | bytes 2097152 | tf_op jit(solution)/shard_map/pallas_call | solution.py:218
  1.9 3.1 %collective-permute-start.3 = (bf16[2,128,512]{2,1,0:T(8,128)(2,1)S(1)}, bf16[2,128,512]{2,1,0:T(8,128)(2,1)S(1)}, u32[]{:S(2)}, u32[]{:S(2)}) collective-permute-start(bf16[2,128,512]{2,1,0:T(8,128)(2,1)S(1)} %get-tuple-element.23), channel_id=1, source_target_pairs={{0,4},{4,0},{8,12},{12,8},{1,5},{5,1},{9,13},{13,9},{2,6},{6,2},{1... | collective-permute-start | bytes 786440 | tf_op jit(solution)/shard_map/ppermute | solution.py:192
  5.1 2.6 %collective-permute-start.5 = (bf16[2,128,512]{2,1,0:T(8,128)(2,1)S(1)}, bf16[2,128,512]{2,1,0:T(8,128)(2,1)S(1)}, u32[]{:S(2)}, u32[]{:S(2)}) collective-permute-start(bf16[2,128,512]{2,1,0:T(8,128)(2,1)S(1)} %get-tuple-element.24), channel_id=1, source_target_pairs={{0,8},{4,12},{8,0},{12,4},{1,9},{5,13},{9,1},{13,5},{2,10},{6,14},... | collective-permute-start | bytes 786440 | tf_op jit(solution)/shard_map/ppermute | solution.py:192
  7.6 0.0 collective-permute-start.2
  7.6 9.2 %collective-permute-done.3.refs_2_ = bf16[2,128,512]{2,1,0:T(8,128)(2,1)S(1)} collective-permute-done((bf16[2,128,512]{2,1,0:T(8,128)(2,1)S(1)}, bf16[2,128,512]{2,1,0:T(8,128)(2,1)S(1)}, u32[]{:S(2)}, u32[]{:S(2)}) %collective-permute-start.3) | collective-permute-done | bytes 262176 | tf_op jit(solution)/shard_map/ppermute | solution.py:192
  16.9 0.0 collective-permute-start.4
  16.9 2.5 %collective-permute-done.5.refs_4_ = bf16[2,128,512]{2,1,0:T(8,128)(2,1)S(1)} collective-permute-done((bf16[2,128,512]{2,1,0:T(8,128)(2,1)S(1)}, bf16[2,128,512]{2,1,0:T(8,128)(2,1)S(1)}, u32[]{:S(2)}, u32[]{:S(2)}) %collective-permute-start.5) | collective-permute-done | bytes 262176 | tf_op jit(solution)/shard_map/ppermute | solution.py:192
  20.7 0.0 copy-start
  20.7 0.7 %copy-done = f32[1,512]{1,0:T(1,128)S(1)} copy-done((f32[1,512]{1,0:T(1,128)S(1)}, f32[1,512]{1,0:T(1,128)}, u32[]{:S(2)}) %copy-start) | copy-done | bytes 2072
  21.4 1.8 %shard_map.68 = (bf16[8,512,256]{2,1,0:T(8,128)(2,1)S(1)}, bf16[2,512,256]{2,1,0:T(8,128)(2,1)S(1)}, f32[512,128]{1,0:T(8,128)S(1)}) custom-call(bf16[2,512,1024]{2,1,0:T(8,128)(2,1)} %bitcast.7, f32[1,512]{1,0:T(1,128)S(1)} %copy-done), custom_call_target="tpu_custom_call" | custom-call | bytes 2097152 | tf_op jit(solution)/shard_map/pallas_call | solution.py:218
  23.2 0.0 collective-permute-done.2.refs_1_
  23.2 0.0 collective-permute-done.4.refs_3_
  23.2 1.8 %shard_map.70 = (f32[2,512,256]{2,1,0:T(8,128)S(1)}, f32[2,512,256]{2,1,0:T(8,128)S(1)}) custom-call(s32[1]{0:T(128)S(6)} %copy.8.m_ref, s32[1]{0:T(128)S(6)} %copy.9.mask_ref, bf16[8,512,256]{2,1,0:T(8,128)(2,1)S(1)} %get-tuple-element.19.left_ref, bf16[2,128,512]{2,1,0:T(8,128)(2,1)S(1)} %get-tuple-element.22.refs_0_, ...), custom_call_target="tpu_custom_call" | custom-call | flops 1610612736 | bytes 5242880 | tf_op jit(solution)/shard_map/pallas_call | solution.py:218
  25.1 0.6 %collective-permute-start.7 = (f32[2,512,256]{2,1,0:T(8,128)S(1)}, f32[2,512,256]{2,1,0:T(8,128)S(1)}, u32[]{:S(2)}, u32[]{:S(2)}) collective-permute-start(f32[2,512,256]{2,1,0:T(8,128)S(1)} %get-tuple-element.26), channel_id=1, source_target_pairs={{0,1},{1,0},{2,3},{3,2},{4,5},{5,4},{6,7},{7,6},{8,9},{9,8},{10,11... | collective-permute-start | bytes 3145736 | tf_op jit(solution)/shard_map/ppermute | solution.py:198
  25.6 0.1 collective-permute-start
  25.7 0.4 collective-permute-start.1
  26.1 2.5 %collective-permute-start.8 = (bf16[2,128,256]{2,1,0:T(8,128)(2,1)S(1)}, bf16[2,128,256]{2,1,0:T(8,128)(2,1)S(1)}, u32[]{:S(2)}, u32[]{:S(2)}) collective-permute-start(bf16[2,128,256]{2,1,0:T(8,128)(2,1)S(1)} %get-tuple-element.27), channel_id=1, source_target_pairs={{0,12},{4,8},{8,4},{12,0},{1,13},{5,9},{9,5},{13,1},{2,14},{6,10},... | collective-permute-start | bytes 393224 | tf_op jit(solution)/shard_map/ppermute | solution.py:192
  28.6 0.8 %collective-permute-start.9 = (bf16[2,128,256]{2,1,0:T(8,128)(2,1)S(1)}, bf16[2,128,256]{2,1,0:T(8,128)(2,1)S(1)}, u32[]{:S(2)}, u32[]{:S(2)}) collective-permute-start(bf16[2,128,256]{2,1,0:T(8,128)(2,1)S(1)} %get-tuple-element.30), channel_id=1, source_target_pairs={{0,13},{1,12},{4,9},{5,8},{8,5},{9,4},{12,1},{13,0},{2,15},{3,14},... | collective-permute-start | bytes 393224 | tf_op jit(solution)/shard_map/ppermute | solution.py:198
  29.4 4.2 %collective-permute-done.8.block_ref = bf16[2,128,256]{2,1,0:T(8,128)(2,1)S(1)} collective-permute-done((bf16[2,128,256]{2,1,0:T(8,128)(2,1)S(1)}, bf16[2,128,256]{2,1,0:T(8,128)(2,1)S(1)}, u32[]{:S(2)}, u32[]{:S(2)}) %collective-permute-start.8) | collective-permute-done | bytes 131104 | tf_op jit(solution)/shard_map/ppermute | solution.py:192
  33.6 0.4 shard_map.71
  34.0 2.2 %collective-permute-done.9.block_ref = bf16[2,128,256]{2,1,0:T(8,128)(2,1)S(1)} collective-permute-done((bf16[2,128,256]{2,1,0:T(8,128)(2,1)S(1)}, bf16[2,128,256]{2,1,0:T(8,128)(2,1)S(1)}, u32[]{:S(2)}, u32[]{:S(2)}) %collective-permute-start.9) | collective-permute-done | bytes 131104 | tf_op jit(solution)/shard_map/ppermute | solution.py:198
  36.3 0.6 %shard_map.72 = (f32[2,512,256]{2,1,0:T(8,128)S(1)}, f32[2,512,256]{2,1,0:T(8,128)S(1)}, f32[8,128]{1,0:T(8,128)S(1)}) custom-call(s32[1]{0:T(128)S(6)} %copy.8.m_ref, s32[1]{0:T(128)S(6)} %copy.9.mask_ref, bf16[8,512,256]{2,1,0:T(8,128)(2,1)S(1)} %get-tuple-element.19.left_ref, bf16[2,512,256]{2,1,0:T(8,128)(2,1)S(1)} %collective-permute-done.share_ref, ...), custom_call_target="tpu_custom_call" | custom-call | flops 268435456 | bytes 2621440 | tf_op jit(solution)/shard_map/pallas_call | solution.py:218
  36.9 0.1 collective-permute-start.14
  37.0 0.5 collective-permute-start.10
  37.5 2.2 %collective-permute-done.10 = f32[8,128]{1,0:T(8,128)S(1)} collective-permute-done((f32[8,128]{1,0:T(8,128)S(1)}, f32[8,128]{1,0:T(8,128)S(1)}, u32[]{:S(2)}, u32[]{:S(2)}) %collective-permute-start.10) | collective-permute-done | bytes 4128 | tf_op jit(solution)/shard_map/ppermute | solution.py:198
  39.6 1.2 %collective-permute-start.11 = (f32[8,128]{1,0:T(8,128)S(1)}, f32[8,128]{1,0:T(8,128)S(1)}, u32[]{:S(2)}, u32[]{:S(2)}) collective-permute-start(f32[8,128]{1,0:T(8,128)S(1)} %add.12), channel_id=1, source_target_pairs={{0,3},{1,2},{2,1},{3,0},{4,7},{5,6},{6,5},{7,4},{8,11},{9,10},{10,... | collective-permute-start | bytes 12296 | tf_op jit(solution)/shard_map/ppermute | solution.py:198
  40.9 1.8 %collective-permute-done.11 = f32[8,128]{1,0:T(8,128)S(1)} collective-permute-done((f32[8,128]{1,0:T(8,128)S(1)}, f32[8,128]{1,0:T(8,128)S(1)}, u32[]{:S(2)}, u32[]{:S(2)}) %collective-permute-start.11) | collective-permute-done | bytes 4128 | tf_op jit(solution)/shard_map/ppermute | solution.py:198
  42.7 2.0 %collective-permute-start.12 = (f32[8,128]{1,0:T(8,128)S(1)}, f32[8,128]{1,0:T(8,128)S(1)}, u32[]{:S(2)}, u32[]{:S(2)}) collective-permute-start(f32[8,128]{1,0:T(8,128)S(1)} %add.13), channel_id=1, source_target_pairs={{0,13},{1,12},{4,9},{5,8},{8,5},{9,4},{12,1},{13,0},{2,15},{3,14},... | collective-permute-start | bytes 12296 | tf_op jit(solution)/shard_map/ppermute | solution.py:198
  44.6 2.9 %collective-permute-done.12 = f32[8,128]{1,0:T(8,128)S(1)} collective-permute-done((f32[8,128]{1,0:T(8,128)S(1)}, f32[8,128]{1,0:T(8,128)S(1)}, u32[]{:S(2)}, u32[]{:S(2)}) %collective-permute-start.12) | collective-permute-done | bytes 4128 | tf_op jit(solution)/shard_map/ppermute | solution.py:198
  47.5 1.9 %collective-permute-start.13 = (f32[8,128]{1,0:T(8,128)S(1)}, f32[8,128]{1,0:T(8,128)S(1)}, u32[]{:S(2)}, u32[]{:S(2)}) collective-permute-start(f32[8,128]{1,0:T(8,128)S(1)} %add.14), channel_id=1, source_target_pairs={{0,5},{1,4},{4,1},{5,0},{8,13},{9,12},{12,9},{13,8},{2,7},{3,6},{6... | collective-permute-start | bytes 12296 | tf_op jit(solution)/shard_map/ppermute | solution.py:198
  49.4 1.3 %collective-permute-done.13 = f32[8,128]{1,0:T(8,128)S(1)} collective-permute-done((f32[8,128]{1,0:T(8,128)S(1)}, f32[8,128]{1,0:T(8,128)S(1)}, u32[]{:S(2)}, u32[]{:S(2)}) %collective-permute-start.13) | collective-permute-done | bytes 4128 | tf_op jit(solution)/shard_map/ppermute | solution.py:198
  50.7 1.2 %shard_map.73 = (bf16[2,512,512]{2,1,0:T(8,128)(2,1)}, f32[1,128]{1,0:T(1,128)}) custom-call(s32[1]{0:T(128)S(6)} %copy.9.mask_ref, f32[8,128]{1,0:T(8,128)S(1)} %add.15.total_ref, f32[2,512,256]{2,1,0:T(8,128)S(1)} %get-tuple-element.32.near_ref, f32[2,512,256]{2,1,0:T(8,128)S(1)} %collective-permute-done.14.got_ref), custom_call_target="tpu_custom_call" | custom-call | bytes 2097152 | tf_op jit(solution)/shard_map/pallas_call | solution.py:218
  (10 shorter events, 0.0 us)
Async XLA Ops:
  1.9 14.9 %collective-permute-start.3 = (bf16[2,128,512]{2,1,0:T(8,128)(2,1)S(1)}, bf16[2,128,512]{2,1,0:T(8,128)(2,1)S(1)}, u32[]{:S(2)}, u32[]{:S(2)}) collective-permute-start(bf16[2,128,512]{2,1,0:T(8,128)(2,1)S(1)} %get-tuple-element.23), channel_id=1, source_target_pairs={{0,4},{4,0},{8,12},{12,8},{1,5},{5,1},{9,13},{13,9},{2,6},{6,2},{1... | collective-permute-start | bytes 786440 | tf_op jit(solution)/shard_map/ppermute | solution.py:192
  5.1 14.3 %collective-permute-start.5 = (bf16[2,128,512]{2,1,0:T(8,128)(2,1)S(1)}, bf16[2,128,512]{2,1,0:T(8,128)(2,1)S(1)}, u32[]{:S(2)}, u32[]{:S(2)}) collective-permute-start(bf16[2,128,512]{2,1,0:T(8,128)(2,1)S(1)} %get-tuple-element.24), channel_id=1, source_target_pairs={{0,8},{4,12},{8,0},{12,4},{1,9},{5,13},{9,1},{13,5},{2,10},{6,14},... | collective-permute-start | bytes 786440 | tf_op jit(solution)/shard_map/ppermute | solution.py:192
  7.6 15.6 %collective-permute-start.2 = (bf16[2,128,512]{2,1,0:T(8,128)(2,1)S(1)}, bf16[2,128,512]{2,1,0:T(8,128)(2,1)S(1)}, u32[]{:S(2)}, u32[]{:S(2)}) collective-permute-start(bf16[2,128,512]{2,1,0:T(8,128)(2,1)S(1)} %get-tuple-element.22.refs_0_), channel_id=1, source_target_pairs={{0,1},{1,0},{2,3},{3,2},{4,5},{5,4},{6,7},{7,6},{8,9},{9,8},{10,11... | collective-permute-start | bytes 786440 | tf_op jit(solution)/shard_map/ppermute | solution.py:198
  16.9 6.4 %collective-permute-start.4 = (bf16[2,128,512]{2,1,0:T(8,128)(2,1)S(1)}, bf16[2,128,512]{2,1,0:T(8,128)(2,1)S(1)}, u32[]{:S(2)}, u32[]{:S(2)}) collective-permute-start(bf16[2,128,512]{2,1,0:T(8,128)(2,1)S(1)} %collective-permute-done.3.refs_2_), channel_id=1, source_target_pairs={{0,1},{1,0},{2,3},{3,2},{4,5},{5,4},{6,7},{7,6},{8,9},{9,8},{10,11... | collective-permute-start | bytes 786440 | tf_op jit(solution)/shard_map/ppermute | solution.py:198
  19.4 3.9 %collective-permute-start.6 = (bf16[2,128,512]{2,1,0:T(8,128)(2,1)S(1)}, bf16[2,128,512]{2,1,0:T(8,128)(2,1)S(1)}, u32[]{:S(2)}, u32[]{:S(2)}) collective-permute-start(bf16[2,128,512]{2,1,0:T(8,128)(2,1)S(1)} %collective-permute-done.5.refs_4_), channel_id=1, source_target_pairs={{0,1},{1,0},{2,3},{3,2},{4,5},{5,4},{6,7},{7,6},{8,9},{9,8},{10,11... | collective-permute-start | bytes 786440 | tf_op jit(solution)/shard_map/ppermute | solution.py:198
  20.7 0.7 %copy-start = (f32[1,512]{1,0:T(1,128)S(1)}, f32[1,512]{1,0:T(1,128)}, u32[]{:S(2)}) copy-start(f32[1,512]{1,0:T(1,128)} %noise_ref.1) | copy-start | bytes 6148
  25.1 8.5 %collective-permute-start.7 = (f32[2,512,256]{2,1,0:T(8,128)S(1)}, f32[2,512,256]{2,1,0:T(8,128)S(1)}, u32[]{:S(2)}, u32[]{:S(2)}) collective-permute-start(f32[2,512,256]{2,1,0:T(8,128)S(1)} %get-tuple-element.26), channel_id=1, source_target_pairs={{0,1},{1,0},{2,3},{3,2},{4,5},{5,4},{6,7},{7,6},{8,9},{9,8},{10,11... | collective-permute-start | bytes 3145736 | tf_op jit(solution)/shard_map/ppermute | solution.py:198
  25.6 8.0 %collective-permute-start = (bf16[2,512,256]{2,1,0:T(8,128)(2,1)S(1)}, bf16[2,512,256]{2,1,0:T(8,128)(2,1)S(1)}, u32[]{:S(2)}, u32[]{:S(2)}) collective-permute-start(bf16[2,512,256]{2,1,0:T(8,128)(2,1)S(1)} %get-tuple-element.20), channel_id=1, source_target_pairs={{0,1},{1,0},{2,3},{3,2},{4,5},{5,4},{6,7},{7,6},{8,9},{9,8},{10,11... | collective-permute-start | bytes 1572872 | tf_op jit(solution)/shard_map/ppermute | solution.py:198
  25.7 10.6 %collective-permute-start.1 = (f32[512,128]{1,0:T(8,128)S(1)}, f32[512,128]{1,0:T(8,128)S(1)}, u32[]{:S(2)}, u32[]{:S(2)}) collective-permute-start(f32[512,128]{1,0:T(8,128)S(1)} %get-tuple-element.21.weight_ref), channel_id=1, source_target_pairs={{0,1},{1,0},{2,3},{3,2},{4,5},{5,4},{6,7},{7,6},{8,9},{9,8},{10,11... | collective-permute-start | bytes 786440 | tf_op jit(solution)/shard_map/ppermute | solution.py:198
  26.1 7.4 %collective-permute-start.8 = (bf16[2,128,256]{2,1,0:T(8,128)(2,1)S(1)}, bf16[2,128,256]{2,1,0:T(8,128)(2,1)S(1)}, u32[]{:S(2)}, u32[]{:S(2)}) collective-permute-start(bf16[2,128,256]{2,1,0:T(8,128)(2,1)S(1)} %get-tuple-element.27), channel_id=1, source_target_pairs={{0,12},{4,8},{8,4},{12,0},{1,13},{5,9},{9,5},{13,1},{2,14},{6,10},... | collective-permute-start | bytes 393224 | tf_op jit(solution)/shard_map/ppermute | solution.py:192
  28.6 7.6 %collective-permute-start.9 = (bf16[2,128,256]{2,1,0:T(8,128)(2,1)S(1)}, bf16[2,128,256]{2,1,0:T(8,128)(2,1)S(1)}, u32[]{:S(2)}, u32[]{:S(2)}) collective-permute-start(bf16[2,128,256]{2,1,0:T(8,128)(2,1)S(1)} %get-tuple-element.30), channel_id=1, source_target_pairs={{0,13},{1,12},{4,9},{5,8},{8,5},{9,4},{12,1},{13,0},{2,15},{3,14},... | collective-permute-start | bytes 393224 | tf_op jit(solution)/shard_map/ppermute | solution.py:198
  36.9 13.8 %collective-permute-start.14 = (f32[2,512,256]{2,1,0:T(8,128)S(1)}, f32[2,512,256]{2,1,0:T(8,128)S(1)}, u32[]{:S(2)}, u32[]{:S(2)}) collective-permute-start(f32[2,512,256]{2,1,0:T(8,128)S(1)} %get-tuple-element.33), channel_id=1, source_target_pairs={{0,1},{1,0},{2,3},{3,2},{4,5},{5,4},{6,7},{7,6},{8,9},{9,8},{10,11... | collective-permute-start | bytes 3145736 | tf_op jit(solution)/shard_map/ppermute | solution.py:198
  37.0 2.6 %collective-permute-start.10 = (f32[8,128]{1,0:T(8,128)S(1)}, f32[8,128]{1,0:T(8,128)S(1)}, u32[]{:S(2)}, u32[]{:S(2)}) collective-permute-start(f32[8,128]{1,0:T(8,128)S(1)} %get-tuple-element.31), channel_id=1, source_target_pairs={{0,1},{1,0},{2,3},{3,2},{4,5},{5,4},{6,7},{7,6},{8,9},{9,8},{10,11... | collective-permute-start | bytes 12296 | tf_op jit(solution)/shard_map/ppermute | solution.py:198
  39.6 3.0 %collective-permute-start.11 = (f32[8,128]{1,0:T(8,128)S(1)}, f32[8,128]{1,0:T(8,128)S(1)}, u32[]{:S(2)}, u32[]{:S(2)}) collective-permute-start(f32[8,128]{1,0:T(8,128)S(1)} %add.12), channel_id=1, source_target_pairs={{0,3},{1,2},{2,1},{3,0},{4,7},{5,6},{6,5},{7,4},{8,11},{9,10},{10,... | collective-permute-start | bytes 12296 | tf_op jit(solution)/shard_map/ppermute | solution.py:198
  42.7 4.8 %collective-permute-start.12 = (f32[8,128]{1,0:T(8,128)S(1)}, f32[8,128]{1,0:T(8,128)S(1)}, u32[]{:S(2)}, u32[]{:S(2)}) collective-permute-start(f32[8,128]{1,0:T(8,128)S(1)} %add.13), channel_id=1, source_target_pairs={{0,13},{1,12},{4,9},{5,8},{8,5},{9,4},{12,1},{13,0},{2,15},{3,14},... | collective-permute-start | bytes 12296 | tf_op jit(solution)/shard_map/ppermute | solution.py:198
  47.5 3.2 %collective-permute-start.13 = (f32[8,128]{1,0:T(8,128)S(1)}, f32[8,128]{1,0:T(8,128)S(1)}, u32[]{:S(2)}, u32[]{:S(2)}) collective-permute-start(f32[8,128]{1,0:T(8,128)S(1)} %add.14), channel_id=1, source_target_pairs={{0,5},{1,4},{4,1},{5,0},{8,13},{9,12},{12,9},{13,8},{2,7},{3,6},{6... | collective-permute-start | bytes 12296 | tf_op jit(solution)/shard_map/ppermute | solution.py:198

commit v6 on v5

--- a/solution.py
+++ b/solution.py
@@ -87,15 +87,14 @@
 dot = functools.partial(jnp.dot, preferred_element_type=jnp.float32)
 
 
-def first_kernel(steps, m_ref, mask_ref, left_ref, *refs):
+def first_kernel(steps, other, m_ref, mask_ref, left_ref, *refs):
     del mask_ref
-    *block_refs, mine_ref, give_ref = refs
-    pol, count = lax.axis_index("pol"), mine_ref.shape[2]
-    for ref, owner in ((mine_ref, pol), (give_ref, pol ^ 1)):
-        blocks, *rights = operands(m_ref, block_refs, steps, maps_of(owner, count))
-        left = jnp.concatenate([left_ref[block] for block in blocks], axis=1)
-        for c, right in enumerate(rights):
-            ref[c] = dot(left, right)
+    *block_refs, vis_ref = refs
+    maps = maps_of(lax.axis_index("pol") ^ other, vis_ref.shape[2])
+    blocks, *rights = operands(m_ref, block_refs, steps, maps)
+    left = jnp.concatenate([left_ref[block] for block in blocks], axis=1)
+    for c, right in enumerate(rights):
+        vis_ref[c] = dot(left, right)
 
 
 def same_kernel(step, m_ref, left_ref, share_ref, mine_ref, got_ref, block_ref, near_ref, far_ref):
@@ -268,12 +267,15 @@
     share = swap(share, "pol", 1)
     other_weight = swap(weight, "pol", 1)
     steps = ((0, 0), (0, 1), (1, 0), (1, 1), (2, 0), (2, 1))
-    mine, give = call(
-        functools.partial(first_kernel, steps),
-        (visible(half), visible(half)),
-        (m_table, chan_mask),
-        (left, own, own_far, one, one_far, two, two_far),
-        6,
+    give, mine = (
+        call(
+            functools.partial(first_kernel, steps, other),
+            visible(half),
+            (m_table, chan_mask),
+            (left, own, own_far, one, one_far, two, two_far),
+            3,
+        )
+        for other in (1, 0)
     )
     got = swap(give, "pol", 1)
     mine, got = call(

time: 52.1 us -> 51.3 us (0.985)
  waiting for transfers between devices: 26.3 us -> 25.3 us
    ppermute x3, waiting for transfers between devices: 15.9 us -> 15 us  [straight(): return lax.ppermute(x, name, [(i, i ^ step) for i in range(size)])]
    pallas_call x6 -> x7, Pallas kernels: 7.23 us -> 7.4 us  [call(): pl.pallas_call(kernel, out_shape=out_shape, in_specs=more.pop('in_specs',...]
  transfers between devices with their start and end apart: 15 -> 15, of which waited for: 8 -> 8; matrix products, arithmetic and copies ran while one was open for 0% -> 0% of each run, Pallas kernels for 4% -> 6%
where the time goes in v6:
time: 51.3 us; the launch traced here: 51.1 us
  waiting for transfers between devices  25.3 us (49%)
  starting transfers between devices  15.7 us (31%)
  Pallas kernels  7.4 us (14%)
  between operations  2.01 us (4%)
  local copies, waits for them, and re-layouts  0.68 us (1%)
    ppermute x3, waiting for transfers between devices, straight(): return lax.ppermute(x, name, [(i, i ^ step) for i in range(size)])  15 us
    ppermute x12, waiting for transfers between devices, swap(): return lax.ppermute(x, names, [(i, i ^ flip) for i in range(size)])  10.4 us
    ppermute x3, starting transfers between devices, straight(): return lax.ppermute(x, name, [(i, i ^ step) for i in range(size)])  8.18 us
    ppermute x12, starting transfers between devices, swap(): return lax.ppermute(x, names, [(i, i ^ flip) for i in range(size)])  7.48 us
    pallas_call x7, Pallas kernels, call(): pl.pallas_call(kernel, out_shape=out_shape, in_specs=more.pop('in_specs',...  7.4 us
  transfers between devices with their start and end apart: 15, of which 8 were waited for; matrix products, arithmetic and copies ran while one was open for 0% of the time, Pallas kernels for 6%

profile of v6, /device:TPU:0, one launch (start us, length us, event | category | flops | bytes accessed | tf_op | source)
XLA Modules:
  0.0 51.1 jit_solution(18205303458804946027)
XLA Ops:
  0.6 1.3 %shard_map.69 = (bf16[2,128,512]{2,1,0:T(8,128)(2,1)S(1)}, bf16[2,128,512]{2,1,0:T(8,128)(2,1)S(1)}, bf16[2,128,256]{2,1,0:T(8,128)(2,1)S(1)}, bf16[2,128,256]{2,1,0:T(8,128)(2,1)S(1)}, bf16[2,128,512]{2,1,0:T(8,128)(2,1)S(1)}) custom-call(bf16[2,128,4,512]{3,2,1,0:T(4,128)(2,1)} %bitcast.8), custom_call_target="tpu_custom_call" | custom-call | bytes 2097152 | tf_op jit(solution)/shard_map/pallas_call | solution.py:217
  1.9 3.1 %collective-permute-start.3 = (bf16[2,128,512]{2,1,0:T(8,128)(2,1)S(1)}, bf16[2,128,512]{2,1,0:T(8,128)(2,1)S(1)}, u32[]{:S(2)}, u32[]{:S(2)}) collective-permute-start(bf16[2,128,512]{2,1,0:T(8,128)(2,1)S(1)} %get-tuple-element.21), channel_id=1, source_target_pairs={{0,4},{4,0},{8,12},{12,8},{1,5},{5,1},{9,13},{13,9},{2,6},{6,2},{1... | collective-permute-start | bytes 786440 | tf_op jit(solution)/shard_map/ppermute | solution.py:191
  5.1 2.6 %collective-permute-start.5 = (bf16[2,128,512]{2,1,0:T(8,128)(2,1)S(1)}, bf16[2,128,512]{2,1,0:T(8,128)(2,1)S(1)}, u32[]{:S(2)}, u32[]{:S(2)}) collective-permute-start(bf16[2,128,512]{2,1,0:T(8,128)(2,1)S(1)} %get-tuple-element.22), channel_id=1, source_target_pairs={{0,8},{4,12},{8,0},{12,4},{1,9},{5,13},{9,1},{13,5},{2,10},{6,14},... | collective-permute-start | bytes 786440 | tf_op jit(solution)/shard_map/ppermute | solution.py:191
  7.6 0.0 collective-permute-start.2
  7.6 9.2 %collective-permute-done.3.refs_2_ = bf16[2,128,512]{2,1,0:T(8,128)(2,1)S(1)} collective-permute-done((bf16[2,128,512]{2,1,0:T(8,128)(2,1)S(1)}, bf16[2,128,512]{2,1,0:T(8,128)(2,1)S(1)}, u32[]{:S(2)}, u32[]{:S(2)}) %collective-permute-start.3) | collective-permute-done | bytes 262176 | tf_op jit(solution)/shard_map/ppermute | solution.py:191
  16.9 0.0 collective-permute-start.4
  16.9 2.5 %collective-permute-done.5.refs_4_ = bf16[2,128,512]{2,1,0:T(8,128)(2,1)S(1)} collective-permute-done((bf16[2,128,512]{2,1,0:T(8,128)(2,1)S(1)}, bf16[2,128,512]{2,1,0:T(8,128)(2,1)S(1)}, u32[]{:S(2)}, u32[]{:S(2)}) %collective-permute-start.5) | collective-permute-done | bytes 262176 | tf_op jit(solution)/shard_map/ppermute | solution.py:191
  20.7 0.0 copy-start
  20.7 0.7 %copy-done = f32[1,512]{1,0:T(1,128)S(1)} copy-done((f32[1,512]{1,0:T(1,128)S(1)}, f32[1,512]{1,0:T(1,128)}, u32[]{:S(2)}) %copy-start) | copy-done | bytes 2072
  21.4 1.8 %shard_map.68 = (bf16[8,512,256]{2,1,0:T(8,128)(2,1)S(1)}, bf16[2,512,256]{2,1,0:T(8,128)(2,1)S(1)}, f32[512,128]{1,0:T(8,128)S(1)}) custom-call(bf16[2,512,1024]{2,1,0:T(8,128)(2,1)} %bitcast.7, f32[1,512]{1,0:T(1,128)S(1)} %copy-done), custom_call_target="tpu_custom_call" | custom-call | bytes 2097152 | tf_op jit(solution)/shard_map/pallas_call | solution.py:217
  23.2 0.0 collective-permute-done.2.refs_1_
  23.2 1.0 %shard_map.71 = f32[2,512,256]{2,1,0:T(8,128)S(1)} custom-call(s32[1]{0:T(128)S(6)} %copy.8.m_ref, s32[1]{0:T(128)S(6)} %copy.9.mask_ref, bf16[8,512,256]{2,1,0:T(8,128)(2,1)S(1)} %get-tuple-element.17.left_ref, bf16[2,128,512]{2,1,0:T(8,128)(2,1)S(1)} %get-tuple-element.20.refs_0_, bf16[2,128,512]{2,1,0:T(8,128)(2,1)S(1)} %collective-permute-done.2.refs_1_, ...), custom_call_target="tpu_custom_call" | custom-call | flops 805306368 | bytes 3670016 | tf_op jit(solution)/shard_map/pallas_call | solution.py:217
  24.2 0.6 %collective-permute-start.7 = (f32[2,512,256]{2,1,0:T(8,128)S(1)}, f32[2,512,256]{2,1,0:T(8,128)S(1)}, u32[]{:S(2)}, u32[]{:S(2)}) collective-permute-start(f32[2,512,256]{2,1,0:T(8,128)S(1)} %shard_map.71), channel_id=1, source_target_pairs={{0,1},{1,0},{2,3},{3,2},{4,5},{5,4},{6,7},{7,6},{8,9},{9,8},{10,11... | collective-permute-start | bytes 3145736 | tf_op jit(solution)/shard_map/ppermute | solution.py:197
  24.8 0.1 collective-permute-start
  24.9 0.4 collective-permute-start.1
  25.3 2.5 %collective-permute-start.8 = (bf16[2,128,256]{2,1,0:T(8,128)(2,1)S(1)}, bf16[2,128,256]{2,1,0:T(8,128)(2,1)S(1)}, u32[]{:S(2)}, u32[]{:S(2)}) collective-permute-start(bf16[2,128,256]{2,1,0:T(8,128)(2,1)S(1)} %get-tuple-element.23), channel_id=1, source_target_pairs={{0,12},{4,8},{8,4},{12,0},{1,13},{5,9},{9,5},{13,1},{2,14},{6,10},... | collective-permute-start | bytes 393224 | tf_op jit(solution)/shard_map/ppermute | solution.py:191
  27.8 0.8 %collective-permute-start.9 = (bf16[2,128,256]{2,1,0:T(8,128)(2,1)S(1)}, bf16[2,128,256]{2,1,0:T(8,128)(2,1)S(1)}, u32[]{:S(2)}, u32[]{:S(2)}) collective-permute-start(bf16[2,128,256]{2,1,0:T(8,128)(2,1)S(1)} %get-tuple-element.26), channel_id=1, source_target_pairs={{0,13},{1,12},{4,9},{5,8},{8,5},{9,4},{12,1},{13,0},{2,15},{3,14},... | collective-permute-start | bytes 393224 | tf_op jit(solution)/shard_map/ppermute | solution.py:197
  28.6 1.0 %shard_map.70.mine_ref = f32[2,512,256]{2,1,0:T(8,128)S(1)} custom-call(s32[1]{0:T(128)S(6)} %copy.8.m_ref, s32[1]{0:T(128)S(6)} %copy.9.mask_ref, bf16[8,512,256]{2,1,0:T(8,128)(2,1)S(1)} %get-tuple-element.17.left_ref, bf16[2,128,512]{2,1,0:T(8,128)(2,1)S(1)} %get-tuple-element.20.refs_0_, bf16[2,128,512]{2,1,0:T(8,128)(2,1)S(1)} %collective-permute-done.2.refs_1_, ...), custom_call_target="tpu_custom_call" | custom-call | flops 805306368 | bytes 3670016 | tf_op jit(solution)/shard_map/pallas_call | solution.py:217
  29.5 3.2 %collective-permute-done.8.block_ref = bf16[2,128,256]{2,1,0:T(8,128)(2,1)S(1)} collective-permute-done((bf16[2,128,256]{2,1,0:T(8,128)(2,1)S(1)}, bf16[2,128,256]{2,1,0:T(8,128)(2,1)S(1)}, u32[]{:S(2)}, u32[]{:S(2)}) %collective-permute-start.8) | collective-permute-done | bytes 131104 | tf_op jit(solution)/shard_map/ppermute | solution.py:191
  32.8 0.5 shard_map.72
  33.2 2.2 %collective-permute-done.9.block_ref = bf16[2,128,256]{2,1,0:T(8,128)(2,1)S(1)} collective-permute-done((bf16[2,128,256]{2,1,0:T(8,128)(2,1)S(1)}, bf16[2,128,256]{2,1,0:T(8,128)(2,1)S(1)}, u32[]{:S(2)}, u32[]{:S(2)}) %collective-permute-start.9) | collective-permute-done | bytes 131104 | tf_op jit(solution)/shard_map/ppermute | solution.py:197
  35.4 0.6 %shard_map.73 = (f32[2,512,256]{2,1,0:T(8,128)S(1)}, f32[2,512,256]{2,1,0:T(8,128)S(1)}, f32[8,128]{1,0:T(8,128)S(1)}) custom-call(s32[1]{0:T(128)S(6)} %copy.8.m_ref, s32[1]{0:T(128)S(6)} %copy.9.mask_ref, bf16[8,512,256]{2,1,0:T(8,128)(2,1)S(1)} %get-tuple-element.17.left_ref, bf16[2,512,256]{2,1,0:T(8,128)(2,1)S(1)} %collective-permute-done.share_ref, ...), custom_call_target="tpu_custom_call" | custom-call | flops 268435456 | bytes 2621440 | tf_op jit(solution)/shard_map/pallas_call | solution.py:217
  36.1 0.1 collective-permute-start.14
  36.2 0.5 collective-permute-start.10
  36.6 2.2 %collective-permute-done.10 = f32[8,128]{1,0:T(8,128)S(1)} collective-permute-done((f32[8,128]{1,0:T(8,128)S(1)}, f32[8,128]{1,0:T(8,128)S(1)}, u32[]{:S(2)}, u32[]{:S(2)}) %collective-permute-start.10) | collective-permute-done | bytes 4128 | tf_op jit(solution)/shard_map/ppermute | solution.py:197
  38.8 1.2 %collective-permute-start.11 = (f32[8,128]{1,0:T(8,128)S(1)}, f32[8,128]{1,0:T(8,128)S(1)}, u32[]{:S(2)}, u32[]{:S(2)}) collective-permute-start(f32[8,128]{1,0:T(8,128)S(1)} %add.12), channel_id=1, source_target_pairs={{0,3},{1,2},{2,1},{3,0},{4,7},{5,6},{6,5},{7,4},{8,11},{9,10},{10,... | collective-permute-start | bytes 12296 | tf_op jit(solution)/shard_map/ppermute | solution.py:197
  40.0 1.8 %collective-permute-done.11 = f32[8,128]{1,0:T(8,128)S(1)} collective-permute-done((f32[8,128]{1,0:T(8,128)S(1)}, f32[8,128]{1,0:T(8,128)S(1)}, u32[]{:S(2)}, u32[]{:S(2)}) %collective-permute-start.11) | collective-permute-done | bytes 4128 | tf_op jit(solution)/shard_map/ppermute | solution.py:197
  41.8 2.0 %collective-permute-start.12 = (f32[8,128]{1,0:T(8,128)S(1)}, f32[8,128]{1,0:T(8,128)S(1)}, u32[]{:S(2)}, u32[]{:S(2)}) collective-permute-start(f32[8,128]{1,0:T(8,128)S(1)} %add.13), channel_id=1, source_target_pairs={{0,13},{1,12},{4,9},{5,8},{8,5},{9,4},{12,1},{13,0},{2,15},{3,14},... | collective-permute-start | bytes 12296 | tf_op jit(solution)/shard_map/ppermute | solution.py:197
  43.8 2.9 %collective-permute-done.12 = f32[8,128]{1,0:T(8,128)S(1)} collective-permute-done((f32[8,128]{1,0:T(8,128)S(1)}, f32[8,128]{1,0:T(8,128)S(1)}, u32[]{:S(2)}, u32[]{:S(2)}) %collective-permute-start.12) | collective-permute-done | bytes 4128 | tf_op jit(solution)/shard_map/ppermute | solution.py:197
  46.7 1.9 %collective-permute-start.13 = (f32[8,128]{1,0:T(8,128)S(1)}, f32[8,128]{1,0:T(8,128)S(1)}, u32[]{:S(2)}, u32[]{:S(2)}) collective-permute-start(f32[8,128]{1,0:T(8,128)S(1)} %add.14), channel_id=1, source_target_pairs={{0,5},{1,4},{4,1},{5,0},{8,13},{9,12},{12,9},{13,8},{2,7},{3,6},{6... | collective-permute-start | bytes 12296 | tf_op jit(solution)/shard_map/ppermute | solution.py:197
  48.5 1.3 %collective-permute-done.13 = f32[8,128]{1,0:T(8,128)S(1)} collective-permute-done((f32[8,128]{1,0:T(8,128)S(1)}, f32[8,128]{1,0:T(8,128)S(1)}, u32[]{:S(2)}, u32[]{:S(2)}) %collective-permute-start.13) | collective-permute-done | bytes 4128 | tf_op jit(solution)/shard_map/ppermute | solution.py:197
  49.9 1.2 %shard_map.74 = (bf16[2,512,512]{2,1,0:T(8,128)(2,1)}, f32[1,128]{1,0:T(1,128)}) custom-call(s32[1]{0:T(128)S(6)} %copy.9.mask_ref, f32[8,128]{1,0:T(8,128)S(1)} %add.15.total_ref, f32[2,512,256]{2,1,0:T(8,128)S(1)} %get-tuple-element.28.near_ref, f32[2,512,256]{2,1,0:T(8,128)S(1)} %collective-permute-done.14.got_ref), custom_call_target="tpu_custom_call" | custom-call | bytes 2097152 | tf_op jit(solution)/shard_map/pallas_call | solution.py:217
  (11 shorter events, 0.0 us)
Async XLA Ops:
  1.9 14.9 %collective-permute-start.3 = (bf16[2,128,512]{2,1,0:T(8,128)(2,1)S(1)}, bf16[2,128,512]{2,1,0:T(8,128)(2,1)S(1)}, u32[]{:S(2)}, u32[]{:S(2)}) collective-permute-start(bf16[2,128,512]{2,1,0:T(8,128)(2,1)S(1)} %get-tuple-element.21), channel_id=1, source_target_pairs={{0,4},{4,0},{8,12},{12,8},{1,5},{5,1},{9,13},{13,9},{2,6},{6,2},{1... | collective-permute-start | bytes 786440 | tf_op jit(solution)/shard_map/ppermute | solution.py:191
  5.1 14.3 %collective-permute-start.5 = (bf16[2,128,512]{2,1,0:T(8,128)(2,1)S(1)}, bf16[2,128,512]{2,1,0:T(8,128)(2,1)S(1)}, u32[]{:S(2)}, u32[]{:S(2)}) collective-permute-start(bf16[2,128,512]{2,1,0:T(8,128)(2,1)S(1)} %get-tuple-element.22), channel_id=1, source_target_pairs={{0,8},{4,12},{8,0},{12,4},{1,9},{5,13},{9,1},{13,5},{2,10},{6,14},... | collective-permute-start | bytes 786440 | tf_op jit(solution)/shard_map/ppermute | solution.py:191
  7.6 15.6 %collective-permute-start.2 = (bf16[2,128,512]{2,1,0:T(8,128)(2,1)S(1)}, bf16[2,128,512]{2,1,0:T(8,128)(2,1)S(1)}, u32[]{:S(2)}, u32[]{:S(2)}) collective-permute-start(bf16[2,128,512]{2,1,0:T(8,128)(2,1)S(1)} %get-tuple-element.20.refs_0_), channel_id=1, source_target_pairs={{0,1},{1,0},{2,3},{3,2},{4,5},{5,4},{6,7},{7,6},{8,9},{9,8},{10,11... | collective-permute-start | bytes 786440 | tf_op jit(solution)/shard_map/ppermute | solution.py:197
  16.9 6.4 %collective-permute-start.4 = (bf16[2,128,512]{2,1,0:T(8,128)(2,1)S(1)}, bf16[2,128,512]{2,1,0:T(8,128)(2,1)S(1)}, u32[]{:S(2)}, u32[]{:S(2)}) collective-permute-start(bf16[2,128,512]{2,1,0:T(8,128)(2,1)S(1)} %collective-permute-done.3.refs_2_), channel_id=1, source_target_pairs={{0,1},{1,0},{2,3},{3,2},{4,5},{5,4},{6,7},{7,6},{8,9},{9,8},{10,11... | collective-permute-start | bytes 786440 | tf_op jit(solution)/shard_map/ppermute | solution.py:197
  19.4 3.9 %collective-permute-start.6 = (bf16[2,128,512]{2,1,0:T(8,128)(2,1)S(1)}, bf16[2,128,512]{2,1,0:T(8,128)(2,1)S(1)}, u32[]{:S(2)}, u32[]{:S(2)}) collective-permute-start(bf16[2,128,512]{2,1,0:T(8,128)(2,1)S(1)} %collective-permute-done.5.refs_4_), channel_id=1, source_target_pairs={{0,1},{1,0},{2,3},{3,2},{4,5},{5,4},{6,7},{7,6},{8,9},{9,8},{10,11... | collective-permute-start | bytes 786440 | tf_op jit(solution)/shard_map/ppermute | solution.py:197
  20.7 0.7 %copy-start = (f32[1,512]{1,0:T(1,128)S(1)}, f32[1,512]{1,0:T(1,128)}, u32[]{:S(2)}) copy-start(f32[1,512]{1,0:T(1,128)} %noise_ref.1) | copy-start | bytes 6148
  24.2 8.5 %collective-permute-start.7 = (f32[2,512,256]{2,1,0:T(8,128)S(1)}, f32[2,512,256]{2,1,0:T(8,128)S(1)}, u32[]{:S(2)}, u32[]{:S(2)}) collective-permute-start(f32[2,512,256]{2,1,0:T(8,128)S(1)} %shard_map.71), channel_id=1, source_target_pairs={{0,1},{1,0},{2,3},{3,2},{4,5},{5,4},{6,7},{7,6},{8,9},{9,8},{10,11... | collective-permute-start | bytes 3145736 | tf_op jit(solution)/shard_map/ppermute | solution.py:197
  24.8 8.0 %collective-permute-start = (bf16[2,512,256]{2,1,0:T(8,128)(2,1)S(1)}, bf16[2,512,256]{2,1,0:T(8,128)(2,1)S(1)}, u32[]{:S(2)}, u32[]{:S(2)}) collective-permute-start(bf16[2,512,256]{2,1,0:T(8,128)(2,1)S(1)} %get-tuple-element.18), channel_id=1, source_target_pairs={{0,1},{1,0},{2,3},{3,2},{4,5},{5,4},{6,7},{7,6},{8,9},{9,8},{10,11... | collective-permute-start | bytes 1572872 | tf_op jit(solution)/shard_map/ppermute | solution.py:197
  24.9 10.6 %collective-permute-start.1 = (f32[512,128]{1,0:T(8,128)S(1)}, f32[512,128]{1,0:T(8,128)S(1)}, u32[]{:S(2)}, u32[]{:S(2)}) collective-permute-start(f32[512,128]{1,0:T(8,128)S(1)} %get-tuple-element.19.weight_ref), channel_id=1, source_target_pairs={{0,1},{1,0},{2,3},{3,2},{4,5},{5,4},{6,7},{7,6},{8,9},{9,8},{10,11... | collective-permute-start | bytes 786440 | tf_op jit(solution)/shard_map/ppermute | solution.py:197
  25.3 7.4 %collective-permute-start.8 = (bf16[2,128,256]{2,1,0:T(8,128)(2,1)S(1)}, bf16[2,128,256]{2,1,0:T(8,128)(2,1)S(1)}, u32[]{:S(2)}, u32[]{:S(2)}) collective-permute-start(bf16[2,128,256]{2,1,0:T(8,128)(2,1)S(1)} %get-tuple-element.23), channel_id=1, source_target_pairs={{0,12},{4,8},{8,4},{12,0},{1,13},{5,9},{9,5},{13,1},{2,14},{6,10},... | collective-permute-start | bytes 393224 | tf_op jit(solution)/shard_map/ppermute | solution.py:191
  27.8 7.6 %collective-permute-start.9 = (bf16[2,128,256]{2,1,0:T(8,128)(2,1)S(1)}, bf16[2,128,256]{2,1,0:T(8,128)(2,1)S(1)}, u32[]{:S(2)}, u32[]{:S(2)}) collective-permute-start(bf16[2,128,256]{2,1,0:T(8,128)(2,1)S(1)} %get-tuple-element.26), channel_id=1, source_target_pairs={{0,13},{1,12},{4,9},{5,8},{8,5},{9,4},{12,1},{13,0},{2,15},{3,14},... | collective-permute-start | bytes 393224 | tf_op jit(solution)/shard_map/ppermute | solution.py:197
  36.1 13.8 %collective-permute-start.14 = (f32[2,512,256]{2,1,0:T(8,128)S(1)}, f32[2,512,256]{2,1,0:T(8,128)S(1)}, u32[]{:S(2)}, u32[]{:S(2)}) collective-permute-start(f32[2,512,256]{2,1,0:T(8,128)S(1)} %get-tuple-element.29), channel_id=1, source_target_pairs={{0,1},{1,0},{2,3},{3,2},{4,5},{5,4},{6,7},{7,6},{8,9},{9,8},{10,11... | collective-permute-start | bytes 3145736 | tf_op jit(solution)/shard_map/ppermute | solution.py:197
  36.2 2.6 %collective-permute-start.10 = (f32[8,128]{1,0:T(8,128)S(1)}, f32[8,128]{1,0:T(8,128)S(1)}, u32[]{:S(2)}, u32[]{:S(2)}) collective-permute-start(f32[8,128]{1,0:T(8,128)S(1)} %get-tuple-element.27), channel_id=1, source_target_pairs={{0,1},{1,0},{2,3},{3,2},{4,5},{5,4},{6,7},{7,6},{8,9},{9,8},{10,11... | collective-permute-start | bytes 12296 | tf_op jit(solution)/shard_map/ppermute | solution.py:197
  38.8 3.0 %collective-permute-start.11 = (f32[8,128]{1,0:T(8,128)S(1)}, f32[8,128]{1,0:T(8,128)S(1)}, u32[]{:S(2)}, u32[]{:S(2)}) collective-permute-start(f32[8,128]{1,0:T(8,128)S(1)} %add.12), channel_id=1, source_target_pairs={{0,3},{1,2},{2,1},{3,0},{4,7},{5,6},{6,5},{7,4},{8,11},{9,10},{10,... | collective-permute-start | bytes 12296 | tf_op jit(solution)/shard_map/ppermute | solution.py:197
  41.8 4.8 %collective-permute-start.12 = (f32[8,128]{1,0:T(8,128)S(1)}, f32[8,128]{1,0:T(8,128)S(1)}, u32[]{:S(2)}, u32[]{:S(2)}) collective-permute-start(f32[8,128]{1,0:T(8,128)S(1)} %add.13), channel_id=1, source_target_pairs={{0,13},{1,12},{4,9},{5,8},{8,5},{9,4},{12,1},{13,0},{2,15},{3,14},... | collective-permute-start | bytes 12296 | tf_op jit(solution)/shard_map/ppermute | solution.py:197
  46.7 3.2 %collective-permute-start.13 = (f32[8,128]{1,0:T(8,128)S(1)}, f32[8,128]{1,0:T(8,128)S(1)}, u32[]{:S(2)}, u32[]{:S(2)}) collective-permute-start(f32[8,128]{1,0:T(8,128)S(1)} %add.14), channel_id=1, source_target_pairs={{0,5},{1,4},{4,1},{5,0},{8,13},{9,12},{12,9},{13,8},{2,7},{3,6},{6... | collective-permute-start | bytes 12296 | tf_op jit(solution)/shard_map/ppermute | solution.py:197

commit v7 on v6

--- a/solution.py
+++ b/solution.py
@@ -1,4 +1,5 @@
 import functools
+import math
 
 import jax
 import jax.numpy as jnp
@@ -197,6 +198,13 @@
     return lax.ppermute(x, names, [(i, i ^ flip) for i in range(size)])
 
 
+def corner_swap(x):
+    names = ("ma", "freq", "pol")
+    sizes = [lax.axis_size(name) for name in names]
+    flip = (sizes[1] + 1) * sizes[2] + 1
+    return lax.ppermute(x, names, [(i, i ^ flip) for i in range(math.prod(sizes))])
+
+
 def on_device(alm, beam, m_table, chan_mask, noise):
     n_ma, n_pol, n_freq = (lax.axis_size(name) for name in ("ma", "pol", "freq"))
     parts, _, ell, _, maps = alm.shape
@@ -293,8 +301,12 @@
         1,
     )
     far = swap(far, "pol", 1)
-    for name, step in (("pol", 1), ("freq", 1), ("ma", 3), ("ma", 1)):
+    for name, step in (("pol", 1), ("ma", 3)):
         total = total + swap(total, name, step)
+    beside = swap(total, "ma", 1)
+    across = swap(total, "freq", 1)
+    corner = corner_swap(total)
+    total = total + beside + across + corner
     scaled, own_power = call(
         functools.partial(finish_kernel, n_freq, n_ma * n_pol * modes * maps),
         (

time: 51.3 us -> 52.1 us (1.016)
  waiting for transfers between devices: 25.3 us -> 26.1 us
    ppermute x0 -> x1, waiting for transfers between devices: none -> 2.13 us  [corner_swap(): lax.ppermute(x, names, [(i, i ^ flip) for i in range(math.prod(sizes))])]
    ppermute x12, waiting for transfers between devices: 10.4 us -> 9.04 us  [swap(): return lax.ppermute(x, names, [(i, i ^ flip) for i in range(size)])]
  transfers between devices with their start and end apart: 15 -> 16, of which waited for: 8 -> 9; matrix products, arithmetic and copies ran while one was open for 0% -> 0% of each run, Pallas kernels for 6% -> 6%
where the time goes in v7:
time: 52.1 us; the launch traced here: 51.9 us
  waiting for transfers between devices  26.1 us (50%)
  starting transfers between devices  15.7 us (30%)
  Pallas kernels  7.4 us (14%)
  between operations  2.02 us (4%)
  local copies, waits for them, and re-layouts  0.68 us (1%)
    ppermute x3, waiting for transfers between devices, straight(): return lax.ppermute(x, name, [(i, i ^ step) for i in range(size)])  15 us
    ppermute x12, waiting for transfers between devices, swap(): return lax.ppermute(x, names, [(i, i ^ flip) for i in range(size)])  9.04 us
    ppermute x3, starting transfers between devices, straight(): return lax.ppermute(x, name, [(i, i ^ step) for i in range(size)])  8.18 us
    ppermute x12, starting transfers between devices, swap(): return lax.ppermute(x, names, [(i, i ^ flip) for i in range(size)])  7.48 us
    pallas_call x7, Pallas kernels, call(): pl.pallas_call(kernel, out_shape=out_shape, in_specs=more.pop('in_specs',...  7.4 us
    ppermute x1, waiting for transfers between devices, corner_swap(): lax.ppermute(x, names, [(i, i ^ flip) for i in range(math.prod(sizes))])  2.13 us
  transfers between devices with their start and end apart: 16, of which 9 were waited for; matrix products, arithmetic and copies ran while one was open for 0% of the time, Pallas kernels for 6%

profile of v7, /device:TPU:0, one launch (start us, length us, event | category | flops | bytes accessed | tf_op | source)
XLA Modules:
  0.0 51.9 jit_solution(17019941804660234889)
XLA Ops:
  0.6 1.3 %shard_map.69 = (bf16[2,128,512]{2,1,0:T(8,128)(2,1)S(1)}, bf16[2,128,512]{2,1,0:T(8,128)(2,1)S(1)}, bf16[2,128,256]{2,1,0:T(8,128)(2,1)S(1)}, bf16[2,128,256]{2,1,0:T(8,128)(2,1)S(1)}, bf16[2,128,512]{2,1,0:T(8,128)(2,1)S(1)}) custom-call(bf16[2,128,4,512]{3,2,1,0:T(4,128)(2,1)} %bitcast.8), custom_call_target="tpu_custom_call" | custom-call | bytes 2097152 | tf_op jit(solution)/shard_map/pallas_call | solution.py:225
  1.9 3.1 %collective-permute-start.3 = (bf16[2,128,512]{2,1,0:T(8,128)(2,1)S(1)}, bf16[2,128,512]{2,1,0:T(8,128)(2,1)S(1)}, u32[]{:S(2)}, u32[]{:S(2)}) collective-permute-start(bf16[2,128,512]{2,1,0:T(8,128)(2,1)S(1)} %get-tuple-element.21), channel_id=1, source_target_pairs={{0,4},{4,0},{8,12},{12,8},{1,5},{5,1},{9,13},{13,9},{2,6},{6,2},{1... | collective-permute-start | bytes 786440 | tf_op jit(solution)/shard_map/ppermute | solution.py:192
  5.1 2.6 %collective-permute-start.5 = (bf16[2,128,512]{2,1,0:T(8,128)(2,1)S(1)}, bf16[2,128,512]{2,1,0:T(8,128)(2,1)S(1)}, u32[]{:S(2)}, u32[]{:S(2)}) collective-permute-start(bf16[2,128,512]{2,1,0:T(8,128)(2,1)S(1)} %get-tuple-element.22), channel_id=1, source_target_pairs={{0,8},{4,12},{8,0},{12,4},{1,9},{5,13},{9,1},{13,5},{2,10},{6,14},... | collective-permute-start | bytes 786440 | tf_op jit(solution)/shard_map/ppermute | solution.py:192
  7.6 0.0 collective-permute-start.2
  7.6 9.2 %collective-permute-done.3.refs_2_ = bf16[2,128,512]{2,1,0:T(8,128)(2,1)S(1)} collective-permute-done((bf16[2,128,512]{2,1,0:T(8,128)(2,1)S(1)}, bf16[2,128,512]{2,1,0:T(8,128)(2,1)S(1)}, u32[]{:S(2)}, u32[]{:S(2)}) %collective-permute-start.3) | collective-permute-done | bytes 262176 | tf_op jit(solution)/shard_map/ppermute | solution.py:192
  16.9 0.0 collective-permute-start.4
  16.9 2.5 %collective-permute-done.5.refs_4_ = bf16[2,128,512]{2,1,0:T(8,128)(2,1)S(1)} collective-permute-done((bf16[2,128,512]{2,1,0:T(8,128)(2,1)S(1)}, bf16[2,128,512]{2,1,0:T(8,128)(2,1)S(1)}, u32[]{:S(2)}, u32[]{:S(2)}) %collective-permute-start.5) | collective-permute-done | bytes 262176 | tf_op jit(solution)/shard_map/ppermute | solution.py:192
  20.7 0.0 copy-start
  20.7 0.7 %copy-done = f32[1,512]{1,0:T(1,128)S(1)} copy-done((f32[1,512]{1,0:T(1,128)S(1)}, f32[1,512]{1,0:T(1,128)}, u32[]{:S(2)}) %copy-start) | copy-done | bytes 2072
  21.4 1.8 %shard_map.68 = (bf16[8,512,256]{2,1,0:T(8,128)(2,1)S(1)}, bf16[2,512,256]{2,1,0:T(8,128)(2,1)S(1)}, f32[512,128]{1,0:T(8,128)S(1)}) custom-call(bf16[2,512,1024]{2,1,0:T(8,128)(2,1)} %bitcast.7, f32[1,512]{1,0:T(1,128)S(1)} %copy-done), custom_call_target="tpu_custom_call" | custom-call | bytes 2097152 | tf_op jit(solution)/shard_map/pallas_call | solution.py:225
  23.2 1.0 %shard_map.71 = f32[2,512,256]{2,1,0:T(8,128)S(1)} custom-call(s32[1]{0:T(128)S(6)} %copy.8.m_ref, s32[1]{0:T(128)S(6)} %copy.9.mask_ref, bf16[8,512,256]{2,1,0:T(8,128)(2,1)S(1)} %get-tuple-element.17.left_ref, bf16[2,128,512]{2,1,0:T(8,128)(2,1)S(1)} %get-tuple-element.20.refs_0_, bf16[2,128,512]{2,1,0:T(8,128)(2,1)S(1)} %collective-permute-done.2.refs_1_, ...), custom_call_target="tpu_custom_call" | custom-call | flops 805306368 | bytes 3670016 | tf_op jit(solution)/shard_map/pallas_call | solution.py:225
  24.2 0.6 %collective-permute-start.7 = (f32[2,512,256]{2,1,0:T(8,128)S(1)}, f32[2,512,256]{2,1,0:T(8,128)S(1)}, u32[]{:S(2)}, u32[]{:S(2)}) collective-permute-start(f32[2,512,256]{2,1,0:T(8,128)S(1)} %shard_map.71), channel_id=1, source_target_pairs={{0,1},{1,0},{2,3},{3,2},{4,5},{5,4},{6,7},{7,6},{8,9},{9,8},{10,11... | collective-permute-start | bytes 3145736 | tf_op jit(solution)/shard_map/ppermute | solution.py:198
  24.8 0.1 collective-permute-start
  24.9 0.4 collective-permute-start.1
  25.3 2.5 %collective-permute-start.8 = (bf16[2,128,256]{2,1,0:T(8,128)(2,1)S(1)}, bf16[2,128,256]{2,1,0:T(8,128)(2,1)S(1)}, u32[]{:S(2)}, u32[]{:S(2)}) collective-permute-start(bf16[2,128,256]{2,1,0:T(8,128)(2,1)S(1)} %get-tuple-element.23), channel_id=1, source_target_pairs={{0,12},{4,8},{8,4},{12,0},{1,13},{5,9},{9,5},{13,1},{2,14},{6,10},... | collective-permute-start | bytes 393224 | tf_op jit(solution)/shard_map/ppermute | solution.py:192
  27.8 0.8 %collective-permute-start.9 = (bf16[2,128,256]{2,1,0:T(8,128)(2,1)S(1)}, bf16[2,128,256]{2,1,0:T(8,128)(2,1)S(1)}, u32[]{:S(2)}, u32[]{:S(2)}) collective-permute-start(bf16[2,128,256]{2,1,0:T(8,128)(2,1)S(1)} %get-tuple-element.26), channel_id=1, source_target_pairs={{0,13},{1,12},{4,9},{5,8},{8,5},{9,4},{12,1},{13,0},{2,15},{3,14},... | collective-permute-start | bytes 393224 | tf_op jit(solution)/shard_map/ppermute | solution.py:198
  28.6 1.0 %shard_map.70.mine_ref = f32[2,512,256]{2,1,0:T(8,128)S(1)} custom-call(s32[1]{0:T(128)S(6)} %copy.8.m_ref, s32[1]{0:T(128)S(6)} %copy.9.mask_ref, bf16[8,512,256]{2,1,0:T(8,128)(2,1)S(1)} %get-tuple-element.17.left_ref, bf16[2,128,512]{2,1,0:T(8,128)(2,1)S(1)} %get-tuple-element.20.refs_0_, bf16[2,128,512]{2,1,0:T(8,128)(2,1)S(1)} %collective-permute-done.2.refs_1_, ...), custom_call_target="tpu_custom_call" | custom-call | flops 805306368 | bytes 3670016 | tf_op jit(solution)/shard_map/pallas_call | solution.py:225
  29.5 3.2 %collective-permute-done.8.block_ref = bf16[2,128,256]{2,1,0:T(8,128)(2,1)S(1)} collective-permute-done((bf16[2,128,256]{2,1,0:T(8,128)(2,1)S(1)}, bf16[2,128,256]{2,1,0:T(8,128)(2,1)S(1)}, u32[]{:S(2)}, u32[]{:S(2)}) %collective-permute-start.8) | collective-permute-done | bytes 131104 | tf_op jit(solution)/shard_map/ppermute | solution.py:192
  32.8 0.5 shard_map.72
  33.2 2.2 %collective-permute-done.9.block_ref = bf16[2,128,256]{2,1,0:T(8,128)(2,1)S(1)} collective-permute-done((bf16[2,128,256]{2,1,0:T(8,128)(2,1)S(1)}, bf16[2,128,256]{2,1,0:T(8,128)(2,1)S(1)}, u32[]{:S(2)}, u32[]{:S(2)}) %collective-permute-start.9) | collective-permute-done | bytes 131104 | tf_op jit(solution)/shard_map/ppermute | solution.py:198
  35.4 0.6 %shard_map.73 = (f32[2,512,256]{2,1,0:T(8,128)S(1)}, f32[2,512,256]{2,1,0:T(8,128)S(1)}, f32[8,128]{1,0:T(8,128)S(1)}) custom-call(s32[1]{0:T(128)S(6)} %copy.8.m_ref, s32[1]{0:T(128)S(6)} %copy.9.mask_ref, bf16[8,512,256]{2,1,0:T(8,128)(2,1)S(1)} %get-tuple-element.17.left_ref, bf16[2,512,256]{2,1,0:T(8,128)(2,1)S(1)} %collective-permute-done.share_ref, ...), custom_call_target="tpu_custom_call" | custom-call | flops 268435456 | bytes 2621440 | tf_op jit(solution)/shard_map/pallas_call | solution.py:225
  36.1 0.1 collective-permute-start.15
  36.2 0.5 collective-permute-start.10
  36.6 2.2 %collective-permute-done.10 = f32[8,128]{1,0:T(8,128)S(1)} collective-permute-done((f32[8,128]{1,0:T(8,128)S(1)}, f32[8,128]{1,0:T(8,128)S(1)}, u32[]{:S(2)}, u32[]{:S(2)}) %collective-permute-start.10) | collective-permute-done | bytes 4128 | tf_op jit(solution)/shard_map/ppermute | solution.py:198
  38.8 2.0 %collective-permute-start.11 = (f32[8,128]{1,0:T(8,128)S(1)}, f32[8,128]{1,0:T(8,128)S(1)}, u32[]{:S(2)}, u32[]{:S(2)}) collective-permute-start(f32[8,128]{1,0:T(8,128)S(1)} %add.15), channel_id=1, source_target_pairs={{0,13},{1,12},{4,9},{5,8},{8,5},{9,4},{12,1},{13,0},{2,15},{3,14},... | collective-permute-start | bytes 12296 | tf_op jit(solution)/shard_map/ppermute | solution.py:198
  40.8 2.9 %collective-permute-done.11 = f32[8,128]{1,0:T(8,128)S(1)} collective-permute-done((f32[8,128]{1,0:T(8,128)S(1)}, f32[8,128]{1,0:T(8,128)S(1)}, u32[]{:S(2)}, u32[]{:S(2)}) %collective-permute-start.11) | collective-permute-done | bytes 4128 | tf_op jit(solution)/shard_map/ppermute | solution.py:198
  43.6 1.9 %collective-permute-start.12 = (f32[8,128]{1,0:T(8,128)S(1)}, f32[8,128]{1,0:T(8,128)S(1)}, u32[]{:S(2)}, u32[]{:S(2)}) collective-permute-start(f32[8,128]{1,0:T(8,128)S(1)} %add.16), channel_id=1, source_target_pairs={{0,5},{1,4},{4,1},{5,0},{8,13},{9,12},{12,9},{13,8},{2,7},{3,6},{6... | collective-permute-start | bytes 12296 | tf_op jit(solution)/shard_map/ppermute | solution.py:198
  45.5 1.2 %collective-permute-start.13 = (f32[8,128]{1,0:T(8,128)S(1)}, f32[8,128]{1,0:T(8,128)S(1)}, u32[]{:S(2)}, u32[]{:S(2)}) collective-permute-start(f32[8,128]{1,0:T(8,128)S(1)} %add.16), channel_id=1, source_target_pairs={{0,3},{1,2},{2,1},{3,0},{4,7},{5,6},{6,5},{7,4},{8,11},{9,10},{10,... | collective-permute-start | bytes 12296 | tf_op jit(solution)/shard_map/ppermute | solution.py:198
  46.7 0.1 collective-permute-done.12
  46.8 1.7 %collective-permute-done.13 = f32[8,128]{1,0:T(8,128)S(1)} collective-permute-done((f32[8,128]{1,0:T(8,128)S(1)}, f32[8,128]{1,0:T(8,128)S(1)}, u32[]{:S(2)}, u32[]{:S(2)}) %collective-permute-start.13) | collective-permute-done | bytes 4128 | tf_op jit(solution)/shard_map/ppermute | solution.py:198
  48.5 2.1 %collective-permute-done.14 = f32[8,128]{1,0:T(8,128)S(1)} collective-permute-done((f32[8,128]{1,0:T(8,128)S(1)}, f32[8,128]{1,0:T(8,128)S(1)}, u32[]{:S(2)}, u32[]{:S(2)}) %collective-permute-start.14) | collective-permute-done | bytes 4128 | tf_op jit(solution)/shard_map/ppermute | solution.py:205
  50.7 1.2 %shard_map.74 = (bf16[2,512,512]{2,1,0:T(8,128)(2,1)}, f32[1,128]{1,0:T(1,128)}) custom-call(s32[1]{0:T(128)S(6)} %copy.9.mask_ref, f32[8,128]{1,0:T(8,128)S(1)} %add_add_fusion.total_ref, f32[2,512,256]{2,1,0:T(8,128)S(1)} %get-tuple-element.28.near_ref, f32[2,512,256]{2,1,0:T(8,128)S(1)} %collective-permute-done.15.got_ref), custom_call_target="tpu_custom_call" | custom-call | bytes 2097152 | tf_op jit(solution)/shard_map/pallas_call | solution.py:225
  (12 shorter events, 0.0 us)
Async XLA Ops:
  1.9 14.9 %collective-permute-start.3 = (bf16[2,128,512]{2,1,0:T(8,128)(2,1)S(1)}, bf16[2,128,512]{2,1,0:T(8,128)(2,1)S(1)}, u32[]{:S(2)}, u32[]{:S(2)}) collective-permute-start(bf16[2,128,512]{2,1,0:T(8,128)(2,1)S(1)} %get-tuple-element.21), channel_id=1, source_target_pairs={{0,4},{4,0},{8,12},{12,8},{1,5},{5,1},{9,13},{13,9},{2,6},{6,2},{1... | collective-permute-start | bytes 786440 | tf_op jit(solution)/shard_map/ppermute | solution.py:192
  5.1 14.3 %collective-permute-start.5 = (bf16[2,128,512]{2,1,0:T(8,128)(2,1)S(1)}, bf16[2,128,512]{2,1,0:T(8,128)(2,1)S(1)}, u32[]{:S(2)}, u32[]{:S(2)}) collective-permute-start(bf16[2,128,512]{2,1,0:T(8,128)(2,1)S(1)} %get-tuple-element.22), channel_id=1, source_target_pairs={{0,8},{4,12},{8,0},{12,4},{1,9},{5,13},{9,1},{13,5},{2,10},{6,14},... | collective-permute-start | bytes 786440 | tf_op jit(solution)/shard_map/ppermute | solution.py:192
  7.6 15.6 %collective-permute-start.2 = (bf16[2,128,512]{2,1,0:T(8,128)(2,1)S(1)}, bf16[2,128,512]{2,1,0:T(8,128)(2,1)S(1)}, u32[]{:S(2)}, u32[]{:S(2)}) collective-permute-start(bf16[2,128,512]{2,1,0:T(8,128)(2,1)S(1)} %get-tuple-element.20.refs_0_), channel_id=1, source_target_pairs={{0,1},{1,0},{2,3},{3,2},{4,5},{5,4},{6,7},{7,6},{8,9},{9,8},{10,11... | collective-permute-start | bytes 786440 | tf_op jit(solution)/shard_map/ppermute | solution.py:198
  16.9 6.4 %collective-permute-start.4 = (bf16[2,128,512]{2,1,0:T(8,128)(2,1)S(1)}, bf16[2,128,512]{2,1,0:T(8,128)(2,1)S(1)}, u32[]{:S(2)}, u32[]{:S(2)}) collective-permute-start(bf16[2,128,512]{2,1,0:T(8,128)(2,1)S(1)} %collective-permute-done.3.refs_2_), channel_id=1, source_target_pairs={{0,1},{1,0},{2,3},{3,2},{4,5},{5,4},{6,7},{7,6},{8,9},{9,8},{10,11... | collective-permute-start | bytes 786440 | tf_op jit(solution)/shard_map/ppermute | solution.py:198
  19.4 3.9 %collective-permute-start.6 = (bf16[2,128,512]{2,1,0:T(8,128)(2,1)S(1)}, bf16[2,128,512]{2,1,0:T(8,128)(2,1)S(1)}, u32[]{:S(2)}, u32[]{:S(2)}) collective-permute-start(bf16[2,128,512]{2,1,0:T(8,128)(2,1)S(1)} %collective-permute-done.5.refs_4_), channel_id=1, source_target_pairs={{0,1},{1,0},{2,3},{3,2},{4,5},{5,4},{6,7},{7,6},{8,9},{9,8},{10,11... | collective-permute-start | bytes 786440 | tf_op jit(solution)/shard_map/ppermute | solution.py:198
  20.7 0.7 %copy-start = (f32[1,512]{1,0:T(1,128)S(1)}, f32[1,512]{1,0:T(1,128)}, u32[]{:S(2)}) copy-start(f32[1,512]{1,0:T(1,128)} %noise_ref.1) | copy-start | bytes 6148
  24.2 8.5 %collective-permute-start.7 = (f32[2,512,256]{2,1,0:T(8,128)S(1)}, f32[2,512,256]{2,1,0:T(8,128)S(1)}, u32[]{:S(2)}, u32[]{:S(2)}) collective-permute-start(f32[2,512,256]{2,1,0:T(8,128)S(1)} %shard_map.71), channel_id=1, source_target_pairs={{0,1},{1,0},{2,3},{3,2},{4,5},{5,4},{6,7},{7,6},{8,9},{9,8},{10,11... | collective-permute-start | bytes 3145736 | tf_op jit(solution)/shard_map/ppermute | solution.py:198
  24.8 8.0 %collective-permute-start = (bf16[2,512,256]{2,1,0:T(8,128)(2,1)S(1)}, bf16[2,512,256]{2,1,0:T(8,128)(2,1)S(1)}, u32[]{:S(2)}, u32[]{:S(2)}) collective-permute-start(bf16[2,512,256]{2,1,0:T(8,128)(2,1)S(1)} %get-tuple-element.18), channel_id=1, source_target_pairs={{0,1},{1,0},{2,3},{3,2},{4,5},{5,4},{6,7},{7,6},{8,9},{9,8},{10,11... | collective-permute-start | bytes 1572872 | tf_op jit(solution)/shard_map/ppermute | solution.py:198
  24.9 10.6 %collective-permute-start.1 = (f32[512,128]{1,0:T(8,128)S(1)}, f32[512,128]{1,0:T(8,128)S(1)}, u32[]{:S(2)}, u32[]{:S(2)}) collective-permute-start(f32[512,128]{1,0:T(8,128)S(1)} %get-tuple-element.19.weight_ref), channel_id=1, source_target_pairs={{0,1},{1,0},{2,3},{3,2},{4,5},{5,4},{6,7},{7,6},{8,9},{9,8},{10,11... | collective-permute-start | bytes 786440 | tf_op jit(solution)/shard_map/ppermute | solution.py:198
  25.3 7.4 %collective-permute-start.8 = (bf16[2,128,256]{2,1,0:T(8,128)(2,1)S(1)}, bf16[2,128,256]{2,1,0:T(8,128)(2,1)S(1)}, u32[]{:S(2)}, u32[]{:S(2)}) collective-permute-start(bf16[2,128,256]{2,1,0:T(8,128)(2,1)S(1)} %get-tuple-element.23), channel_id=1, source_target_pairs={{0,12},{4,8},{8,4},{12,0},{1,13},{5,9},{9,5},{13,1},{2,14},{6,10},... | collective-permute-start | bytes 393224 | tf_op jit(solution)/shard_map/ppermute | solution.py:192
  27.8 7.6 %collective-permute-start.9 = (bf16[2,128,256]{2,1,0:T(8,128)(2,1)S(1)}, bf16[2,128,256]{2,1,0:T(8,128)(2,1)S(1)}, u32[]{:S(2)}, u32[]{:S(2)}) collective-permute-start(bf16[2,128,256]{2,1,0:T(8,128)(2,1)S(1)} %get-tuple-element.26), channel_id=1, source_target_pairs={{0,13},{1,12},{4,9},{5,8},{8,5},{9,4},{12,1},{13,0},{2,15},{3,14},... | collective-permute-start | bytes 393224 | tf_op jit(solution)/shard_map/ppermute | solution.py:198
  36.1 14.6 %collective-permute-start.15 = (f32[2,512,256]{2,1,0:T(8,128)S(1)}, f32[2,512,256]{2,1,0:T(8,128)S(1)}, u32[]{:S(2)}, u32[]{:S(2)}) collective-permute-start(f32[2,512,256]{2,1,0:T(8,128)S(1)} %get-tuple-element.29), channel_id=1, source_target_pairs={{0,1},{1,0},{2,3},{3,2},{4,5},{5,4},{6,7},{7,6},{8,9},{9,8},{10,11... | collective-permute-start | bytes 3145736 | tf_op jit(solution)/shard_map/ppermute | solution.py:198
  36.2 2.6 %collective-permute-start.10 = (f32[8,128]{1,0:T(8,128)S(1)}, f32[8,128]{1,0:T(8,128)S(1)}, u32[]{:S(2)}, u32[]{:S(2)}) collective-permute-start(f32[8,128]{1,0:T(8,128)S(1)} %get-tuple-element.27), channel_id=1, source_target_pairs={{0,1},{1,0},{2,3},{3,2},{4,5},{5,4},{6,7},{7,6},{8,9},{9,8},{10,11... | collective-permute-start | bytes 12296 | tf_op jit(solution)/shard_map/ppermute | solution.py:198
  38.8 4.8 %collective-permute-start.11 = (f32[8,128]{1,0:T(8,128)S(1)}, f32[8,128]{1,0:T(8,128)S(1)}, u32[]{:S(2)}, u32[]{:S(2)}) collective-permute-start(f32[8,128]{1,0:T(8,128)S(1)} %add.15), channel_id=1, source_target_pairs={{0,13},{1,12},{4,9},{5,8},{8,5},{9,4},{12,1},{13,0},{2,15},{3,14},... | collective-permute-start | bytes 12296 | tf_op jit(solution)/shard_map/ppermute | solution.py:198
  43.6 3.2 %collective-permute-start.12 = (f32[8,128]{1,0:T(8,128)S(1)}, f32[8,128]{1,0:T(8,128)S(1)}, u32[]{:S(2)}, u32[]{:S(2)}) collective-permute-start(f32[8,128]{1,0:T(8,128)S(1)} %add.16), channel_id=1, source_target_pairs={{0,5},{1,4},{4,1},{5,0},{8,13},{9,12},{12,9},{13,8},{2,7},{3,6},{6... | collective-permute-start | bytes 12296 | tf_op jit(solution)/shard_map/ppermute | solution.py:198
  45.5 3.0 %collective-permute-start.13 = (f32[8,128]{1,0:T(8,128)S(1)}, f32[8,128]{1,0:T(8,128)S(1)}, u32[]{:S(2)}, u32[]{:S(2)}) collective-permute-start(f32[8,128]{1,0:T(8,128)S(1)} %add.16), channel_id=1, source_target_pairs={{0,3},{1,2},{2,1},{3,0},{4,7},{5,6},{6,5},{7,4},{8,11},{9,10},{10,... | collective-permute-start | bytes 12296 | tf_op jit(solution)/shard_map/ppermute | solution.py:198
  46.7 3.9 %collective-permute-start.14 = (f32[8,128]{1,0:T(8,128)S(1)}, f32[8,128]{1,0:T(8,128)S(1)}, u32[]{:S(2)}, u32[]{:S(2)}) collective-permute-start(f32[8,128]{1,0:T(8,128)S(1)} %add.16), channel_id=1, source_target_pairs={{0,7},{1,6},{2,5},{3,4},{4,3},{5,2},{6,1},{7,0},{8,15},{9,14},{10,... | collective-permute-start | bytes 12296 | tf_op jit(solution)/shard_map/ppermute | solution.py:205

commit v8 on v7

--- a/solution.py
+++ b/solution.py
@@ -39,11 +39,13 @@
         copy.wait()
         rows = slice(j * size, (j + 1) * size)
         modes_ref[...] = pltpu.einshape("lms->mls", held_ref[c, rows])
-        for ref, (step, other) in zip(slab_refs, pieces, strict=True):
+        for ref, (step, other, start, half) in zip(slab_refs, pieces, strict=True):
+            count = ref.shape[2]
             if other is None:
                 ref[c, rows] = modes_ref[place ^ step]
             else:
-                ref[c, rows] = modes_ref[place ^ step, :, maps_of(pol ^ other, ref.shape[2])]
+                first = pl.multiple_of((pol ^ other) * half + start, 128)
+                ref[c, rows] = modes_ref[place ^ step, :, pl.ds(first, count)]
 
 
 def load_kernel(step, beam_ref, noise_ref, left_ref, share_ref, weight_ref, sems):
@@ -98,12 +100,20 @@
         vis_ref[c] = dot(left, right)
 
 
-def same_kernel(step, m_ref, left_ref, share_ref, mine_ref, got_ref, block_ref, near_ref, far_ref):
+def same_kernel(step, m_ref, left_ref, share_ref, mine_ref, got_ref, block_ref, *refs):
     (block,), *rights = operands(m_ref, [block_ref], [(step, 0)], slice(None))
     shared = share_ref[lax.axis_index("pol")]
-    for c, right in enumerate(rights):
-        near_ref[c] = mine_ref[c] + dot(left_ref[block], right)
-        far_ref[c] = got_ref[c] + dot(shared, right)
+    for before_ref, left, pieces in (
+        (mine_ref, left_ref[block], refs[0::2]),
+        (got_ref, shared, refs[1::2]),
+    ):
+        for c, right in enumerate(rights):
+            vis = before_ref[c] + dot(left, right)
+            start = 0
+            for ref in pieces:
+                end = start + ref.shape[2]
+                ref[c] = vis[:, start:end]
+                start = end
 
 
 def weigh(vis, weight):
@@ -112,35 +122,33 @@
     )
 
 
-def last_kernel(
-    step,
-    slots,
-    m_ref,
-    mask_ref,
-    left_ref,
-    share_ref,
-    weight_ref,
-    other_ref,
-    mine_ref,
-    got_ref,
-    block_ref,
-    near_ref,
-    far_ref,
-    power_ref,
-):
+def whole(step, m_ref, left_ref, share_ref, weight_ref, other_ref, mine_ref, got_ref, block_ref, near_ref, far_ref):
     (block,), *rights = operands(m_ref, [block_ref], [(step, 1)], slice(None))
+    right = jnp.concatenate(rights, axis=1)
+    maps = near_ref.shape[2]
     sums = jnp.zeros(weight_ref.shape, jnp.float32)
     for left, before_ref, weights_ref, ref in (
         (share_ref[lax.axis_index("pol") ^ 1], got_ref, other_ref, far_ref),
         (left_ref[block], mine_ref, weight_ref, near_ref),
     ):
         weight = weights_ref[...]
-        for c, right in enumerate(rights):
-            vis = weigh(before_ref[c] + dot(left, right), weight)
+        terms = dot(left, right)
+        for c in range(len(rights)):
+            vis = weigh(before_ref[c] + terms[:, c * maps : (c + 1) * maps], weight)
             ref[c] = vis
-            for i in range(0, vis.shape[1], 128):
+            for i in range(0, maps, 128):
                 sums += vis[:, i : i + 128] * vis[:, i : i + 128]
-    total = jnp.sum(sums)
+    return jnp.sum(sums)
+
+
+def piece_kernel(step, m_ref, *refs):
+    *rest, power_ref = refs
+    power_ref[...] = jnp.full(power_ref.shape, whole(step, m_ref, *rest))
+
+
+def last_kernel(step, slots, m_ref, mask_ref, early_ref, *refs):
+    *rest, power_ref = refs
+    total = early_ref[...] + whole(step, m_ref, *rest)
     lane = lax.broadcasted_iota(jnp.int32, power_ref.shape, 1)
     leader = (lax.axis_index("ma") == 0) & (lax.axis_index("pol") == 0)
     live = jnp.where(leader, mask_ref[0], 0).astype(jnp.float32)
@@ -150,7 +158,7 @@
     )
 
 
-def finish_kernel(slots, modes, mask_ref, total_ref, near_ref, got_ref, scaled_ref, power_ref, held_ref, own_ref, sems):
+def finish_kernel(slots, modes, mask_ref, total_ref, near_a, got_a, near_b, got_b, scaled_ref, power_ref, held_ref, own_ref, sems):
     lane = lax.broadcasted_iota(jnp.int32, (1, 128), 1)
     totals = total_ref[0:1, :]
     powers = totals / modes
@@ -166,15 +174,21 @@
     own_ref[...] = jnp.where(lane == 0, own, 0.0)
     copies = [pltpu.make_async_copy(own_ref, power_ref, sems.at[0])]
     copies[0].start()
-    parts, rows, count = near_ref.shape
+    _, parts, rows, count = held_ref.shape
     pol = lax.axis_index("pol")
     chunk = rows // 2
     for c in range(parts):
         for j in range(0, rows, chunk):
-            for half, (ref, owner) in enumerate(((near_ref, pol), (got_ref, pol ^ 1))):
-                held_ref[half, c, j : j + chunk] = (ref[c, j : j + chunk] * factor).astype(
-                    scaled_ref.dtype
-                )
+            for half, (pieces, owner) in enumerate(
+                (((near_a, near_b), pol), ((got_a, got_b), pol ^ 1))
+            ):
+                start = 0
+                for ref in pieces:
+                    end = start + ref.shape[2]
+                    held_ref[half, c, j : j + chunk, start:end] = (
+                        ref[c, j : j + chunk] * factor
+                    ).astype(scaled_ref.dtype)
+                    start = end
                 copies.append(
                     pltpu.make_async_copy(
                         held_ref.at[half, c, pl.ds(j, chunk)],
@@ -218,7 +232,7 @@
     def slab(count):
         return jax.ShapeDtypeStruct((parts, ell, count), alm.dtype)
 
-    row = jax.ShapeDtypeStruct((8, 128), jnp.float32)
+    row = jax.ShapeDtypeStruct((1, 128), jnp.float32)
     weights = jax.ShapeDtypeStruct((modes, 128), jnp.float32)
 
     def call(kernel, out_shape, scalars, operands, blocks, **more):
@@ -237,10 +251,19 @@
         )(*scalars, *operands)
 
     half = maps // n_pol
-    pieces = ((2, None), (1, None), (3, 0), (3, 1), (0, None))
-    two, one, same, cross, own = call(
+    early = half // 2 // 128 * 128 or half
+    late = half - early
+    pieces = (
+        (2, None, 0, maps),
+        (1, None, 0, maps),
+        (3, 0, 0, half),
+        (3, 1, 0, half),
+        (3, 1, early, half),
+        (0, None, 0, maps),
+    )
+    two, one, same, cross_a, cross_b, own = call(
         functools.partial(split_kernel, pieces),
-        [slab(maps if other is None else half) for _, other in pieces],
+        [slab(count) for count in (maps, maps, half, early, late, maps)],
         (),
         (pltpu.with_memory_space_constraint(alm[:, 0], pltpu.HBM),),
         0,
@@ -254,7 +277,8 @@
     two = straight(two, "ma", 2)
     one = straight(one, "ma", 1)
     same = straight(same, "ma", 3)
-    cross = swap(cross, "ma", 3)
+    cross_a = swap(cross_a, "ma", 3)
+    cross_b = swap(cross_b, "ma", 3)
     own_far = swap(own, "pol", 1)
     one_far = swap(one, "pol", 1)
     two_far = swap(two, "pol", 1)
@@ -286,21 +310,29 @@
         for other in (1, 0)
     )
     got = swap(give, "pol", 1)
-    mine, got = call(
+    mine_a, got_a, mine_b, got_b = call(
         functools.partial(same_kernel, 3),
-        (visible(half), visible(half)),
+        [visible(early), visible(early), visible(late), visible(late)],
         (m_table,),
         (left, share, mine, got, same),
         1,
     )
-    near, far, total = call(
+    near_a, far_a, power = call(
+        functools.partial(piece_kernel, 3),
+        (visible(early), visible(early), row),
+        (m_table,),
+        (left, share, weight, other_weight, mine_a, got_a, cross_a),
+        1,
+    )
+    far_a = swap(far_a, "pol", 1)
+    near_b, far_b, total = call(
         functools.partial(last_kernel, 3, n_freq),
-        (visible(half), visible(half), row),
+        (visible(late), visible(late), row),
         (m_table, chan_mask),
-        (left, share, weight, other_weight, mine, got, cross),
+        (power, left, share, weight, other_weight, mine_b, got_b, cross_b),
         1,
     )
-    far = swap(far, "pol", 1)
+    far_b = swap(far_b, "pol", 1)
     for name, step in (("pol", 1), ("ma", 3)):
         total = total + swap(total, name, step)
     beside = swap(total, "ma", 1)
@@ -314,7 +346,7 @@
             jax.ShapeDtypeStruct((1, 128), jnp.float32),
         ),
         (chan_mask,),
-        (total, near, far),
+        (total, near_a, far_a, near_b, far_b),
         0,
         out_specs=(HBM, HBM),
         scratch_shapes=[

time: 52.1 us -> 53.5 us (1.027)
  starting transfers between devices: 15.7 us -> 17.1 us
    ppermute x1, starting transfers between devices: 0.01 us -> 1.67 us  [corner_swap(): lax.ppermute(x, names, [(i, i ^ flip) for i in range(math.prod(sizes))])]
    ppermute x12 -> x14, waiting for transfers between devices: 9.04 us -> 7.67 us  [swap(): return lax.ppermute(x, names, [(i, i ^ flip) for i in range(size)])]
    ppermute x3, waiting for transfers between devices: 15 us -> 15.9 us  [straight(): return lax.ppermute(x, name, [(i, i ^ step) for i in range(size)])]
    pallas_call x7 -> x8, Pallas kernels: 7.4 us -> 7.67 us  [call(): pl.pallas_call(kernel, out_shape=out_shape, in_specs=more.pop('in_specs',...]
    ppermute x12 -> x14, starting transfers between devices: 7.48 us -> 7.25 us  [swap(): return lax.ppermute(x, names, [(i, i ^ flip) for i in range(size)])]
  transfers between devices with their start and end apart: 16 -> 18, of which waited for: 9 -> 7; matrix products, arithmetic and copies ran while one was open for 0% -> 0% of each run, Pallas kernels for 6% -> 7%
where the time goes in v8:
time: 53.5 us; the launch traced here: 53.3 us
  waiting for transfers between devices  25.8 us (48%)
  starting transfers between devices  17.1 us (32%)
  Pallas kernels  7.67 us (14%)
  between operations  2.07 us (4%)
  local copies, waits for them, and re-layouts  0.68 us (1%)
    ppermute x3, waiting for transfers between devices, straight(): return lax.ppermute(x, name, [(i, i ^ step) for i in range(size)])  15.9 us
    ppermute x3, starting transfers between devices, straight(): return lax.ppermute(x, name, [(i, i ^ step) for i in range(size)])  8.18 us
    pallas_call x8, Pallas kernels, call(): pl.pallas_call(kernel, out_shape=out_shape, in_specs=more.pop('in_specs',...  7.67 us
    ppermute x14, waiting for transfers between devices, swap(): return lax.ppermute(x, names, [(i, i ^ flip) for i in range(size)])  7.67 us
    ppermute x14, starting transfers between devices, swap(): return lax.ppermute(x, names, [(i, i ^ flip) for i in range(size)])  7.25 us
    ppermute x1, waiting for transfers between devices, corner_swap(): lax.ppermute(x, names, [(i, i ^ flip) for i in range(math.prod(sizes))])  2.18 us
    ppermute x1, starting transfers between devices, corner_swap(): lax.ppermute(x, names, [(i, i ^ flip) for i in range(math.prod(sizes))])  1.67 us
  transfers between devices with their start and end apart: 18, of which 7 were waited for; matrix products, arithmetic and copies ran while one was open for 0% of the time, Pallas kernels for 7%

profile of v8, /device:TPU:0, one launch (start us, length us, event | category | flops | bytes accessed | tf_op | source)
XLA Modules:
  0.0 53.3 jit_solution(11341555608032832040)
XLA Ops:
  0.6 1.3 %shard_map.69 = (bf16[2,128,512]{2,1,0:T(8,128)(2,1)S(1)}, bf16[2,128,512]{2,1,0:T(8,128)(2,1)S(1)}, bf16[2,128,256]{2,1,0:T(8,128)(2,1)S(1)}, bf16[2,128,128]{2...) custom-call(bf16[2,128,4,512]{3,2,1,0:T(4,128)(2,1)} %bitcast.8), custom_call_target="tpu_custom_call" | custom-call | bytes 2097152 | tf_op jit(solution)/shard_map/pallas_call | solution.py:239
  1.9 3.1 %collective-permute-start.3 = (bf16[2,128,512]{2,1,0:T(8,128)(2,1)S(1)}, bf16[2,128,512]{2,1,0:T(8,128)(2,1)S(1)}, u32[]{:S(2)}, u32[]{:S(2)}) collective-permute-start(bf16[2,128,512]{2,1,0:T(8,128)(2,1)S(1)} %get-tuple-element.27), channel_id=1, source_target_pairs={{0,4},{4,0},{8,12},{12,8},{1,5},{5,1},{9,13},{13,9},{2,6},{6,2},{1... | collective-permute-start | bytes 786440 | tf_op jit(solution)/shard_map/ppermute | solution.py:206
  5.1 2.6 %collective-permute-start.5 = (bf16[2,128,512]{2,1,0:T(8,128)(2,1)S(1)}, bf16[2,128,512]{2,1,0:T(8,128)(2,1)S(1)}, u32[]{:S(2)}, u32[]{:S(2)}) collective-permute-start(bf16[2,128,512]{2,1,0:T(8,128)(2,1)S(1)} %get-tuple-element.28), channel_id=1, source_target_pairs={{0,8},{4,12},{8,0},{12,4},{1,9},{5,13},{9,1},{13,5},{2,10},{6,14},... | collective-permute-start | bytes 786440 | tf_op jit(solution)/shard_map/ppermute | solution.py:206
  7.7 9.2 %collective-permute-done.3.refs_2_ = bf16[2,128,512]{2,1,0:T(8,128)(2,1)S(1)} collective-permute-done((bf16[2,128,512]{2,1,0:T(8,128)(2,1)S(1)}, bf16[2,128,512]{2,1,0:T(8,128)(2,1)S(1)}, u32[]{:S(2)}, u32[]{:S(2)}) %collective-permute-start.3) | collective-permute-done | bytes 262176 | tf_op jit(solution)/shard_map/ppermute | solution.py:206
  16.9 2.5 %collective-permute-done.5.refs_4_ = bf16[2,128,512]{2,1,0:T(8,128)(2,1)S(1)} collective-permute-done((bf16[2,128,512]{2,1,0:T(8,128)(2,1)S(1)}, bf16[2,128,512]{2,1,0:T(8,128)(2,1)S(1)}, u32[]{:S(2)}, u32[]{:S(2)}) %collective-permute-start.5) | collective-permute-done | bytes 262176 | tf_op jit(solution)/shard_map/ppermute | solution.py:206
  20.7 0.0 copy-start
  20.7 0.7 %copy-done = f32[1,512]{1,0:T(1,128)S(1)} copy-done((f32[1,512]{1,0:T(1,128)S(1)}, f32[1,512]{1,0:T(1,128)}, u32[]{:S(2)}) %copy-start) | copy-done | bytes 2072
  21.4 1.8 %shard_map.68 = (bf16[8,512,256]{2,1,0:T(8,128)(2,1)S(1)}, bf16[2,512,256]{2,1,0:T(8,128)(2,1)S(1)}, f32[512,128]{1,0:T(8,128)S(1)}) custom-call(bf16[2,512,1024]{2,1,0:T(8,128)(2,1)} %bitcast.7, f32[1,512]{1,0:T(1,128)S(1)} %copy-done), custom_call_target="tpu_custom_call" | custom-call | bytes 2097152 | tf_op jit(solution)/shard_map/pallas_call | solution.py:239
  23.2 1.0 %shard_map.71 = f32[2,512,256]{2,1,0:T(8,128)S(1)} custom-call(s32[1]{0:T(128)S(6)} %copy.8.m_ref, s32[1]{0:T(128)S(6)} %copy.9.mask_ref, bf16[8,512,256]{2,1,0:T(8,128)(2,1)S(1)} %get-tuple-element.23.left_ref.refs_0_, bf16[2,128,512]{2,1,0:T(8,128)(2,1)S(1)} %get-tuple-element.26.refs_0_, bf16[2,128,512]{2,1,0:T(8,128)(2,1)S(1)} %collective-permute-done.2.refs_1_, ...), custom_call_target="tpu_custom_call" | custom-call | flops 805306368 | bytes 3670016 | tf_op jit(solution)/shard_map/pallas_call | solution.py:239
  24.2 0.6 %collective-permute-start.7 = (f32[2,512,256]{2,1,0:T(8,128)S(1)}, f32[2,512,256]{2,1,0:T(8,128)S(1)}, u32[]{:S(2)}, u32[]{:S(2)}) collective-permute-start(f32[2,512,256]{2,1,0:T(8,128)S(1)} %shard_map.71), channel_id=1, source_target_pairs={{0,1},{1,0},{2,3},{3,2},{4,5},{5,4},{6,7},{7,6},{8,9},{9,8},{10,11... | collective-permute-start | bytes 3145736 | tf_op jit(solution)/shard_map/ppermute | solution.py:212
  24.8 0.1 collective-permute-start
  24.9 0.4 collective-permute-start.1
  25.3 2.5 %collective-permute-start.8 = (bf16[2,128,256]{2,1,0:T(8,128)(2,1)S(1)}, bf16[2,128,256]{2,1,0:T(8,128)(2,1)S(1)}, u32[]{:S(2)}, u32[]{:S(2)}) collective-permute-start(bf16[2,128,256]{2,1,0:T(8,128)(2,1)S(1)} %get-tuple-element.29), channel_id=1, source_target_pairs={{0,12},{4,8},{8,4},{12,0},{1,13},{5,9},{9,5},{13,1},{2,14},{6,10},... | collective-permute-start | bytes 393224 | tf_op jit(solution)/shard_map/ppermute | solution.py:206
  27.8 0.8 %collective-permute-start.9 = (bf16[2,128,128]{2,1,0:T(8,128)(2,1)S(1)}, bf16[2,128,128]{2,1,0:T(8,128)(2,1)S(1)}, u32[]{:S(2)}, u32[]{:S(2)}) collective-permute-start(bf16[2,128,128]{2,1,0:T(8,128)(2,1)S(1)} %get-tuple-element.32), channel_id=1, source_target_pairs={{0,13},{1,12},{4,9},{5,8},{8,5},{9,4},{12,1},{13,0},{2,15},{3,14},... | collective-permute-start | bytes 196616 | tf_op jit(solution)/shard_map/ppermute | solution.py:212
  28.6 4.2 %collective-permute-done.8.block_ref = bf16[2,128,256]{2,1,0:T(8,128)(2,1)S(1)} collective-permute-done((bf16[2,128,256]{2,1,0:T(8,128)(2,1)S(1)}, bf16[2,128,256]{2,1,0:T(8,128)(2,1)S(1)}, u32[]{:S(2)}, u32[]{:S(2)}) %collective-permute-start.8) | collective-permute-done | bytes 131104 | tf_op jit(solution)/shard_map/ppermute | solution.py:206
  32.8 1.2 %collective-permute-start.10 = (bf16[2,128,128]{2,1,0:T(8,128)(2,1)S(1)}, bf16[2,128,128]{2,1,0:T(8,128)(2,1)S(1)}, u32[]{:S(2)}, u32[]{:S(2)}) collective-permute-start(bf16[2,128,128]{2,1,0:T(8,128)(2,1)S(1)} %get-tuple-element.36), channel_id=1, source_target_pairs={{0,13},{1,12},{4,9},{5,8},{8,5},{9,4},{12,1},{13,0},{2,15},{3,14},... | collective-permute-start | bytes 196616 | tf_op jit(solution)/shard_map/ppermute | solution.py:212
  33.9 1.0 %shard_map.70.mine_ref = f32[2,512,256]{2,1,0:T(8,128)S(1)} custom-call(s32[1]{0:T(128)S(6)} %copy.8.m_ref, s32[1]{0:T(128)S(6)} %copy.9.mask_ref, bf16[8,512,256]{2,1,0:T(8,128)(2,1)S(1)} %get-tuple-element.23.left_ref.refs_0_, bf16[2,128,512]{2,1,0:T(8,128)(2,1)S(1)} %get-tuple-element.26.refs_0_, bf16[2,128,512]{2,1,0:T(8,128)(2,1)S(1)} %collective-permute-done.2.refs_1_, ...), custom_call_target="tpu_custom_call" | custom-call | flops 805306368 | bytes 3670016 | tf_op jit(solution)/shard_map/pallas_call | solution.py:239
  35.0 0.5 shard_map.72
  35.4 0.5 shard_map.73
  35.9 3.0 %collective-permute-done.10.refs_6_ = bf16[2,128,128]{2,1,0:T(8,128)(2,1)S(1)} collective-permute-done((bf16[2,128,128]{2,1,0:T(8,128)(2,1)S(1)}, bf16[2,128,128]{2,1,0:T(8,128)(2,1)S(1)}, u32[]{:S(2)}, u32[]{:S(2)}) %collective-permute-start.10) | collective-permute-done | bytes 65568 | tf_op jit(solution)/shard_map/ppermute | solution.py:212
  38.9 0.4 shard_map.74
  39.4 0.1 collective-permute-start.17
  39.4 0.5 collective-permute-start.16
  39.9 0.1 collective-permute-start.11
  40.0 2.1 %collective-permute-done.11 = f32[1,128]{1,0:T(1,128)S(1)} collective-permute-done((f32[1,128]{1,0:T(1,128)S(1)}, f32[1,128]{1,0:T(1,128)S(1)}, u32[]{:S(2)}, u32[]{:S(2)}) %collective-permute-start.11) | collective-permute-done | bytes 544 | tf_op jit(solution)/shard_map/ppermute | solution.py:212
  42.1 2.3 %collective-permute-start.12 = (f32[1,128]{1,0:T(1,128)S(1)}, f32[1,128]{1,0:T(1,128)S(1)}, u32[]{:S(2)}, u32[]{:S(2)}) collective-permute-start(f32[1,128]{1,0:T(1,128)S(1)} %add.15), channel_id=1, source_target_pairs={{0,13},{1,12},{4,9},{5,8},{8,5},{9,4},{12,1},{13,0},{2,15},{3,14},... | collective-permute-start | bytes 1544 | tf_op jit(solution)/shard_map/ppermute | solution.py:212
  44.4 2.5 %collective-permute-done.12 = f32[1,128]{1,0:T(1,128)S(1)} collective-permute-done((f32[1,128]{1,0:T(1,128)S(1)}, f32[1,128]{1,0:T(1,128)S(1)}, u32[]{:S(2)}, u32[]{:S(2)}) %collective-permute-start.12) | collective-permute-done | bytes 544 | tf_op jit(solution)/shard_map/ppermute | solution.py:212
  46.9 1.3 %collective-permute-start.14 = (f32[1,128]{1,0:T(1,128)S(1)}, f32[1,128]{1,0:T(1,128)S(1)}, u32[]{:S(2)}, u32[]{:S(2)}) collective-permute-start(f32[1,128]{1,0:T(1,128)S(1)} %add.16), channel_id=1, source_target_pairs={{0,3},{1,2},{2,1},{3,0},{4,7},{5,6},{6,5},{7,4},{8,11},{9,10},{10,... | collective-permute-start | bytes 1544 | tf_op jit(solution)/shard_map/ppermute | solution.py:212
  48.2 1.7 %collective-permute-start.15 = (f32[1,128]{1,0:T(1,128)S(1)}, f32[1,128]{1,0:T(1,128)S(1)}, u32[]{:S(2)}, u32[]{:S(2)}) collective-permute-start(f32[1,128]{1,0:T(1,128)S(1)} %add.16), channel_id=1, source_target_pairs={{0,7},{1,6},{2,5},{3,4},{4,3},{5,2},{6,1},{7,0},{8,15},{9,14},{10,... | collective-permute-start | bytes 1544 | tf_op jit(solution)/shard_map/ppermute | solution.py:219
  49.8 0.0 collective-permute-done.13
  49.9 2.2 %collective-permute-done.15 = f32[1,128]{1,0:T(1,128)S(1)} collective-permute-done((f32[1,128]{1,0:T(1,128)S(1)}, f32[1,128]{1,0:T(1,128)S(1)}, u32[]{:S(2)}, u32[]{:S(2)}) %collective-permute-start.15) | collective-permute-done | bytes 544 | tf_op jit(solution)/shard_map/ppermute | solution.py:219
  52.1 1.2 %shard_map.75 = (bf16[2,512,512]{2,1,0:T(8,128)(2,1)}, f32[1,128]{1,0:T(1,128)}) custom-call(s32[1]{0:T(128)S(6)} %copy.9.mask_ref, f32[1,128]{1,0:T(1,128)S(1)} %add_add_fusion.total_ref, f32[2,512,128]{2,1,0:T(8,128)S(1)} %get-tuple-element.38.near_a, f32[2,512,128]{2,1,0:T(8,128)S(1)} %collective-permute-done.16.got_a, ...), custom_call_target="tpu_custom_call" | custom-call | bytes 2097152 | tf_op jit(solution)/shard_map/pallas_call | solution.py:239
  (17 shorter events, 0.0 us)
Async XLA Ops:
  1.9 14.9 %collective-permute-start.3 = (bf16[2,128,512]{2,1,0:T(8,128)(2,1)S(1)}, bf16[2,128,512]{2,1,0:T(8,128)(2,1)S(1)}, u32[]{:S(2)}, u32[]{:S(2)}) collective-permute-start(bf16[2,128,512]{2,1,0:T(8,128)(2,1)S(1)} %get-tuple-element.27), channel_id=1, source_target_pairs={{0,4},{4,0},{8,12},{12,8},{1,5},{5,1},{9,13},{13,9},{2,6},{6,2},{1... | collective-permute-start | bytes 786440 | tf_op jit(solution)/shard_map/ppermute | solution.py:206
  5.1 14.3 %collective-permute-start.5 = (bf16[2,128,512]{2,1,0:T(8,128)(2,1)S(1)}, bf16[2,128,512]{2,1,0:T(8,128)(2,1)S(1)}, u32[]{:S(2)}, u32[]{:S(2)}) collective-permute-start(bf16[2,128,512]{2,1,0:T(8,128)(2,1)S(1)} %get-tuple-element.28), channel_id=1, source_target_pairs={{0,8},{4,12},{8,0},{12,4},{1,9},{5,13},{9,1},{13,5},{2,10},{6,14},... | collective-permute-start | bytes 786440 | tf_op jit(solution)/shard_map/ppermute | solution.py:206
  7.6 15.6 %collective-permute-start.2 = (bf16[2,128,512]{2,1,0:T(8,128)(2,1)S(1)}, bf16[2,128,512]{2,1,0:T(8,128)(2,1)S(1)}, u32[]{:S(2)}, u32[]{:S(2)}) collective-permute-start(bf16[2,128,512]{2,1,0:T(8,128)(2,1)S(1)} %get-tuple-element.26.refs_0_), channel_id=1, source_target_pairs={{0,1},{1,0},{2,3},{3,2},{4,5},{5,4},{6,7},{7,6},{8,9},{9,8},{10,11... | collective-permute-start | bytes 786440 | tf_op jit(solution)/shard_map/ppermute | solution.py:212
  16.9 6.4 %collective-permute-start.4 = (bf16[2,128,512]{2,1,0:T(8,128)(2,1)S(1)}, bf16[2,128,512]{2,1,0:T(8,128)(2,1)S(1)}, u32[]{:S(2)}, u32[]{:S(2)}) collective-permute-start(bf16[2,128,512]{2,1,0:T(8,128)(2,1)S(1)} %collective-permute-done.3.refs_2_), channel_id=1, source_target_pairs={{0,1},{1,0},{2,3},{3,2},{4,5},{5,4},{6,7},{7,6},{8,9},{9,8},{10,11... | collective-permute-start | bytes 786440 | tf_op jit(solution)/shard_map/ppermute | solution.py:212
  19.4 3.9 %collective-permute-start.6 = (bf16[2,128,512]{2,1,0:T(8,128)(2,1)S(1)}, bf16[2,128,512]{2,1,0:T(8,128)(2,1)S(1)}, u32[]{:S(2)}, u32[]{:S(2)}) collective-permute-start(bf16[2,128,512]{2,1,0:T(8,128)(2,1)S(1)} %collective-permute-done.5.refs_4_), channel_id=1, source_target_pairs={{0,1},{1,0},{2,3},{3,2},{4,5},{5,4},{6,7},{7,6},{8,9},{9,8},{10,11... | collective-permute-start | bytes 786440 | tf_op jit(solution)/shard_map/ppermute | solution.py:212
  20.7 0.7 %copy-start = (f32[1,512]{1,0:T(1,128)S(1)}, f32[1,512]{1,0:T(1,128)}, u32[]{:S(2)}) copy-start(f32[1,512]{1,0:T(1,128)} %noise_ref.1) | copy-start | bytes 6148
  24.2 10.7 %collective-permute-start.7 = (f32[2,512,256]{2,1,0:T(8,128)S(1)}, f32[2,512,256]{2,1,0:T(8,128)S(1)}, u32[]{:S(2)}, u32[]{:S(2)}) collective-permute-start(f32[2,512,256]{2,1,0:T(8,128)S(1)} %shard_map.71), channel_id=1, source_target_pairs={{0,1},{1,0},{2,3},{3,2},{4,5},{5,4},{6,7},{7,6},{8,9},{9,8},{10,11... | collective-permute-start | bytes 3145736 | tf_op jit(solution)/shard_map/ppermute | solution.py:212
  24.8 10.1 %collective-permute-start = (bf16[2,512,256]{2,1,0:T(8,128)(2,1)S(1)}, bf16[2,512,256]{2,1,0:T(8,128)(2,1)S(1)}, u32[]{:S(2)}, u32[]{:S(2)}) collective-permute-start(bf16[2,512,256]{2,1,0:T(8,128)(2,1)S(1)} %get-tuple-element.24), channel_id=1, source_target_pairs={{0,1},{1,0},{2,3},{3,2},{4,5},{5,4},{6,7},{7,6},{8,9},{9,8},{10,11... | collective-permute-start | bytes 1572872 | tf_op jit(solution)/shard_map/ppermute | solution.py:212
  24.9 10.5 %collective-permute-start.1 = (f32[512,128]{1,0:T(8,128)S(1)}, f32[512,128]{1,0:T(8,128)S(1)}, u32[]{:S(2)}, u32[]{:S(2)}) collective-permute-start(f32[512,128]{1,0:T(8,128)S(1)} %get-tuple-element.25.refs_2_), channel_id=1, source_target_pairs={{0,1},{1,0},{2,3},{3,2},{4,5},{5,4},{6,7},{7,6},{8,9},{9,8},{10,11... | collective-permute-start | bytes 786440 | tf_op jit(solution)/shard_map/ppermute | solution.py:212
  25.3 7.4 %collective-permute-start.8 = (bf16[2,128,256]{2,1,0:T(8,128)(2,1)S(1)}, bf16[2,128,256]{2,1,0:T(8,128)(2,1)S(1)}, u32[]{:S(2)}, u32[]{:S(2)}) collective-permute-start(bf16[2,128,256]{2,1,0:T(8,128)(2,1)S(1)} %get-tuple-element.29), channel_id=1, source_target_pairs={{0,12},{4,8},{8,4},{12,0},{1,13},{5,9},{9,5},{13,1},{2,14},{6,10},... | collective-permute-start | bytes 393224 | tf_op jit(solution)/shard_map/ppermute | solution.py:206
  27.8 7.6 %collective-permute-start.9 = (bf16[2,128,128]{2,1,0:T(8,128)(2,1)S(1)}, bf16[2,128,128]{2,1,0:T(8,128)(2,1)S(1)}, u32[]{:S(2)}, u32[]{:S(2)}) collective-permute-start(bf16[2,128,128]{2,1,0:T(8,128)(2,1)S(1)} %get-tuple-element.32), channel_id=1, source_target_pairs={{0,13},{1,12},{4,9},{5,8},{8,5},{9,4},{12,1},{13,0},{2,15},{3,14},... | collective-permute-start | bytes 196616 | tf_op jit(solution)/shard_map/ppermute | solution.py:212
  32.8 6.2 %collective-permute-start.10 = (bf16[2,128,128]{2,1,0:T(8,128)(2,1)S(1)}, bf16[2,128,128]{2,1,0:T(8,128)(2,1)S(1)}, u32[]{:S(2)}, u32[]{:S(2)}) collective-permute-start(bf16[2,128,128]{2,1,0:T(8,128)(2,1)S(1)} %get-tuple-element.36), channel_id=1, source_target_pairs={{0,13},{1,12},{4,9},{5,8},{8,5},{9,4},{12,1},{13,0},{2,15},{3,14},... | collective-permute-start | bytes 196616 | tf_op jit(solution)/shard_map/ppermute | solution.py:212
  39.4 12.7 %collective-permute-start.17 = (f32[2,512,128]{2,1,0:T(8,128)S(1)}, f32[2,512,128]{2,1,0:T(8,128)S(1)}, u32[]{:S(2)}, u32[]{:S(2)}) collective-permute-start(f32[2,512,128]{2,1,0:T(8,128)S(1)} %get-tuple-element.41), channel_id=1, source_target_pairs={{0,1},{1,0},{2,3},{3,2},{4,5},{5,4},{6,7},{7,6},{8,9},{9,8},{10,11... | collective-permute-start | bytes 1572872 | tf_op jit(solution)/shard_map/ppermute | solution.py:212
  39.4 12.6 %collective-permute-start.16 = (f32[2,512,128]{2,1,0:T(8,128)S(1)}, f32[2,512,128]{2,1,0:T(8,128)S(1)}, u32[]{:S(2)}, u32[]{:S(2)}) collective-permute-start(f32[2,512,128]{2,1,0:T(8,128)S(1)} %get-tuple-element.39), channel_id=1, source_target_pairs={{0,1},{1,0},{2,3},{3,2},{4,5},{5,4},{6,7},{7,6},{8,9},{9,8},{10,11... | collective-permute-start | bytes 1572872 | tf_op jit(solution)/shard_map/ppermute | solution.py:212
  39.9 2.1 %collective-permute-start.11 = (f32[1,128]{1,0:T(1,128)S(1)}, f32[1,128]{1,0:T(1,128)S(1)}, u32[]{:S(2)}, u32[]{:S(2)}) collective-permute-start(f32[1,128]{1,0:T(1,128)S(1)} %get-tuple-element.37), channel_id=1, source_target_pairs={{0,1},{1,0},{2,3},{3,2},{4,5},{5,4},{6,7},{7,6},{8,9},{9,8},{10,11... | collective-permute-start | bytes 1544 | tf_op jit(solution)/shard_map/ppermute | solution.py:212
  42.1 4.8 %collective-permute-start.12 = (f32[1,128]{1,0:T(1,128)S(1)}, f32[1,128]{1,0:T(1,128)S(1)}, u32[]{:S(2)}, u32[]{:S(2)}) collective-permute-start(f32[1,128]{1,0:T(1,128)S(1)} %add.15), channel_id=1, source_target_pairs={{0,13},{1,12},{4,9},{5,8},{8,5},{9,4},{12,1},{13,0},{2,15},{3,14},... | collective-permute-start | bytes 1544 | tf_op jit(solution)/shard_map/ppermute | solution.py:212
  46.9 3.0 %collective-permute-start.13 = (f32[1,128]{1,0:T(1,128)S(1)}, f32[1,128]{1,0:T(1,128)S(1)}, u32[]{:S(2)}, u32[]{:S(2)}) collective-permute-start(f32[1,128]{1,0:T(1,128)S(1)} %add.16), channel_id=1, source_target_pairs={{0,5},{1,4},{4,1},{5,0},{8,13},{9,12},{12,9},{13,8},{2,7},{3,6},{6... | collective-permute-start | bytes 1544 | tf_op jit(solution)/shard_map/ppermute | solution.py:212
  46.9 3.0 %collective-permute-start.14 = (f32[1,128]{1,0:T(1,128)S(1)}, f32[1,128]{1,0:T(1,128)S(1)}, u32[]{:S(2)}, u32[]{:S(2)}) collective-permute-start(f32[1,128]{1,0:T(1,128)S(1)} %add.16), channel_id=1, source_target_pairs={{0,3},{1,2},{2,1},{3,0},{4,7},{5,6},{6,5},{7,4},{8,11},{9,10},{10,... | collective-permute-start | bytes 1544 | tf_op jit(solution)/shard_map/ppermute | solution.py:212
  48.2 3.9 %collective-permute-start.15 = (f32[1,128]{1,0:T(1,128)S(1)}, f32[1,128]{1,0:T(1,128)S(1)}, u32[]{:S(2)}, u32[]{:S(2)}) collective-permute-start(f32[1,128]{1,0:T(1,128)S(1)} %add.16), channel_id=1, source_target_pairs={{0,7},{1,6},{2,5},{3,4},{4,3},{5,2},{6,1},{7,0},{8,15},{9,14},{10,... | collective-permute-start | bytes 1544 | tf_op jit(solution)/shard_map/ppermute | solution.py:219

commit v9 on v8

--- a/solution.py
+++ b/solution.py
@@ -138,39 +138,38 @@
             ref[c] = vis
             for i in range(0, maps, 128):
                 sums += vis[:, i : i + 128] * vis[:, i : i + 128]
-    return jnp.sum(sums)
+    return jnp.sum(sums, axis=0, keepdims=True)
 
 
 def piece_kernel(step, m_ref, *refs):
     *rest, power_ref = refs
-    power_ref[...] = jnp.full(power_ref.shape, whole(step, m_ref, *rest))
+    power_ref[...] = whole(step, m_ref, *rest)
 
 
 def last_kernel(step, slots, m_ref, mask_ref, early_ref, *refs):
     *rest, power_ref = refs
     total = early_ref[...] + whole(step, m_ref, *rest)
+    place = lax.broadcasted_iota(jnp.int32, power_ref.shape, 0)
     lane = lax.broadcasted_iota(jnp.int32, power_ref.shape, 1)
     leader = (lax.axis_index("ma") == 0) & (lax.axis_index("pol") == 0)
     live = jnp.where(leader, mask_ref[0], 0).astype(jnp.float32)
     channel = lax.axis_index("freq")
-    power_ref[...] = jnp.where(lane == channel, total, 0.0) + jnp.where(
-        lane == channel + slots, live, 0.0
+    power_ref[...] = jnp.where(place == channel, total, 0.0) + jnp.where(
+        (place == channel + slots) & (lane == 0), live, 0.0
     )
 
 
 def finish_kernel(slots, modes, mask_ref, total_ref, near_a, got_a, near_b, got_b, scaled_ref, power_ref, held_ref, own_ref, sems):
     lane = lax.broadcasted_iota(jnp.int32, (1, 128), 1)
-    totals = total_ref[0:1, :]
-    powers = totals / modes
-    masks = pltpu.roll(totals, 128 - slots, 1)
-
-    def over(where, values):
-        return jnp.sum(jnp.where(where, values, 0.0), axis=1, keepdims=True)
-
-    band = over(lane < slots, powers * masks) / over(lane < slots, masks)
-    own = over(lane == lax.axis_index("freq"), powers)
+    powers = jnp.sum(total_ref[:slots], axis=1, keepdims=True) / modes
+    masks = jnp.sum(total_ref[slots:], axis=1, keepdims=True)
+    place = lax.broadcasted_iota(jnp.int32, powers.shape, 0)
+    band = jnp.sum(powers * masks, axis=0, keepdims=True) / jnp.sum(masks, axis=0, keepdims=True)
+    own = jnp.sum(
+        jnp.where(place == lax.axis_index("freq"), powers, 0.0), axis=0, keepdims=True
+    )
     mask = mask_ref[0].astype(jnp.float32)
-    factor = mask / jnp.sqrt(0.5 * own + 0.5 * band + 1e-06)
+    factor = mask * lax.rsqrt(0.5 * own + 0.5 * band + 1e-06)
     own_ref[...] = jnp.where(lane == 0, own, 0.0)
     copies = [pltpu.make_async_copy(own_ref, power_ref, sems.at[0])]
     copies[0].start()
@@ -327,7 +326,7 @@
     far_a = swap(far_a, "pol", 1)
     near_b, far_b, total = call(
         functools.partial(last_kernel, 3, n_freq),
-        (visible(late), visible(late), row),
+        (visible(late), visible(late), jax.ShapeDtypeStruct((2 * n_freq, 128), jnp.float32)),
         (m_table, chan_mask),
         (power, left, share, weight, other_weight, mine_b, got_b, cross_b),
         1,

time: 53.5 us -> 53.4 us (level)
  transfers between devices with their start and end apart: 18 -> 18, of which waited for: 7 -> 8; matrix products, arithmetic and copies ran while one was open for 0% -> 0% of each run, Pallas kernels for 7% -> 7%
where the time goes in v9:
time: 53.4 us; the launch traced here: 53.2 us
  waiting for transfers between devices  25.9 us (49%)
  starting transfers between devices  17.1 us (32%)
  Pallas kernels  7.38 us (14%)
  between operations  2.06 us (4%)
  local copies, waits for them, and re-layouts  0.68 us (1%)
    ppermute x3, waiting for transfers between devices, straight(): return lax.ppermute(x, name, [(i, i ^ step) for i in range(size)])  15.9 us
    ppermute x3, starting transfers between devices, straight(): return lax.ppermute(x, name, [(i, i ^ step) for i in range(size)])  8.18 us
    ppermute x14, waiting for transfers between devices, swap(): return lax.ppermute(x, names, [(i, i ^ flip) for i in range(size)])  7.82 us
    pallas_call x8, Pallas kernels, call(): pl.pallas_call(kernel, out_shape=out_shape, in_specs=more.pop('in_specs',...  7.38 us
    ppermute x14, starting transfers between devices, swap(): return lax.ppermute(x, names, [(i, i ^ flip) for i in range(size)])  7.25 us
    ppermute x1, waiting for transfers between devices, corner_swap(): lax.ppermute(x, names, [(i, i ^ flip) for i in range(math.prod(sizes))])  2.18 us
    ppermute x1, starting transfers between devices, corner_swap(): lax.ppermute(x, names, [(i, i ^ flip) for i in range(math.prod(sizes))])  1.67 us
  transfers between devices with their start and end apart: 18, of which 8 were waited for; matrix products, arithmetic and copies ran while one was open for 0% of the time, Pallas kernels for 7%

profile of v9, /device:TPU:0, one launch (start us, length us, event | category | flops | bytes accessed | tf_op | source)
XLA Modules:
  0.0 53.2 jit_solution(5484549294982631917)
XLA Ops:
  0.6 1.3 %shard_map.69 = (bf16[2,128,512]{2,1,0:T(8,128)(2,1)S(1)}, bf16[2,128,512]{2,1,0:T(8,128)(2,1)S(1)}, bf16[2,128,256]{2,1,0:T(8,128)(2,1)S(1)}, bf16[2,128,128]{2...) custom-call(bf16[2,128,4,512]{3,2,1,0:T(4,128)(2,1)} %bitcast.8), custom_call_target="tpu_custom_call" | custom-call | bytes 2097152 | tf_op jit(solution)/shard_map/pallas_call | solution.py:238
  1.9 3.1 %collective-permute-start.3 = (bf16[2,128,512]{2,1,0:T(8,128)(2,1)S(1)}, bf16[2,128,512]{2,1,0:T(8,128)(2,1)S(1)}, u32[]{:S(2)}, u32[]{:S(2)}) collective-permute-start(bf16[2,128,512]{2,1,0:T(8,128)(2,1)S(1)} %get-tuple-element.27), channel_id=1, source_target_pairs={{0,4},{4,0},{8,12},{12,8},{1,5},{5,1},{9,13},{13,9},{2,6},{6,2},{1... | collective-permute-start | bytes 786440 | tf_op jit(solution)/shard_map/ppermute | solution.py:205
  5.1 2.6 %collective-permute-start.5 = (bf16[2,128,512]{2,1,0:T(8,128)(2,1)S(1)}, bf16[2,128,512]{2,1,0:T(8,128)(2,1)S(1)}, u32[]{:S(2)}, u32[]{:S(2)}) collective-permute-start(bf16[2,128,512]{2,1,0:T(8,128)(2,1)S(1)} %get-tuple-element.28), channel_id=1, source_target_pairs={{0,8},{4,12},{8,0},{12,4},{1,9},{5,13},{9,1},{13,5},{2,10},{6,14},... | collective-permute-start | bytes 786440 | tf_op jit(solution)/shard_map/ppermute | solution.py:205
  7.7 9.2 %collective-permute-done.3.refs_2_ = bf16[2,128,512]{2,1,0:T(8,128)(2,1)S(1)} collective-permute-done((bf16[2,128,512]{2,1,0:T(8,128)(2,1)S(1)}, bf16[2,128,512]{2,1,0:T(8,128)(2,1)S(1)}, u32[]{:S(2)}, u32[]{:S(2)}) %collective-permute-start.3) | collective-permute-done | bytes 262176 | tf_op jit(solution)/shard_map/ppermute | solution.py:205
  16.9 2.5 %collective-permute-done.5.refs_4_ = bf16[2,128,512]{2,1,0:T(8,128)(2,1)S(1)} collective-permute-done((bf16[2,128,512]{2,1,0:T(8,128)(2,1)S(1)}, bf16[2,128,512]{2,1,0:T(8,128)(2,1)S(1)}, u32[]{:S(2)}, u32[]{:S(2)}) %collective-permute-start.5) | collective-permute-done | bytes 262176 | tf_op jit(solution)/shard_map/ppermute | solution.py:205
  20.7 0.0 copy-start
  20.7 0.7 %copy-done = f32[1,512]{1,0:T(1,128)S(1)} copy-done((f32[1,512]{1,0:T(1,128)S(1)}, f32[1,512]{1,0:T(1,128)}, u32[]{:S(2)}) %copy-start) | copy-done | bytes 2072
  21.4 1.8 %shard_map.68 = (bf16[8,512,256]{2,1,0:T(8,128)(2,1)S(1)}, bf16[2,512,256]{2,1,0:T(8,128)(2,1)S(1)}, f32[512,128]{1,0:T(8,128)S(1)}) custom-call(bf16[2,512,1024]{2,1,0:T(8,128)(2,1)} %bitcast.7, f32[1,512]{1,0:T(1,128)S(1)} %copy-done), custom_call_target="tpu_custom_call" | custom-call | bytes 2097152 | tf_op jit(solution)/shard_map/pallas_call | solution.py:238
  23.2 1.0 %shard_map.71 = f32[2,512,256]{2,1,0:T(8,128)S(1)} custom-call(s32[1]{0:T(128)S(6)} %copy.8.m_ref, s32[1]{0:T(128)S(6)} %copy.9.mask_ref, bf16[8,512,256]{2,1,0:T(8,128)(2,1)S(1)} %get-tuple-element.23.left_ref.refs_0_, bf16[2,128,512]{2,1,0:T(8,128)(2,1)S(1)} %get-tuple-element.26.refs_0_, bf16[2,128,512]{2,1,0:T(8,128)(2,1)S(1)} %collective-permute-done.2.refs_1_, ...), custom_call_target="tpu_custom_call" | custom-call | flops 805306368 | bytes 3670016 | tf_op jit(solution)/shard_map/pallas_call | solution.py:238
  24.2 0.6 %collective-permute-start.7 = (f32[2,512,256]{2,1,0:T(8,128)S(1)}, f32[2,512,256]{2,1,0:T(8,128)S(1)}, u32[]{:S(2)}, u32[]{:S(2)}) collective-permute-start(f32[2,512,256]{2,1,0:T(8,128)S(1)} %shard_map.71), channel_id=1, source_target_pairs={{0,1},{1,0},{2,3},{3,2},{4,5},{5,4},{6,7},{7,6},{8,9},{9,8},{10,11... | collective-permute-start | bytes 3145736 | tf_op jit(solution)/shard_map/ppermute | solution.py:211
  24.8 0.1 collective-permute-start
  24.9 0.4 collective-permute-start.1
  25.3 2.5 %collective-permute-start.8 = (bf16[2,128,256]{2,1,0:T(8,128)(2,1)S(1)}, bf16[2,128,256]{2,1,0:T(8,128)(2,1)S(1)}, u32[]{:S(2)}, u32[]{:S(2)}) collective-permute-start(bf16[2,128,256]{2,1,0:T(8,128)(2,1)S(1)} %get-tuple-element.29), channel_id=1, source_target_pairs={{0,12},{4,8},{8,4},{12,0},{1,13},{5,9},{9,5},{13,1},{2,14},{6,10},... | collective-permute-start | bytes 393224 | tf_op jit(solution)/shard_map/ppermute | solution.py:205
  27.8 0.8 %collective-permute-start.9 = (bf16[2,128,128]{2,1,0:T(8,128)(2,1)S(1)}, bf16[2,128,128]{2,1,0:T(8,128)(2,1)S(1)}, u32[]{:S(2)}, u32[]{:S(2)}) collective-permute-start(bf16[2,128,128]{2,1,0:T(8,128)(2,1)S(1)} %get-tuple-element.32), channel_id=1, source_target_pairs={{0,13},{1,12},{4,9},{5,8},{8,5},{9,4},{12,1},{13,0},{2,15},{3,14},... | collective-permute-start | bytes 196616 | tf_op jit(solution)/shard_map/ppermute | solution.py:211
  28.6 4.2 %collective-permute-done.8.block_ref = bf16[2,128,256]{2,1,0:T(8,128)(2,1)S(1)} collective-permute-done((bf16[2,128,256]{2,1,0:T(8,128)(2,1)S(1)}, bf16[2,128,256]{2,1,0:T(8,128)(2,1)S(1)}, u32[]{:S(2)}, u32[]{:S(2)}) %collective-permute-start.8) | collective-permute-done | bytes 131104 | tf_op jit(solution)/shard_map/ppermute | solution.py:205
  32.8 1.2 %collective-permute-start.10 = (bf16[2,128,128]{2,1,0:T(8,128)(2,1)S(1)}, bf16[2,128,128]{2,1,0:T(8,128)(2,1)S(1)}, u32[]{:S(2)}, u32[]{:S(2)}) collective-permute-start(bf16[2,128,128]{2,1,0:T(8,128)(2,1)S(1)} %get-tuple-element.36), channel_id=1, source_target_pairs={{0,13},{1,12},{4,9},{5,8},{8,5},{9,4},{12,1},{13,0},{2,15},{3,14},... | collective-permute-start | bytes 196616 | tf_op jit(solution)/shard_map/ppermute | solution.py:211
  33.9 1.0 %shard_map.70.mine_ref = f32[2,512,256]{2,1,0:T(8,128)S(1)} custom-call(s32[1]{0:T(128)S(6)} %copy.8.m_ref, s32[1]{0:T(128)S(6)} %copy.9.mask_ref, bf16[8,512,256]{2,1,0:T(8,128)(2,1)S(1)} %get-tuple-element.23.left_ref.refs_0_, bf16[2,128,512]{2,1,0:T(8,128)(2,1)S(1)} %get-tuple-element.26.refs_0_, bf16[2,128,512]{2,1,0:T(8,128)(2,1)S(1)} %collective-permute-done.2.refs_1_, ...), custom_call_target="tpu_custom_call" | custom-call | flops 805306368 | bytes 3670016 | tf_op jit(solution)/shard_map/pallas_call | solution.py:238
  35.0 0.5 shard_map.72
  35.4 0.3 shard_map.73
  35.8 3.1 %collective-permute-done.10.refs_6_ = bf16[2,128,128]{2,1,0:T(8,128)(2,1)S(1)} collective-permute-done((bf16[2,128,128]{2,1,0:T(8,128)(2,1)S(1)}, bf16[2,128,128]{2,1,0:T(8,128)(2,1)S(1)}, u32[]{:S(2)}, u32[]{:S(2)}) %collective-permute-start.10) | collective-permute-done | bytes 65568 | tf_op jit(solution)/shard_map/ppermute | solution.py:211
  38.9 0.3 shard_map.74
  39.2 0.1 collective-permute-start.17
  39.3 0.5 collective-permute-start.16
  39.8 0.1 collective-permute-start.11
  39.9 2.1 %collective-permute-done.11 = f32[4,128]{1,0:T(4,128)S(1)} collective-permute-done((f32[4,128]{1,0:T(4,128)S(1)}, f32[4,128]{1,0:T(4,128)S(1)}, u32[]{:S(2)}, u32[]{:S(2)}) %collective-permute-start.11) | collective-permute-done | bytes 2080 | tf_op jit(solution)/shard_map/ppermute | solution.py:211
  42.0 2.3 %collective-permute-start.12 = (f32[4,128]{1,0:T(4,128)S(1)}, f32[4,128]{1,0:T(4,128)S(1)}, u32[]{:S(2)}, u32[]{:S(2)}) collective-permute-start(f32[4,128]{1,0:T(4,128)S(1)} %add.15), channel_id=1, source_target_pairs={{0,13},{1,12},{4,9},{5,8},{8,5},{9,4},{12,1},{13,0},{2,15},{3,14},... | collective-permute-start | bytes 6152 | tf_op jit(solution)/shard_map/ppermute | solution.py:211
  44.3 2.5 %collective-permute-done.12 = f32[4,128]{1,0:T(4,128)S(1)} collective-permute-done((f32[4,128]{1,0:T(4,128)S(1)}, f32[4,128]{1,0:T(4,128)S(1)}, u32[]{:S(2)}, u32[]{:S(2)}) %collective-permute-start.12) | collective-permute-done | bytes 2080 | tf_op jit(solution)/shard_map/ppermute | solution.py:211
  46.8 1.3 %collective-permute-start.14 = (f32[4,128]{1,0:T(4,128)S(1)}, f32[4,128]{1,0:T(4,128)S(1)}, u32[]{:S(2)}, u32[]{:S(2)}) collective-permute-start(f32[4,128]{1,0:T(4,128)S(1)} %add.16), channel_id=1, source_target_pairs={{0,3},{1,2},{2,1},{3,0},{4,7},{5,6},{6,5},{7,4},{8,11},{9,10},{10,... | collective-permute-start | bytes 6152 | tf_op jit(solution)/shard_map/ppermute | solution.py:211
  48.1 1.7 %collective-permute-start.15 = (f32[4,128]{1,0:T(4,128)S(1)}, f32[4,128]{1,0:T(4,128)S(1)}, u32[]{:S(2)}, u32[]{:S(2)}) collective-permute-start(f32[4,128]{1,0:T(4,128)S(1)} %add.16), channel_id=1, source_target_pairs={{0,7},{1,6},{2,5},{3,4},{4,3},{5,2},{6,1},{7,0},{8,15},{9,14},{10,... | collective-permute-start | bytes 6152 | tf_op jit(solution)/shard_map/ppermute | solution.py:218
  49.7 0.1 collective-permute-done.13
  49.8 2.2 %collective-permute-done.15 = f32[4,128]{1,0:T(4,128)S(1)} collective-permute-done((f32[4,128]{1,0:T(4,128)S(1)}, f32[4,128]{1,0:T(4,128)S(1)}, u32[]{:S(2)}, u32[]{:S(2)}) %collective-permute-start.15) | collective-permute-done | bytes 2080 | tf_op jit(solution)/shard_map/ppermute | solution.py:218
  52.0 1.2 %shard_map.75 = (bf16[2,512,512]{2,1,0:T(8,128)(2,1)}, f32[1,128]{1,0:T(1,128)}) custom-call(s32[1]{0:T(128)S(6)} %copy.9.mask_ref, f32[4,128]{1,0:T(4,128)S(1)} %add_add_fusion.total_ref, f32[2,512,128]{2,1,0:T(8,128)S(1)} %get-tuple-element.38.near_a, f32[2,512,128]{2,1,0:T(8,128)S(1)} %collective-permute-done.16.got_a, ...), custom_call_target="tpu_custom_call" | custom-call | bytes 2097152 | tf_op jit(solution)/shard_map/pallas_call | solution.py:238
  (17 shorter events, 0.0 us)
Async XLA Ops:
  1.9 14.9 %collective-permute-start.3 = (bf16[2,128,512]{2,1,0:T(8,128)(2,1)S(1)}, bf16[2,128,512]{2,1,0:T(8,128)(2,1)S(1)}, u32[]{:S(2)}, u32[]{:S(2)}) collective-permute-start(bf16[2,128,512]{2,1,0:T(8,128)(2,1)S(1)} %get-tuple-element.27), channel_id=1, source_target_pairs={{0,4},{4,0},{8,12},{12,8},{1,5},{5,1},{9,13},{13,9},{2,6},{6,2},{1... | collective-permute-start | bytes 786440 | tf_op jit(solution)/shard_map/ppermute | solution.py:205
  5.1 14.3 %collective-permute-start.5 = (bf16[2,128,512]{2,1,0:T(8,128)(2,1)S(1)}, bf16[2,128,512]{2,1,0:T(8,128)(2,1)S(1)}, u32[]{:S(2)}, u32[]{:S(2)}) collective-permute-start(bf16[2,128,512]{2,1,0:T(8,128)(2,1)S(1)} %get-tuple-element.28), channel_id=1, source_target_pairs={{0,8},{4,12},{8,0},{12,4},{1,9},{5,13},{9,1},{13,5},{2,10},{6,14},... | collective-permute-start | bytes 786440 | tf_op jit(solution)/shard_map/ppermute | solution.py:205
  7.6 15.6 %collective-permute-start.2 = (bf16[2,128,512]{2,1,0:T(8,128)(2,1)S(1)}, bf16[2,128,512]{2,1,0:T(8,128)(2,1)S(1)}, u32[]{:S(2)}, u32[]{:S(2)}) collective-permute-start(bf16[2,128,512]{2,1,0:T(8,128)(2,1)S(1)} %get-tuple-element.26.refs_0_), channel_id=1, source_target_pairs={{0,1},{1,0},{2,3},{3,2},{4,5},{5,4},{6,7},{7,6},{8,9},{9,8},{10,11... | collective-permute-start | bytes 786440 | tf_op jit(solution)/shard_map/ppermute | solution.py:211
  16.9 6.4 %collective-permute-start.4 = (bf16[2,128,512]{2,1,0:T(8,128)(2,1)S(1)}, bf16[2,128,512]{2,1,0:T(8,128)(2,1)S(1)}, u32[]{:S(2)}, u32[]{:S(2)}) collective-permute-start(bf16[2,128,512]{2,1,0:T(8,128)(2,1)S(1)} %collective-permute-done.3.refs_2_), channel_id=1, source_target_pairs={{0,1},{1,0},{2,3},{3,2},{4,5},{5,4},{6,7},{7,6},{8,9},{9,8},{10,11... | collective-permute-start | bytes 786440 | tf_op jit(solution)/shard_map/ppermute | solution.py:211
  19.4 3.9 %collective-permute-start.6 = (bf16[2,128,512]{2,1,0:T(8,128)(2,1)S(1)}, bf16[2,128,512]{2,1,0:T(8,128)(2,1)S(1)}, u32[]{:S(2)}, u32[]{:S(2)}) collective-permute-start(bf16[2,128,512]{2,1,0:T(8,128)(2,1)S(1)} %collective-permute-done.5.refs_4_), channel_id=1, source_target_pairs={{0,1},{1,0},{2,3},{3,2},{4,5},{5,4},{6,7},{7,6},{8,9},{9,8},{10,11... | collective-permute-start | bytes 786440 | tf_op jit(solution)/shard_map/ppermute | solution.py:211
  20.7 0.7 %copy-start = (f32[1,512]{1,0:T(1,128)S(1)}, f32[1,512]{1,0:T(1,128)}, u32[]{:S(2)}) copy-start(f32[1,512]{1,0:T(1,128)} %noise_ref.1) | copy-start | bytes 6148
  24.2 10.7 %collective-permute-start.7 = (f32[2,512,256]{2,1,0:T(8,128)S(1)}, f32[2,512,256]{2,1,0:T(8,128)S(1)}, u32[]{:S(2)}, u32[]{:S(2)}) collective-permute-start(f32[2,512,256]{2,1,0:T(8,128)S(1)} %shard_map.71), channel_id=1, source_target_pairs={{0,1},{1,0},{2,3},{3,2},{4,5},{5,4},{6,7},{7,6},{8,9},{9,8},{10,11... | collective-permute-start | bytes 3145736 | tf_op jit(solution)/shard_map/ppermute | solution.py:211
  24.8 10.1 %collective-permute-start = (bf16[2,512,256]{2,1,0:T(8,128)(2,1)S(1)}, bf16[2,512,256]{2,1,0:T(8,128)(2,1)S(1)}, u32[]{:S(2)}, u32[]{:S(2)}) collective-permute-start(bf16[2,512,256]{2,1,0:T(8,128)(2,1)S(1)} %get-tuple-element.24), channel_id=1, source_target_pairs={{0,1},{1,0},{2,3},{3,2},{4,5},{5,4},{6,7},{7,6},{8,9},{9,8},{10,11... | collective-permute-start | bytes 1572872 | tf_op jit(solution)/shard_map/ppermute | solution.py:211
  24.9 10.5 %collective-permute-start.1 = (f32[512,128]{1,0:T(8,128)S(1)}, f32[512,128]{1,0:T(8,128)S(1)}, u32[]{:S(2)}, u32[]{:S(2)}) collective-permute-start(f32[512,128]{1,0:T(8,128)S(1)} %get-tuple-element.25.refs_2_), channel_id=1, source_target_pairs={{0,1},{1,0},{2,3},{3,2},{4,5},{5,4},{6,7},{7,6},{8,9},{9,8},{10,11... | collective-permute-start | bytes 786440 | tf_op jit(solution)/shard_map/ppermute | solution.py:211
  25.3 7.4 %collective-permute-start.8 = (bf16[2,128,256]{2,1,0:T(8,128)(2,1)S(1)}, bf16[2,128,256]{2,1,0:T(8,128)(2,1)S(1)}, u32[]{:S(2)}, u32[]{:S(2)}) collective-permute-start(bf16[2,128,256]{2,1,0:T(8,128)(2,1)S(1)} %get-tuple-element.29), channel_id=1, source_target_pairs={{0,12},{4,8},{8,4},{12,0},{1,13},{5,9},{9,5},{13,1},{2,14},{6,10},... | collective-permute-start | bytes 393224 | tf_op jit(solution)/shard_map/ppermute | solution.py:205
  27.8 7.6 %collective-permute-start.9 = (bf16[2,128,128]{2,1,0:T(8,128)(2,1)S(1)}, bf16[2,128,128]{2,1,0:T(8,128)(2,1)S(1)}, u32[]{:S(2)}, u32[]{:S(2)}) collective-permute-start(bf16[2,128,128]{2,1,0:T(8,128)(2,1)S(1)} %get-tuple-element.32), channel_id=1, source_target_pairs={{0,13},{1,12},{4,9},{5,8},{8,5},{9,4},{12,1},{13,0},{2,15},{3,14},... | collective-permute-start | bytes 196616 | tf_op jit(solution)/shard_map/ppermute | solution.py:211
  32.8 6.2 %collective-permute-start.10 = (bf16[2,128,128]{2,1,0:T(8,128)(2,1)S(1)}, bf16[2,128,128]{2,1,0:T(8,128)(2,1)S(1)}, u32[]{:S(2)}, u32[]{:S(2)}) collective-permute-start(bf16[2,128,128]{2,1,0:T(8,128)(2,1)S(1)} %get-tuple-element.36), channel_id=1, source_target_pairs={{0,13},{1,12},{4,9},{5,8},{8,5},{9,4},{12,1},{13,0},{2,15},{3,14},... | collective-permute-start | bytes 196616 | tf_op jit(solution)/shard_map/ppermute | solution.py:211
  39.2 12.7 %collective-permute-start.17 = (f32[2,512,128]{2,1,0:T(8,128)S(1)}, f32[2,512,128]{2,1,0:T(8,128)S(1)}, u32[]{:S(2)}, u32[]{:S(2)}) collective-permute-start(f32[2,512,128]{2,1,0:T(8,128)S(1)} %get-tuple-element.41), channel_id=1, source_target_pairs={{0,1},{1,0},{2,3},{3,2},{4,5},{5,4},{6,7},{7,6},{8,9},{9,8},{10,11... | collective-permute-start | bytes 1572872 | tf_op jit(solution)/shard_map/ppermute | solution.py:211
  39.3 12.7 %collective-permute-start.16 = (f32[2,512,128]{2,1,0:T(8,128)S(1)}, f32[2,512,128]{2,1,0:T(8,128)S(1)}, u32[]{:S(2)}, u32[]{:S(2)}) collective-permute-start(f32[2,512,128]{2,1,0:T(8,128)S(1)} %get-tuple-element.39), channel_id=1, source_target_pairs={{0,1},{1,0},{2,3},{3,2},{4,5},{5,4},{6,7},{7,6},{8,9},{9,8},{10,11... | collective-permute-start | bytes 1572872 | tf_op jit(solution)/shard_map/ppermute | solution.py:211
  39.8 2.2 %collective-permute-start.11 = (f32[4,128]{1,0:T(4,128)S(1)}, f32[4,128]{1,0:T(4,128)S(1)}, u32[]{:S(2)}, u32[]{:S(2)}) collective-permute-start(f32[4,128]{1,0:T(4,128)S(1)} %get-tuple-element.37), channel_id=1, source_target_pairs={{0,1},{1,0},{2,3},{3,2},{4,5},{5,4},{6,7},{7,6},{8,9},{9,8},{10,11... | collective-permute-start | bytes 6152 | tf_op jit(solution)/shard_map/ppermute | solution.py:211
  42.0 4.8 %collective-permute-start.12 = (f32[4,128]{1,0:T(4,128)S(1)}, f32[4,128]{1,0:T(4,128)S(1)}, u32[]{:S(2)}, u32[]{:S(2)}) collective-permute-start(f32[4,128]{1,0:T(4,128)S(1)} %add.15), channel_id=1, source_target_pairs={{0,13},{1,12},{4,9},{5,8},{8,5},{9,4},{12,1},{13,0},{2,15},{3,14},... | collective-permute-start | bytes 6152 | tf_op jit(solution)/shard_map/ppermute | solution.py:211
  46.8 3.0 %collective-permute-start.13 = (f32[4,128]{1,0:T(4,128)S(1)}, f32[4,128]{1,0:T(4,128)S(1)}, u32[]{:S(2)}, u32[]{:S(2)}) collective-permute-start(f32[4,128]{1,0:T(4,128)S(1)} %add.16), channel_id=1, source_target_pairs={{0,5},{1,4},{4,1},{5,0},{8,13},{9,12},{12,9},{13,8},{2,7},{3,6},{6... | collective-permute-start | bytes 6152 | tf_op jit(solution)/shard_map/ppermute | solution.py:211
  46.8 3.0 %collective-permute-start.14 = (f32[4,128]{1,0:T(4,128)S(1)}, f32[4,128]{1,0:T(4,128)S(1)}, u32[]{:S(2)}, u32[]{:S(2)}) collective-permute-start(f32[4,128]{1,0:T(4,128)S(1)} %add.16), channel_id=1, source_target_pairs={{0,3},{1,2},{2,1},{3,0},{4,7},{5,6},{6,5},{7,4},{8,11},{9,10},{10,... | collective-permute-start | bytes 6152 | tf_op jit(solution)/shard_map/ppermute | solution.py:211
  48.1 3.9 %collective-permute-start.15 = (f32[4,128]{1,0:T(4,128)S(1)}, f32[4,128]{1,0:T(4,128)S(1)}, u32[]{:S(2)}, u32[]{:S(2)}) collective-permute-start(f32[4,128]{1,0:T(4,128)S(1)} %add.16), channel_id=1, source_target_pairs={{0,7},{1,6},{2,5},{3,4},{4,3},{5,2},{6,1},{7,0},{8,15},{9,14},{10,... | collective-permute-start | bytes 6152 | tf_op jit(solution)/shard_map/ppermute | solution.py:218
